TPU v7x, 32 devices: a whole 2x2x4 slice. The times are simulated.
32 devices in a mesh: arc: 2 (over core), par: 16 (over z, y, x).
Axes of the slice: x: 2, y: 2, z: 4, core: 2. Of those that a mesh axis runs over, the one named last changes fastest.
Arguments:
- design: bfloat16 [4, 1024, 40960], P('arc', None, 'par'), may hold values from -0.1875 to 0.1875
- cov_factor: float32 [4, 1024, 1024], P('arc', 'par'), may hold values from -1 to 3, as said below
- active_blocks: int32 [4, 80], P('arc'), may hold values from 0 to 159, all different within a row
- panel_index: int32 [1], replicated, may hold values from 0 to 79
- reg_diag: float32 [40960], replicated, may hold values from 0.5 to 4
Outputs:
- solved: float32 [512, 40960], P(None, ('par', 'arc'))
Inputs may be any that keep to these rules, and one draw needn't show every extreme that they name: Each cov_factor[a] is lower triangular with a positive diagonal.
All inputs are finite; a program needn't handle non-finite values.
Results may differ from a plain program's by a relative error of at most 0.0032.
Values may be sent and summed in bfloat16 or wider, within the bound.
No kernel may reach another device: no remote copies, remote signals or barrier semaphores. Data moves between devices by JAX's collectives and lax.ppermute only.
A program may use at most 192 MiB of HBM per device.

v0:
```python
import functools

import jax
import jax.numpy as jnp
from jax import lax
from jax.experimental import pallas as pl
from jax.experimental.pallas import tpu as pltpu
from jax.sharding import PartitionSpec as P

PANEL = 512
BLK = 256
F32, BF16 = jnp.float32, jnp.bfloat16
LANE = 128


def split(value):
    high = value.astype(BF16)
    return high, (value - high.astype(F32)).astype(BF16)


def mm(a, b, dims=((1,), (0,))):
    return lax.dot_general(a, b, (dims, ((), ())), preferred_element_type=F32)


def mm3(a, b):
    ah, al = split(a)
    bh, bl = split(b)
    return mm(ah, bh) + (mm(ah, bl) + mm(al, bh))


def level_mask(step):
    rows = lax.broadcasted_iota(jnp.int32, (LANE, LANE), 0)
    cols = lax.broadcasted_iota(jnp.int32, (LANE, LANE), 1)
    return (
        (rows // (2 * step) == cols // (2 * step))
        & ((rows // step) % 2 == 1)
        & ((cols // step) % 2 == 0)
    )


def invert_levels(inverse, lower, first, last):
    step = first
    while step < last:
        below = jnp.where(level_mask(step), lower, 0.0)
        inverse = inverse - mm3(inverse, mm3(below, inverse))
        step *= 2
    return inverse


def diag_kernel(off_ref, strip_ref, high, low, square):
    arcs, rows, _ = strip_ref.shape
    off = pl.multiple_of(off_ref[0], 8)
    r = lax.broadcasted_iota(jnp.int32, (LANE, LANE), 0)
    c = lax.broadcasted_iota(jnp.int32, (LANE, LANE), 1)
    eye = r == c
    sub = lax.broadcasted_iota(jnp.int32, (rows, LANE), 1)
    own = (sub >= off) & (sub < off + rows)
    for arc in range(arcs):
        square[arc] = eye.astype(F32)
        square[arc, pl.ds(off, rows), :] = jnp.where(own, strip_ref[arc], 0.0)
    lowers = [square[arc] for arc in range(arcs)]
    invs = [jnp.where(eye, 1.0 / jnp.where(eye, low, 1.0), 0.0) for low in lowers]
    step = 1
    while step < rows:
        mask = level_mask(step)
        parts = [mm3(jnp.where(mask, low, 0.0), inv) for low, inv in zip(lowers, invs)]
        invs = [inv - mm3(inv, part) for inv, part in zip(invs, parts)]
        step *= 2
    for arc in range(arcs):
        square[arc] = invs[arc]
        value = jnp.where(own, square[arc, pl.ds(off, rows), :], strip_ref[arc])
        high[arc], low[arc] = split(value)


def invert_diag(strip, off):
    arcs = strip.shape[0]
    out = jax.ShapeDtypeStruct(strip.shape, BF16)
    return pl.pallas_call(
        diag_kernel,
        out_shape=(out, out),
        in_specs=[pl.BlockSpec(memory_space=pltpu.SMEM), pl.BlockSpec(memory_space=pltpu.VMEM)],
        out_specs=(pl.BlockSpec(memory_space=pltpu.VMEM), pl.BlockSpec(memory_space=pltpu.VMEM)),
        scratch_shapes=[pltpu.VMEM((arcs, LANE, LANE), F32)],
        name="invert_diag",
    )(off, strip)


def invert_factor(rest, fine, high, low, first):
    size = high.shape[0]
    half = max(size // 2, LANE)
    for top in range(0, size, half):
        for ref in (high, low):
            ref[top : top + half, top : top + half] = jnp.zeros((half, half), BF16)
    rows = lax.broadcasted_iota(jnp.int32, (LANE, LANE), 0) // first
    cols = lax.broadcasted_iota(jnp.int32, (LANE, LANE), 1) // first
    blocks = [
        rest[t : t + LANE, t : t + LANE].astype(F32) + fine[t : t + LANE, :].astype(F32)
        for t in range(0, size, LANE)
    ]
    invs = [jnp.where(rows == cols, block, 0.0) for block in blocks]
    step = first
    while step < LANE:
        mask = level_mask(step)
        parts = [mm3(jnp.where(mask, block, 0.0), inv) for block, inv in zip(blocks, invs)]
        invs = [inv - mm3(inv, part) for inv, part in zip(invs, parts)]
        step *= 2
    for index, inv in enumerate(invs):
        at = slice(index * LANE, (index + 1) * LANE)
        high[at, at], low[at, at] = split(inv)
    step = LANE
    while step < size:
        for base in range(0, size, 2 * step):
            left = slice(base, base + step)
            right = slice(base + step, base + 2 * step)
            below = rest[right, left]
            ph, pl_ = split(mm(below, high[left, left]) + mm(below, low[left, left]))
            ch, cl = high[right, right], low[right, right]
            high[right, left], low[right, left] = split(-(mm(ch, ph) + (mm(ch, pl_) + mm(cl, ph))))
        step *= 2


VM = pl.BlockSpec(memory_space=pltpu.VMEM)
SM = pl.BlockSpec(memory_space=pltpu.SMEM)
MIB = 1 << 20


def grant(mib):
    return pltpu.CompilerParams(vmem_limit_bytes=mib * MIB)


def invert_dense_kernel(first, rows_ref, high, low):
    invert_factor(rows_ref.at[:, LANE:], rows_ref.at[:, :LANE], high, low, first)


def invert_pieces_kernel(first, place_ref, p0, p1, p2, p3, high, low, rest, fine):
    rows = p0.shape[0]
    planes = rest.shape[0] // (4 * rows)
    for k, piece in enumerate((p0, p1, p2, p3)):
        seat = place_ref[k]
        left = 0
        for plane in range(planes):
            width = 4 * rows * (plane + 1)
            at = pl.multiple_of((4 * plane + seat) * rows, 16)
            fine[pl.ds(at, rows), :] = piece[:, left : left + LANE]
            rest[pl.ds(at, rows), :width] = piece[:, left + LANE : left + LANE + width]
            left += LANE + width
    invert_factor(rest, fine, high, low, first)


def invert_call(kernel, size, count, scratch):
    out = jax.ShapeDtypeStruct((size, size), BF16)
    return pl.pallas_call(
        kernel,
        out_shape=(out, out),
        in_specs=[SM] * (count > 1) + [VM] * count,
        out_specs=(VM, VM),
        scratch_shapes=scratch,
        compiler_params=grant(20),
        name="invert_factor",
    )


def apply_panel(raw, high, low, pt, q_ref):
    width, size = pt.shape
    span = min(256, size)
    nt = ((1,), (1,))
    for top in range(0, size, span):
        end = top + span
        value = mm(raw[:, :end], high[top:end, :end], nt) + mm(raw[:, :end], low[top:end, :end], nt)
        pt[:, top:end] = value.astype(BF16)
    for top in range(0, size, span):
        end = top + span
        part = pt[:, top:]
        value = mm(part, high[top:, top:end]) + mm(part, low[top:, top:end])
        q_ref[:width, top:end], q_ref[width:, top:end] = split(value)


def apply_kernel(arcs, place_ref, *refs):
    count = (len(refs) - 4) // arcs - 2
    pieces = refs[: arcs * count]
    factors = refs[arcs * count : arcs * (count + 2)]
    q_ref, block_ref, panel, pt = refs[arcs * (count + 2) :]
    nt = ((1,), (1,))
    for arc in range(arcs):
        index = arc * pieces[0].shape[0] * count
        for piece in pieces[arc * count : (arc + 1) * count]:
            rows = piece.shape[1]
            for z in range(piece.shape[0]):
                at = pl.multiple_of(place_ref[index], 16)
                panel[pl.ds(at, rows), :] = piece[z].astype(F32)
                index += 1
        raw = panel[...].T.astype(BF16)
        apply_panel(raw, factors[2 * arc], factors[2 * arc + 1], pt, q_ref.at[arc])
        part = mm(pt[...], pt[...], nt)
        block_ref[...] = part if arc == 0 else block_ref[...] + part


def apply_call(place, pieces, factors):
    arcs = len(factors) // 2
    size = factors[0].shape[0]
    width = pieces[0].shape[2]
    return pl.pallas_call(
        functools.partial(apply_kernel, arcs),
        out_shape=(
            jax.ShapeDtypeStruct((arcs, 2 * width, size), BF16),
            jax.ShapeDtypeStruct((width, width), F32),
        ),
        in_specs=[SM] + [VM] * (len(pieces) + len(factors)),
        out_specs=(VM, VM),
        scratch_shapes=[pltpu.VMEM((size, width), F32), pltpu.VMEM((width, size), BF16)],
        compiler_params=grant(32),
        name="apply_panel",
    )(place, *pieces, *factors)


def normals_kernel(info, own, far, qown, qfar, inv_ref, reg_ref, out_ref, data, qs, acc, sems):
    near = own.shape[0]
    arcs = 2 * near
    size, share = acc.shape
    blocks = share // BLK
    half = size // 2
    left = pl.multiple_of(info[0] * BLK, BLK)
    copies = []
    for arc in range(arcs):
        if arc < near:
            source, q = own.at[arc, :, pl.ds(left, share)], qown.at[arc]
        else:
            source, q = far.at[arc - near], qfar.at[arc - near]
        pair = (
            pltpu.make_async_copy(q, qs.at[arc], sems.at[2 * arc]),
            pltpu.make_async_copy(source, data.at[arc], sems.at[2 * arc + 1]),
        )
        for copy in pair:
            copy.start()
        copies.append(pair)
    acc[...] = jnp.zeros_like(acc)
    for arc in range(arcs):
        for copy in copies[arc]:
            copy.wait()

        def add(block, _):
            @pl.when(info[2 + block * arcs + arc] > 0)
            def _():
                at = pl.ds(pl.multiple_of(block * BLK, BLK), BLK)
                both = mm(qs[arc], data[arc, :, at])
                acc[:, at] += both[:size] + both[size:]

            return 0

        lax.fori_loop(0, blocks, add, 0)
    ih, il = split(inv_ref[...])
    row = lax.broadcasted_iota(jnp.int32, (size, BLK), 0) + info[1]
    col = lax.broadcasted_iota(jnp.int32, (size, BLK), 1)
    for block in range(blocks):
        at = slice(block * BLK, (block + 1) * BLK)
        hit = row == col + block * BLK
        th, tl = split(acc[:, at] + jnp.where(hit, reg_ref[:, at], 0.0))
        for top, end in ((0, half), (half, size)):
            value = mm(ih[top:end, :end], th[:end]) + mm(ih[top:end, :end], tl[:end])
            out_ref[top:end, at] = value + mm(il[top:end, :end], th[:end])


def normals_call(info, own, far, qown, qfar, inverse, reg):
    near, size, _ = own.shape
    arcs = 2 * near
    share = far.shape[2]
    width = inverse.shape[0]
    hbm = pl.BlockSpec(memory_space=pl.ANY)
    return pl.pallas_call(
        normals_kernel,
        out_shape=jax.ShapeDtypeStruct((width, share), F32),
        in_specs=[SM, hbm, hbm, hbm, hbm, VM, VM],
        out_specs=VM,
        scratch_shapes=[
            pltpu.VMEM((arcs, size, share), BF16),
            pltpu.VMEM((arcs, 2 * width, size), BF16),
            pltpu.VMEM((width, share), F32),
            pltpu.SemaphoreType.DMA((2 * arcs,)),
        ],
        compiler_params=grant(36),
        name="normals",
    )(info, own, far, qown, qfar, inverse, reg)

SUB = 8


def three(value):
    high = value.astype(BF16)
    rest = value - high.astype(F32)
    mid = rest.astype(BF16)
    return high, mid, (rest - mid.astype(F32)).astype(BF16)


def factor_diag(work):
    tn = ((0,), (0,))
    wide = work.shape[1]
    for top in range(0, LANE, SUB):
        rows = [work[top + i : top + i + 1, :] for i in range(SUB)]
        e = {}
        for j in range(SUB):
            for i in range(j, SUB):
                at = top + i
                e[j, i] = jnp.broadcast_to(rows[j][:, at : at + 1], (1, LANE))
        for j in range(SUB):
            inv = lax.rsqrt(e[j, j])
            inv2 = jnp.concatenate([inv] * (wide // LANE), axis=1)
            rows[j] = rows[j] * inv2
            for i in range(j + 1, SUB):
                e[j, i] = e[j, i] * inv
            for i in range(j + 1, SUB):
                for k in range(i, SUB):
                    e[i, k] = e[i, k] - e[j, i] * e[j, k]
                coef = jnp.concatenate([e[j, i]] * (wide // LANE), axis=1)
                rows[i] = rows[i] - coef * rows[j]
        part = jnp.concatenate(rows, axis=0)
        work[top : top + SUB, :] = part
        end = top + SUB
        if end < LANE:
            h, m, l = three(part)
            lhs = jnp.concatenate([h, h, m, m, h, l], axis=0)[:, :LANE]
            rhs = jnp.concatenate([h, m, h, m, l, h], axis=0)
            gone = mm(lhs, rhs, tn)
            work[end:, :] = work[end:, :] - gone[end:, :]


def chol_kernel(block_ref, other_ref, reg_ref, out_ref, full, work, upper):
    size = block_ref.shape[0]
    row = lax.broadcasted_iota(jnp.int32, (size, size), 0)
    col = lax.broadcasted_iota(jnp.int32, (size, size), 1)
    full[...] = (block_ref[...] + other_ref[...]) + jnp.where(row == col, reg_ref[...], 0.0)
    r1 = lax.broadcasted_iota(jnp.int32, (LANE, LANE), 0)
    c1 = lax.broadcasted_iota(jnp.int32, (LANE, LANE), 1)
    out_ref[...] = jnp.zeros(out_ref.shape, F32)
    for top in range(0, size, LANE):
        end = top + LANE
        work[:, :LANE] = full[top:end, top:end]
        work[:, LANE:] = (r1 == c1).astype(F32)
        factor_diag(work)
        inverse = jnp.where(r1 >= c1, work[:, LANE:], 0.0)
        out_ref[top:end, top:end] = inverse
        if end < size:
            right = mm3(inverse, full[top:end, end:])
            upper[top:end, end:] = right
            rt = right.T
            full[end:, end:] = full[end:, end:] - mm3(rt, right)
    step = LANE
    while step < size:
        for base in range(0, size, 2 * step):
            left = slice(base, base + step)
            second = slice(base + step, base + 2 * step)
            low = upper[left, second].T
            out_ref[second, left] = -mm3(out_ref[second, second], mm3(low, out_ref[left, left]))
        step *= 2


def chol_inverse(block, other, reg):
    size = block.shape[0]
    vm = pl.BlockSpec(memory_space=pltpu.VMEM)
    return pl.pallas_call(
        chol_kernel,
        out_shape=jax.ShapeDtypeStruct((size, size), F32),
        in_specs=[vm, vm, vm],
        out_specs=vm,
        scratch_shapes=[
            pltpu.VMEM((size, size), F32),
            pltpu.VMEM((LANE, 2 * LANE), F32),
            pltpu.VMEM((size, size), F32),
        ],
        compiler_params=grant(12),
        name="chol_inverse",
    )(block, other, reg)


def block_hits(active, first, count):
    ids = first + jnp.arange(count, dtype=jnp.int32)
    return jnp.any(active[:, :, None] == ids[None, None, :], axis=1)


def factor_rows(cov_factor, me):
    rows = cov_factor.shape[1]
    at = me * rows // LANE * LANE
    strip = lax.dynamic_slice_in_dim(cov_factor, at, LANE, 2)
    high, low = invert_diag(strip, (me * rows % LANE).astype(jnp.int32)[None])
    rest = lax.dynamic_update_slice_in_dim(cov_factor.astype(BF16), high, at, 2)
    return jnp.concatenate([low, rest], axis=2)


def general(design, cov_factor, active_blocks, panel_index, reg_diag):
    arcs, observed, columns = design.shape
    rows = cov_factor.shape[1]
    par_id = lax.axis_index("par")
    arc_id = lax.axis_index("arc")
    lower = lax.all_gather(factor_rows(cov_factor, par_id), "par", axis=1, tiled=True)
    local_blocks = columns // BLK
    hits = block_hits(active_blocks, par_id * local_blocks, local_blocks)
    masked = design * jnp.repeat(hits, BLK, axis=1).astype(BF16)[:, None, :]
    start = panel_index[0] * PANEL
    padded = jnp.pad(masked, ((0, 0), (0, 0), (PANEL, PANEL)))
    window = lax.dynamic_slice_in_dim(
        padded, jnp.clip(start - par_id * columns + PANEL, 0, columns + PANEL), PANEL, 2
    )
    panel = lax.psum(window.astype(F32).astype(BF16), "par")
    factors = []
    for arc in range(arcs):
        call = invert_call(functools.partial(invert_dense_kernel, rows), observed, 1, [])
        factors += call(lower[arc])
    place = jnp.zeros((arcs,), jnp.int32)
    qs, block = apply_call(place, [panel[arc : arc + 1] for arc in range(arcs)], factors)
    both = jnp.einsum("apo,aoc->pc", qs, masked, preferred_element_type=F32)
    gram = both[:PANEL] + both[PANEL:]
    share = columns // lax.axis_size("arc")
    gram, block = lax.psum((gram, block), "arc")
    gram = lax.dynamic_slice_in_dim(gram, arc_id * share, share, 1)
    reg_panel = lax.dynamic_slice_in_dim(reg_diag, start, PANEL)
    inverse = chol_inverse(block, jnp.zeros_like(block), reg_panel[None, :])
    global_cols = par_id * columns + arc_id * share + jnp.arange(share, dtype=jnp.int32)
    rows_at = start + jnp.arange(PANEL, dtype=jnp.int32)
    shifted = gram + jnp.where(global_cols[None, :] == rows_at[:, None], reg_panel[:, None], 0.0)
    return jnp.dot(inverse, shifted, precision=lax.Precision.HIGHEST, preferred_element_type=F32)


def paired(design, cov_factor, active_blocks, panel_index, reg_diag):
    arcs, observed, columns = design.shape
    rows = cov_factor.shape[1]
    chips = lax.axis_size("par")
    planes = chips // 4
    me = lax.axis_index("par")
    core = lax.axis_index("arc")
    sides = (me & 1, (me >> 1) & 1)
    plane = me >> 2
    share = columns // 2
    start = panel_index[0] * PANEL

    def swap(value):
        return lax.ppermute(value, "arc", [(0, 1), (1, 0)])

    def hop(value, bits):
        return lax.ppermute(value, "par", [(p, p ^ bits) for p in range(chips)])

    def spread(value, first):
        second = 3 - first
        direct = hop(value, first)
        return {0: value, first: direct, second: hop(value, second), 3: hop(direct, second)}

    offset = start - me * columns
    inside = (offset >= 0) & (offset < columns)
    live = jnp.repeat(block_hits(active_blocks, start // BLK, PANEL // BLK) & inside, BLK, axis=1)
    left = jnp.clip(offset, 0, columns - PANEL)
    half, quarter = observed // 2, observed // 4

    def window(arc, top):
        value = lax.dynamic_slice(design, (jnp.int32(arc), top, left), (1, half, PANEL))[0]
        return jnp.where(live[arc][None, :], value, 0)

    sends = [window(arc, (1 - sides[arc % 2]) * half) for arc in range(arcs)]
    sends, cov_factor = lax.optimization_barrier((sends, cov_factor))
    keeps = [window(arc, sides[arc % 2] * half) for arc in range(arcs)]
    seeds = []
    for arc in range(arcs):
        first, second = arc % 2, 1 - arc % 2
        gone = hop(sends[arc], 1 << first)

        def piece(side):
            at = side * quarter
            return lax.dynamic_slice_in_dim(keeps[arc], at, quarter, 0) + lax.dynamic_slice_in_dim(
                gone, at, quarter, 0
            )

        value = piece(sides[second]) + hop(piece(1 - sides[second]), 1 << second)
        seeds.append(value.reshape(planes, rows, PANEL))
    seeds = jnp.stack(seeds, axis=1)
    chunk = lax.dynamic_index_in_dim(seeds, plane, 0, False)
    for k in range(1, planes):
        chunk += hop(lax.dynamic_index_in_dim(seeds, plane ^ k, 0, False), 4 * k)

    lower = factor_rows(cov_factor, me)
    stack = [lower] + [hop(lower, 4 * k) for k in range(1, planes)]
    packed = []
    for index in range(planes):
        width = LANE + 4 * rows * (index + 1)
        value = stack[0][:, :, :width]
        for k in range(1, planes):
            value = jnp.where(plane == (index ^ k), stack[k][:, :, :width], value)
        packed.append(value)
    packed = jnp.concatenate(packed, axis=2)
    seats = (me & 3) ^ jnp.arange(4, dtype=jnp.int32)

    first_column = me * columns + core * share
    both = jnp.concatenate([active_blocks, swap(active_blocks)], axis=0)
    lives = block_hits(both, first_column // BLK, share // BLK).T.reshape(-1).astype(jnp.int32)
    info = jnp.stack([core * (share // BLK), start - first_column]).astype(jnp.int32)
    info = jnp.concatenate([info, lives])
    reg = lax.dynamic_slice_in_dim(reg_diag, first_column, share)[None, :]
    reg_panel = lax.dynamic_slice_in_dim(reg_diag, start, PANEL)[None, :]
    source = me ^ (
        jnp.arange(4, dtype=jnp.int32)[:, None] ^ (4 * jnp.arange(planes, dtype=jnp.int32)[None, :])
    )
    place = []
    for arc in range(arcs):
        bits = (source & 1, (source >> 1) & 1)
        order = (bits[arc % 2] * 2 + bits[1 - arc % 2]) * planes + (source >> 2)
        place.append(order.reshape(-1) * rows)
    place = jnp.concatenate(place)
    far = swap(lax.dynamic_slice_in_dim(design, (1 - core) * share, share, 2))
    chunk, seats, info, reg, reg_panel, place = lax.optimization_barrier(
        (chunk, seats, info, reg, reg_panel, place)
    )

    factors = []
    for arc in range(arcs):
        pieces = spread(packed[arc], 1 + arc % 2)
        call = invert_call(
            functools.partial(invert_pieces_kernel, rows), observed, 4,
            [pltpu.VMEM((observed, observed), BF16), pltpu.VMEM((observed, LANE), BF16)],
        )
        factors += call(seats, *[pieces[k] for k in range(4)])

    stack = jnp.stack([chunk] + [hop(chunk, 4 * k) for k in range(1, planes)], axis=1)
    pieces = []
    for arc in range(arcs):
        found = spread(stack[arc], 1 + arc % 2)
        pieces += [found[k] for k in range(4)]
    qs, block = apply_call(place, pieces, factors)
    inverse = chol_inverse(block, swap(block), reg_panel)
    return normals_call(info, design, far, qs, swap(qs), inverse, reg)


def whole(design, cov_factor, *rest):
    chips = lax.axis_size("par")
    columns = design.shape[2]
    fits = (
        lax.axis_size("arc") == 2
        and design.shape[0] == 2
        and chips == 16
        and columns % PANEL == 0
        and columns % (2 * BLK) == 0
        and LANE % cov_factor.shape[1] == 0
    )
    return (paired if fits else general)(design, cov_factor, *rest)


def solution(mesh):
    in_specs = (P("arc", None, "par"), P("arc", "par", None), P("arc", None), P(), P())
    out_specs = P(None, ("par", "arc"))
    return jax.shard_map(
        whole, mesh=mesh, in_specs=in_specs, out_specs=out_specs, check_vma=False
    )
```

profile of v0, /device:TPU:0, one launch (start us, length us, event | category | flops | bytes accessed | tf_op | source)
XLA Modules:
  0.0 170.5 jit_solution(2394882021928110035)
XLA Ops:
  1.2 0.9 compare_reduce_fusion.1
  2.3 2.8 %bitcast_select_fusion = (bf16[512,512]{1,0:T(8,128)(2,1)S(1)}, bf16[512,512]{1,0:T(8,128)(2,1)S(1)}, bf16[512,512]{1,0:T(8,128)(2,1)S(1)}, bf16[512,512]{1,0:T(8,128)(2,1)S(1)}) fusion(bf16[2,1024,2560]{2,1,0:T(8,128)(2,1)} %own.1, s32[]{:T(128)S(6)} %select_n.177, s32[]{:T(128)S(6)} %min.4, pred[512]{0:T(512)(128)(4,1)S(1)} %broadcast_in_dim.55, ...), kind=kLoop, calls=%fused_computation.14 | loop fusion | flops 1048576 | bytes 4195348 | tf_op jit(solution)/shard_map/jit(_where)/select_n | solution.py:453
  5.8 3.8 %invert_diag.1 = (bf16[2,64,128]{2,1,0:T(8,128)(2,1)}, bf16[2,64,128]{2,1,0:T(8,128)(2,1)}) custom-call(s32[1]{0:T(128)} %bitcast.26.off_ref, f32[2,64,128]{2,1,0:T(8,128)} %constant_dynamic-slice_fusion.strip_ref), custom_call_target="tpu_custom_call" | custom-call | tf_op jit(solution)/shard_map/invert_diag/pallas_call | solution.py:78
  10.4 1.5 pad_maximum_fusion.1
  11.9 2.6 %collective-permute-start.20 = (bf16[2,64,1152]{2,1,0:T(8,128)(2,1)}, bf16[2,64,1152]{2,1,0:T(8,128)(2,1)S(1)}, u32[]{:S(2)}, u32[]{:S(2)}) collective-permute-start(bf16[2,64,1152]{2,1,0:T(8,128)(2,1)} %pad_maximum_fusion.1), channel_id=1, source_target_pairs={{0,4},{1,5},{2,6},{3,7},{4,0},{5,1},{6,2},{7,3},{8,12},{9,13},{10,... | collective-permute-start | bytes 884744 | tf_op jit(solution)/shard_map/ppermute | solution.py:438
  14.5 2.8 %collective-permute-start.19 = (bf16[2,64,1152]{2,1,0:T(8,128)(2,1)}, bf16[2,64,1152]{2,1,0:T(8,128)(2,1)S(1)}, u32[]{:S(2)}, u32[]{:S(2)}) collective-permute-start(bf16[2,64,1152]{2,1,0:T(8,128)(2,1)} %pad_maximum_fusion.1), channel_id=1, source_target_pairs={{0,8},{1,9},{2,10},{3,11},{4,12},{5,13},{6,14},{7,15},{8,0},{9,1},... | collective-permute-start | bytes 884744 | tf_op jit(solution)/shard_map/ppermute | solution.py:438
  17.2 1.6 collective-permute-start
  19.9 0.8 dynamic_slice.77
  20.7 1.6 collective-permute-start.2
  22.7 5.6 %collective-permute-done.20 = bf16[2,64,1152]{2,1,0:T(8,128)(2,1)S(1)} collective-permute-done((bf16[2,64,1152]{2,1,0:T(8,128)(2,1)}, bf16[2,64,1152]{2,1,0:T(8,128)(2,1)S(1)}, u32[]{:S(2)}, u32[]{:S(2)}) %collective-permute-start.20) | collective-permute-done | bytes 294944 | tf_op jit(solution)/shard_map/ppermute | solution.py:438
  28.3 9.8 %collective-permute-done.19 = bf16[2,64,1152]{2,1,0:T(8,128)(2,1)S(1)} collective-permute-done((bf16[2,64,1152]{2,1,0:T(8,128)(2,1)}, bf16[2,64,1152]{2,1,0:T(8,128)(2,1)S(1)}, u32[]{:S(2)}, u32[]{:S(2)}) %collective-permute-start.19) | collective-permute-done | bytes 294944 | tf_op jit(solution)/shard_map/ppermute | solution.py:438
  38.2 0.8 fusion.7
  39.0 0.9 fusion.3
  40.1 1.2 dynamic-slice_add_fusion.1
  41.3 1.6 collective-permute-start.1
  42.9 1.1 dynamic-slice_add_fusion
  44.0 1.6 collective-permute-start.3
  45.6 2.9 %collective-permute-done.1 = bf16[256,512]{1,0:T(8,128)(2,1)S(1)} collective-permute-done((bf16[256,512]{1,0:T(8,128)(2,1)S(1)}, bf16[256,512]{1,0:T(8,128)(2,1)S(1)}, u32[]{:S(2)}, u32[]{:S(2)}) %collective-permute-start.1) | collective-permute-done | bytes 262176 | tf_op jit(solution)/shard_map/ppermute | solution.py:438
  48.5 1.1 add_add_fusion.1
  49.5 1.6 collective-permute-done.3
  51.2 1.1 add_add_fusion
  52.3 7.0 %collective-permute-start.4 = (bf16[2,64,512]{2,1,0:T(8,128)(2,1)S(1)}, bf16[2,64,512]{2,1,0:T(8,128)(2,1)S(1)}, u32[]{:S(2)}, u32[]{:S(2)}) collective-permute-start(bf16[2,64,512]{2,1,0:T(8,128)(2,1)S(1)} %get-tuple-element.49), channel_id=1, source_target_pairs={{0,4},{1,5},{2,6},{3,7},{4,0},{5,1},{6,2},{7,3},{8,12},{9,13},{10,... | collective-permute-start | bytes 393224 | tf_op jit(solution)/shard_map/ppermute | solution.py:438
  59.2 1.0 collective-permute-start.5
  60.2 1.5 collective-permute-start.6
  62.4 1.5 collective-permute-start.21
  63.9 6.9 %collective-permute-done.5 = bf16[2,64,512]{2,1,0:T(8,128)(2,1)S(1)} collective-permute-done((bf16[2,64,512]{2,1,0:T(8,128)(2,1)S(1)}, bf16[2,64,512]{2,1,0:T(8,128)(2,1)S(1)}, u32[]{:S(2)}, u32[]{:S(2)}) %collective-permute-start.5) | collective-permute-done | bytes 131104 | tf_op jit(solution)/shard_map/ppermute | solution.py:438
  70.9 3.5 %collective-permute-start.11 = (bf16[2,64,512]{2,1,0:T(8,128)(2,1)S(1)}, bf16[2,64,512]{2,1,0:T(8,128)(2,1)S(1)}, u32[]{:S(2)}, u32[]{:S(2)}) collective-permute-start(bf16[2,64,512]{2,1,0:T(8,128)(2,1)S(1)} %fusion.14), channel_id=1, source_target_pairs={{0,12},{1,13},{2,14},{3,15},{4,8},{5,9},{6,10},{7,11},{8,4},{9,5},... | collective-permute-start | bytes 393224 | tf_op jit(solution)/shard_map/ppermute | solution.py:438
  74.3 2.7 %constant_dynamic-slice_fusion.1 = bf16[2,1024,1280]{2,1,0:T(8,128)(2,1)} fusion(bf16[2,1024,2560]{2,1,0:T(8,128)(2,1)S(1)} %copy-done, s32[]{:T(128)S(6)} %select_n.188), kind=kLoop, calls=%fused_computation.56 | loop fusion | bytes 10485764 | tf_op jit(solution)/shard_map/dynamic_slice | solution.py:504
  77.0 1.5 collective-permute-start.10
  78.5 1.6 collective-permute-start.24
  80.1 1.0 collective-permute-start.22
  81.1 5.5 %collective-permute-done.10 = bf16[2,64,512]{2,1,0:T(8,128)(2,1)S(1)} collective-permute-done((bf16[2,64,512]{2,1,0:T(8,128)(2,1)S(1)}, bf16[2,64,512]{2,1,0:T(8,128)(2,1)S(1)}, u32[]{:S(2)}, u32[]{:S(2)}) %collective-permute-start.10) | collective-permute-done | bytes 131104 | tf_op jit(solution)/shard_map/ppermute | solution.py:438
  86.6 1.5 collective-permute-start.26
  88.5 2.1 %collective-permute-done.24.p1 = bf16[64,3072]{1,0:T(8,128)(2,1)S(1)} collective-permute-done((bf16[64,3072]{1,0:T(8,128)(2,1)S(1)}, bf16[64,3072]{1,0:T(8,128)(2,1)S(1)}, u32[]{:S(2)}, u32[]{:S(2)}) %collective-permute-start.24) | collective-permute-done | bytes 393248 | tf_op jit(solution)/shard_map/ppermute | solution.py:438
  90.6 1.0 collective-permute-start.16
  92.1 1.0 collective-permute-start.12
  93.1 5.9 %collective-permute-done.26.p3 = bf16[64,3072]{1,0:T(8,128)(2,1)S(1)} collective-permute-done((bf16[64,3072]{1,0:T(8,128)(2,1)S(1)}, bf16[64,3072]{1,0:T(8,128)(2,1)S(1)}, u32[]{:S(2)}, u32[]{:S(2)}) %collective-permute-start.26) | collective-permute-done | bytes 393248 | tf_op jit(solution)/shard_map/ppermute | solution.py:438
  99.0 1.5 collective-permute-start.15
  100.5 1.0 collective-permute-start.13
  101.5 4.6 %collective-permute-done.16.refs_6_ = bf16[4,64,512]{2,1,0:T(8,128)(2,1)S(1)} collective-permute-done((bf16[4,64,512]{2,1,0:T(8,128)(2,1)S(1)}, bf16[4,64,512]{2,1,0:T(8,128)(2,1)S(1)}, u32[]{:S(2)}, u32[]{:S(2)}) %collective-permute-start.16) | collective-permute-done | bytes 262176 | tf_op jit(solution)/shard_map/ppermute | solution.py:438
  106.6 1.0 collective-permute-start.14
  107.7 3.7 %invert_factor.3 = (bf16[1024,1024]{1,0:T(8,128)(2,1)S(1)}, bf16[1024,1024]{1,0:T(8,128)(2,1)S(1)}) custom-call(s32[4]{0:T(128)S(1)} %iota_xor_fusion.place_ref, bf16[64,3072]{1,0:T(8,128)(2,1)S(1)} %get-tuple-element.45.p0, bf16[64,3072]{1,0:T(8,128)(2,1)S(1)} %collective-permute-done.24.p1, bf16[64,3072]{1,0:T(8,128)(2,1)S(1)} %collective-permute-done.25.p2, ...), custom_call_target="tpu_custom_call" | custom-call | tf_op jit(solution)/shard_map/invert_factor/pallas_call | solution.py:516
  111.4 3.9 %invert_factor.2 = (bf16[1024,1024]{1,0:T(8,128)(2,1)S(1)}, bf16[1024,1024]{1,0:T(8,128)(2,1)S(1)}) custom-call(s32[4]{0:T(128)S(1)} %iota_xor_fusion.place_ref, bf16[64,3072]{1,0:T(8,128)(2,1)S(1)} %get-tuple-element.46.p0, bf16[64,3072]{1,0:T(8,128)(2,1)S(1)} %collective-permute-done.21.p1, bf16[64,3072]{1,0:T(8,128)(2,1)S(1)} %collective-permute-done.22.p2, ...), custom_call_target="tpu_custom_call" | custom-call | tf_op jit(solution)/shard_map/invert_factor/pallas_call | solution.py:516
  115.4 0.9 collective-permute-done.14.refs_3_
  116.4 7.6 %apply_panel.1 = (bf16[2,1024,1024]{2,1,0:T(8,128)(2,1)S(1)}, f32[512,512]{1,0:T(8,128)S(1)}) custom-call(s32[32]{0:T(128)S(1)} %pad_add_fusion.2.place_ref, bf16[4,64,512]{2,1,0:T(8,128)(2,1)S(1)} %get-tuple-element.48.refs_0_, bf16[4,64,512]{2,1,0:T(8,128)(2,1)S(1)} %collective-permute-done.12.refs_1_, ...), custom_call_target="tpu_custom_call" | custom-call | tf_op jit(solution)/shard_map/apply_panel/pallas_call | solution.py:202
  124.6 8.1 %collective-permute-done.28.other_ref = f32[512,512]{1,0:T(8,128)S(1)} collective-permute-done((f32[512,512]{1,0:T(8,128)S(1)}, f32[512,512]{1,0:T(8,128)S(1)}, u32[]{:S(2)}, u32[]{:S(2)}) %collective-permute-start.28) | collective-permute-done | bytes 1048608 | tf_op jit(solution)/shard_map/ppermute | solution.py:435
  132.7 23.8 %chol_inverse.1.inv_ref = f32[512,512]{1,0:T(8,128)S(1)} custom-call(f32[512,512]{1,0:T(8,128)S(1)} %get-tuple-element.36.block_ref, f32[512,512]{1,0:T(8,128)S(1)} %collective-permute-done.28.other_ref, f32[1,512]{1,0:T(1,128)S(1)} %bitcast.53), custom_call_target="tpu_custom_call" | custom-call | tf_op jit(solution)/shard_map/chol_inverse/pallas_call | solution.py:359
  156.5 13.9 %normals.1 = f32[512,1280]{1,0:T(8,128)} custom-call(s32[22]{0:T(128)S(1)} %pad_add_fusion.1.info, bf16[2,1024,2560]{2,1,0:T(8,128)(2,1)} %own.1, bf16[2,1024,1280]{2,1,0:T(8,128)(2,1)S(1)} %collective-permute-done.8.far, bf16[2,1024,1024]{2,1,0:T(8,128)(2,1)S(1)} %get-tuple-element.35.qown, bf16[2,1024,1024]{2,1,0:T(8,128)(2,1)S(1)} %collective-permute-done.27.qfar, ...), custom_call_target="tpu_custom_call" | custom-call | tf_op jit(solution)/shard_map/normals/pallas_call | solution.py:269
  (69 shorter events, 6.8 us)
Async XLA Ops:
  0.0 20.7 %collective-permute-start.7 = (s32[2,80]{1,0:T(2,128)}, s32[2,80]{1,0:T(2,128)S(1)}, u32[]{:S(2)}, u32[]{:S(2)}) collective-permute-start(s32[2,80]{1,0:T(2,128)} %param.7), channel_id=1, source_target_pairs={{0,16},{16,0},{1,17},{17,1},{2,18},{18,2},{3,19},{19,3},{4,20},{20... | collective-permute-start | bytes 1928 | tf_op jit(solution)/shard_map/ppermute | solution.py:435
  2.3 2.9 %copy-start.2 = (f32[2,64,1024]{2,1,0:T(8,128)S(1)}, f32[2,64,1024]{2,1,0:T(8,128)}, u32[]{:S(2)}) copy-start(f32[2,64,1024]{2,1,0:T(8,128)} %param.6) | copy-start | bytes 1572868
  2.3 20.0 %copy-start.3 = (s32[2,80]{1,0:T(2,128)S(1)}, s32[2,80]{1,0:T(2,128)}, u32[]{:S(2)}) copy-start(s32[2,80]{1,0:T(2,128)} %param.7) | copy-start | bytes 1924
  9.6 30.3 %copy-start.1 = (bf16[2,64,128]{2,1,0:T(8,128)(2,1)S(1)}, bf16[2,64,128]{2,1,0:T(8,128)(2,1)}, u32[]{:S(2)}) copy-start(bf16[2,64,128]{2,1,0:T(8,128)(2,1)} %get-tuple-element.29) | copy-start | bytes 98308
  11.9 16.4 %collective-permute-start.20 = (bf16[2,64,1152]{2,1,0:T(8,128)(2,1)}, bf16[2,64,1152]{2,1,0:T(8,128)(2,1)S(1)}, u32[]{:S(2)}, u32[]{:S(2)}) collective-permute-start(bf16[2,64,1152]{2,1,0:T(8,128)(2,1)} %pad_maximum_fusion.1), channel_id=1, source_target_pairs={{0,4},{1,5},{2,6},{3,7},{4,0},{5,1},{6,2},{7,3},{8,12},{9,13},{10,... | collective-permute-start | bytes 884744 | tf_op jit(solution)/shard_map/ppermute | solution.py:438
  14.5 23.7 %collective-permute-start.19 = (bf16[2,64,1152]{2,1,0:T(8,128)(2,1)}, bf16[2,64,1152]{2,1,0:T(8,128)(2,1)S(1)}, u32[]{:S(2)}, u32[]{:S(2)}) collective-permute-start(bf16[2,64,1152]{2,1,0:T(8,128)(2,1)} %pad_maximum_fusion.1), channel_id=1, source_target_pairs={{0,8},{1,9},{2,10},{3,11},{4,12},{5,13},{6,14},{7,15},{8,0},{9,1},... | collective-permute-start | bytes 884744 | tf_op jit(solution)/shard_map/ppermute | solution.py:438
  17.2 20.9 %collective-permute-start.18 = (bf16[2,64,1152]{2,1,0:T(8,128)(2,1)}, bf16[2,64,1152]{2,1,0:T(8,128)(2,1)S(1)}, u32[]{:S(2)}, u32[]{:S(2)}) collective-permute-start(bf16[2,64,1152]{2,1,0:T(8,128)(2,1)} %pad_maximum_fusion.1), channel_id=1, source_target_pairs={{0,12},{1,13},{2,14},{3,15},{4,8},{5,9},{6,10},{7,11},{8,4},{9,5},... | collective-permute-start | bytes 884744 | tf_op jit(solution)/shard_map/ppermute | solution.py:438
  17.2 22.9 %collective-permute-start = (bf16[512,512]{1,0:T(8,128)(2,1)S(1)}, bf16[512,512]{1,0:T(8,128)(2,1)}, u32[]{:S(2)}, u32[]{:S(2)}) collective-permute-start(bf16[512,512]{1,0:T(8,128)(2,1)S(1)} %get-tuple-element.22), channel_id=1, source_target_pairs={{0,1},{1,0},{2,3},{3,2},{4,5},{5,4},{6,7},{7,6},{8,9},{9,8},{10,11... | collective-permute-start | bytes 1572872 | tf_op jit(solution)/shard_map/ppermute | solution.py:438
  20.7 22.2 %collective-permute-start.2 = (bf16[512,512]{1,0:T(8,128)(2,1)S(1)}, bf16[512,512]{1,0:T(8,128)(2,1)}, u32[]{:S(2)}, u32[]{:S(2)}) collective-permute-start(bf16[512,512]{1,0:T(8,128)(2,1)S(1)} %get-tuple-element.23), channel_id=1, source_target_pairs={{0,2},{1,3},{2,0},{3,1},{4,6},{5,7},{6,4},{7,5},{8,10},{9,11},{10,... | collective-permute-start | bytes 1572872 | tf_op jit(solution)/shard_map/ppermute | solution.py:438
  39.9 34.4 %copy-start = (bf16[2,1024,2560]{2,1,0:T(8,128)(2,1)S(1)}, bf16[2,1024,2560]{2,1,0:T(8,128)(2,1)}, u32[]{:S(2)}) copy-start(bf16[2,1024,2560]{2,1,0:T(8,128)(2,1)} %own.1) | copy-start | bytes 31457284
  41.3 7.2 %collective-permute-start.1 = (bf16[256,512]{1,0:T(8,128)(2,1)S(1)}, bf16[256,512]{1,0:T(8,128)(2,1)S(1)}, u32[]{:S(2)}, u32[]{:S(2)}) collective-permute-start(bf16[256,512]{1,0:T(8,128)(2,1)S(1)} %dynamic-slice_add_fusion.1), channel_id=1, source_target_pairs={{0,2},{1,3},{2,0},{3,1},{4,6},{5,7},{6,4},{7,5},{8,10},{9,11},{10,... | collective-permute-start | bytes 786440 | tf_op jit(solution)/shard_map/ppermute | solution.py:438
  44.0 7.2 %collective-permute-start.3 = (bf16[256,512]{1,0:T(8,128)(2,1)S(1)}, bf16[256,512]{1,0:T(8,128)(2,1)S(1)}, u32[]{:S(2)}, u32[]{:S(2)}) collective-permute-start(bf16[256,512]{1,0:T(8,128)(2,1)S(1)} %dynamic-slice_add_fusion), channel_id=1, source_target_pairs={{0,1},{1,0},{2,3},{3,2},{4,5},{5,4},{6,7},{7,6},{8,9},{9,8},{10,11... | collective-permute-start | bytes 786440 | tf_op jit(solution)/shard_map/ppermute | solution.py:438
  52.3 11.7 %collective-permute-start.4 = (bf16[2,64,512]{2,1,0:T(8,128)(2,1)S(1)}, bf16[2,64,512]{2,1,0:T(8,128)(2,1)S(1)}, u32[]{:S(2)}, u32[]{:S(2)}) collective-permute-start(bf16[2,64,512]{2,1,0:T(8,128)(2,1)S(1)} %get-tuple-element.49), channel_id=1, source_target_pairs={{0,4},{1,5},{2,6},{3,7},{4,0},{5,1},{6,2},{7,3},{8,12},{9,13},{10,... | collective-permute-start | bytes 393224 | tf_op jit(solution)/shard_map/ppermute | solution.py:438
  59.2 11.6 %collective-permute-start.5 = (bf16[2,64,512]{2,1,0:T(8,128)(2,1)S(1)}, bf16[2,64,512]{2,1,0:T(8,128)(2,1)S(1)}, u32[]{:S(2)}, u32[]{:S(2)}) collective-permute-start(bf16[2,64,512]{2,1,0:T(8,128)(2,1)S(1)} %get-tuple-element.50), channel_id=1, source_target_pairs={{0,8},{1,9},{2,10},{3,11},{4,12},{5,13},{6,14},{7,15},{8,0},{9,1},... | collective-permute-start | bytes 393224 | tf_op jit(solution)/shard_map/ppermute | solution.py:438
  60.2 10.6 %collective-permute-start.6 = (bf16[2,64,512]{2,1,0:T(8,128)(2,1)S(1)}, bf16[2,64,512]{2,1,0:T(8,128)(2,1)S(1)}, u32[]{:S(2)}, u32[]{:S(2)}) collective-permute-start(bf16[2,64,512]{2,1,0:T(8,128)(2,1)S(1)} %get-tuple-element.51), channel_id=1, source_target_pairs={{0,12},{1,13},{2,14},{3,15},{4,8},{5,9},{6,10},{7,11},{8,4},{9,5},... | collective-permute-start | bytes 393224 | tf_op jit(solution)/shard_map/ppermute | solution.py:438
  61.7 16.8 %collective-permute-start.25 = (bf16[64,3072]{1,0:T(8,128)(2,1)S(1)}, bf16[64,3072]{1,0:T(8,128)(2,1)S(1)}, u32[]{:S(2)}, u32[]{:S(2)}) collective-permute-start(bf16[64,3072]{1,0:T(8,128)(2,1)S(1)} %get-tuple-element.45.p0), channel_id=1, source_target_pairs={{0,2},{1,3},{2,0},{3,1},{4,6},{5,7},{6,4},{7,5},{8,10},{9,11},{10,... | collective-permute-start | bytes 1179656 | tf_op jit(solution)/shard_map/ppermute | solution.py:438
  62.4 16.1 %collective-permute-start.21 = (bf16[64,3072]{1,0:T(8,128)(2,1)S(1)}, bf16[64,3072]{1,0:T(8,128)(2,1)S(1)}, u32[]{:S(2)}, u32[]{:S(2)}) collective-permute-start(bf16[64,3072]{1,0:T(8,128)(2,1)S(1)} %get-tuple-element.46.p0), channel_id=1, source_target_pairs={{0,1},{1,0},{2,3},{3,2},{4,5},{5,4},{6,7},{7,6},{8,9},{9,8},{10,11... | collective-permute-start | bytes 1179656 | tf_op jit(solution)/shard_map/ppermute | solution.py:438
  70.9 9.3 %collective-permute-start.11 = (bf16[2,64,512]{2,1,0:T(8,128)(2,1)S(1)}, bf16[2,64,512]{2,1,0:T(8,128)(2,1)S(1)}, u32[]{:S(2)}, u32[]{:S(2)}) collective-permute-start(bf16[2,64,512]{2,1,0:T(8,128)(2,1)S(1)} %fusion.14), channel_id=1, source_target_pairs={{0,12},{1,13},{2,14},{3,15},{4,8},{5,9},{6,10},{7,11},{8,4},{9,5},... | collective-permute-start | bytes 393224 | tf_op jit(solution)/shard_map/ppermute | solution.py:438
  77.0 79.5 %collective-permute-start.8 = (bf16[2,1024,1280]{2,1,0:T(8,128)(2,1)}, bf16[2,1024,1280]{2,1,0:T(8,128)(2,1)S(1)}, u32[]{:S(2)}, u32[]{:S(2)}) collective-permute-start(bf16[2,1024,1280]{2,1,0:T(8,128)(2,1)} %constant_dynamic-slice_fusion.1), channel_id=1, source_target_pairs={{0,16},{16,0},{1,17},{17,1},{2,18},{18,2},{3,19},{19,3},{4,20},{20... | collective-permute-start | bytes 15728648 | tf_op jit(solution)/shard_map/ppermute | solution.py:435
  77.0 9.6 %collective-permute-start.10 = (bf16[2,64,512]{2,1,0:T(8,128)(2,1)S(1)}, bf16[2,64,512]{2,1,0:T(8,128)(2,1)S(1)}, u32[]{:S(2)}, u32[]{:S(2)}) collective-permute-start(bf16[2,64,512]{2,1,0:T(8,128)(2,1)S(1)} %fusion.14), channel_id=1, source_target_pairs={{0,8},{1,9},{2,10},{3,11},{4,12},{5,13},{6,14},{7,15},{8,0},{9,1},... | collective-permute-start | bytes 393224 | tf_op jit(solution)/shard_map/ppermute | solution.py:438
  78.5 9.6 %collective-permute-start.9 = (bf16[2,64,512]{2,1,0:T(8,128)(2,1)S(1)}, bf16[2,64,512]{2,1,0:T(8,128)(2,1)S(1)}, u32[]{:S(2)}, u32[]{:S(2)}) collective-permute-start(bf16[2,64,512]{2,1,0:T(8,128)(2,1)S(1)} %fusion.14), channel_id=1, source_target_pairs={{0,4},{1,5},{2,6},{3,7},{4,0},{5,1},{6,2},{7,3},{8,12},{9,13},{10,... | collective-permute-start | bytes 393224 | tf_op jit(solution)/shard_map/ppermute | solution.py:438
  78.5 12.1 %collective-permute-start.24 = (bf16[64,3072]{1,0:T(8,128)(2,1)S(1)}, bf16[64,3072]{1,0:T(8,128)(2,1)S(1)}, u32[]{:S(2)}, u32[]{:S(2)}) collective-permute-start(bf16[64,3072]{1,0:T(8,128)(2,1)S(1)} %get-tuple-element.45.p0), channel_id=1, source_target_pairs={{0,1},{1,0},{2,3},{3,2},{4,5},{5,4},{6,7},{7,6},{8,9},{9,8},{10,11... | collective-permute-start | bytes 1179656 | tf_op jit(solution)/shard_map/ppermute | solution.py:438
  80.1 12.0 %collective-permute-start.22 = (bf16[64,3072]{1,0:T(8,128)(2,1)S(1)}, bf16[64,3072]{1,0:T(8,128)(2,1)S(1)}, u32[]{:S(2)}, u32[]{:S(2)}) collective-permute-start(bf16[64,3072]{1,0:T(8,128)(2,1)S(1)} %get-tuple-element.46.p0), channel_id=1, source_target_pairs={{0,2},{1,3},{2,0},{3,1},{4,6},{5,7},{6,4},{7,5},{8,10},{9,11},{10,... | collective-permute-start | bytes 1179656 | tf_op jit(solution)/shard_map/ppermute | solution.py:438
  86.6 12.4 %collective-permute-start.26 = (bf16[64,3072]{1,0:T(8,128)(2,1)S(1)}, bf16[64,3072]{1,0:T(8,128)(2,1)S(1)}, u32[]{:S(2)}, u32[]{:S(2)}) collective-permute-start(bf16[64,3072]{1,0:T(8,128)(2,1)S(1)} %collective-permute-done.25.p2), channel_id=1, source_target_pairs={{0,1},{1,0},{2,3},{3,2},{4,5},{5,4},{6,7},{7,6},{8,9},{9,8},{10,11... | collective-permute-start | bytes 1179656 | tf_op jit(solution)/shard_map/ppermute | solution.py:438
  88.1 12.4 %collective-permute-start.23 = (bf16[64,3072]{1,0:T(8,128)(2,1)S(1)}, bf16[64,3072]{1,0:T(8,128)(2,1)S(1)}, u32[]{:S(2)}, u32[]{:S(2)}) collective-permute-start(bf16[64,3072]{1,0:T(8,128)(2,1)S(1)} %collective-permute-done.21.p1), channel_id=1, source_target_pairs={{0,2},{1,3},{2,0},{3,1},{4,6},{5,7},{6,4},{7,5},{8,10},{9,11},{10,... | collective-permute-start | bytes 1179656 | tf_op jit(solution)/shard_map/ppermute | solution.py:438
  90.6 15.5 %collective-permute-start.16 = (bf16[4,64,512]{2,1,0:T(8,128)(2,1)S(1)}, bf16[4,64,512]{2,1,0:T(8,128)(2,1)S(1)}, u32[]{:S(2)}, u32[]{:S(2)}) collective-permute-start(bf16[4,64,512]{2,1,0:T(8,128)(2,1)S(1)} %get-tuple-element.47.refs_4_), channel_id=1, source_target_pairs={{0,2},{1,3},{2,0},{3,1},{4,6},{5,7},{6,4},{7,5},{8,10},{9,11},{10,... | collective-permute-start | bytes 786440 | tf_op jit(solution)/shard_map/ppermute | solution.py:438
  92.1 14.6 %collective-permute-start.12 = (bf16[4,64,512]{2,1,0:T(8,128)(2,1)S(1)}, bf16[4,64,512]{2,1,0:T(8,128)(2,1)S(1)}, u32[]{:S(2)}, u32[]{:S(2)}) collective-permute-start(bf16[4,64,512]{2,1,0:T(8,128)(2,1)S(1)} %get-tuple-element.48.refs_0_), channel_id=1, source_target_pairs={{0,1},{1,0},{2,3},{3,2},{4,5},{5,4},{6,7},{7,6},{8,9},{9,8},{10,11... | collective-permute-start | bytes 786440 | tf_op jit(solution)/shard_map/ppermute | solution.py:438
  99.0 16.4 %collective-permute-start.15 = (bf16[4,64,512]{2,1,0:T(8,128)(2,1)S(1)}, bf16[4,64,512]{2,1,0:T(8,128)(2,1)S(1)}, u32[]{:S(2)}, u32[]{:S(2)}) collective-permute-start(bf16[4,64,512]{2,1,0:T(8,128)(2,1)S(1)} %get-tuple-element.47.refs_4_), channel_id=1, source_target_pairs={{0,1},{1,0},{2,3},{3,2},{4,5},{5,4},{6,7},{7,6},{8,9},{9,8},{10,11... | collective-permute-start | bytes 786440 | tf_op jit(solution)/shard_map/ppermute | solution.py:438
  100.5 14.9 %collective-permute-start.13 = (bf16[4,64,512]{2,1,0:T(8,128)(2,1)S(1)}, bf16[4,64,512]{2,1,0:T(8,128)(2,1)S(1)}, u32[]{:S(2)}, u32[]{:S(2)}) collective-permute-start(bf16[4,64,512]{2,1,0:T(8,128)(2,1)S(1)} %get-tuple-element.48.refs_0_), channel_id=1, source_target_pairs={{0,2},{1,3},{2,0},{3,1},{4,6},{5,7},{6,4},{7,5},{8,10},{9,11},{10,... | collective-permute-start | bytes 786440 | tf_op jit(solution)/shard_map/ppermute | solution.py:438
  106.1 9.3 %collective-permute-start.17 = (bf16[4,64,512]{2,1,0:T(8,128)(2,1)S(1)}, bf16[4,64,512]{2,1,0:T(8,128)(2,1)S(1)}, u32[]{:S(2)}, u32[]{:S(2)}) collective-permute-start(bf16[4,64,512]{2,1,0:T(8,128)(2,1)S(1)} %collective-permute-done.16.refs_6_), channel_id=1, source_target_pairs={{0,1},{1,0},{2,3},{3,2},{4,5},{5,4},{6,7},{7,6},{8,9},{9,8},{10,11... | collective-permute-start | bytes 786440 | tf_op jit(solution)/shard_map/ppermute | solution.py:438
  106.6 9.7 %collective-permute-start.14 = (bf16[4,64,512]{2,1,0:T(8,128)(2,1)S(1)}, bf16[4,64,512]{2,1,0:T(8,128)(2,1)S(1)}, u32[]{:S(2)}, u32[]{:S(2)}) collective-permute-start(bf16[4,64,512]{2,1,0:T(8,128)(2,1)S(1)} %collective-permute-done.12.refs_1_), channel_id=1, source_target_pairs={{0,2},{1,3},{2,0},{3,1},{4,6},{5,7},{6,4},{7,5},{8,10},{9,11},{10,... | collective-permute-start | bytes 786440 | tf_op jit(solution)/shard_map/ppermute | solution.py:438
  124.0 32.5 %collective-permute-start.27 = (bf16[2,1024,1024]{2,1,0:T(8,128)(2,1)S(1)}, bf16[2,1024,1024]{2,1,0:T(8,128)(2,1)S(1)}, u32[]{:S(2)}, u32[]{:S(2)}) collective-permute-start(bf16[2,1024,1024]{2,1,0:T(8,128)(2,1)S(1)} %get-tuple-element.35.qown), channel_id=1, source_target_pairs={{0,16},{16,0},{1,17},{17,1},{2,18},{18,2},{3,19},{19,3},{4,20},{20... | collective-permute-start | bytes 12582920 | tf_op jit(solution)/shard_map/ppermute | solution.py:435
  124.1 8.6 %collective-permute-start.28 = (f32[512,512]{1,0:T(8,128)S(1)}, f32[512,512]{1,0:T(8,128)S(1)}, u32[]{:S(2)}, u32[]{:S(2)}) collective-permute-start(f32[512,512]{1,0:T(8,128)S(1)} %get-tuple-element.36.block_ref), channel_id=1, source_target_pairs={{0,16},{16,0},{1,17},{17,1},{2,18},{18,2},{3,19},{19,3},{4,20},{20... | collective-permute-start | bytes 3145736 | tf_op jit(solution)/shard_map/ppermute | solution.py:435
where the time goes:
time: 172 us; the launch traced here: 171 us
  Pallas kernels  56.7 us (33%)
  waiting for transfers between devices  54.5 us (32%)
  starting transfers between devices  39.7 us (23%)
  other arithmetic  12.2 us (7%)
  local copies, waits for them, and re-layouts  6.26 us (4%)
    ppermute x25, waiting for transfers between devices, hop(): return lax.ppermute(value, 'par', [(p, p ^ bits) for p in range(chips)])  46.3 us
    ppermute x25, starting transfers between devices, hop(): return lax.ppermute(value, 'par', [(p, p ^ bits) for p in range(chips)])  38.7 us
    pallas_call x1, Pallas kernels, chol_inverse(): pl.pallas_call(chol_kernel, out_shape=jax.ShapeDtypeStruct((size, size),...  23.8 us
    pallas_call x1, Pallas kernels, normals_call(): pl.pallas_call(normals_kernel, out_shape=jax.ShapeDtypeStruct((width, sha...  13.9 us
    ppermute x4, waiting for transfers between devices, swap(): return lax.ppermute(value, 'arc', [(0, 1), (1, 0)])  8.16 us
    pallas_call x2, Pallas kernels, paired(): factors += call(seats, *[pieces[k] for k in range(4)])  7.68 us
    pallas_call x1, Pallas kernels, apply_call(): pl.pallas_call(functools.partial(apply_kernel, arcs), out_shape=(jax.Shap...  7.63 us
    pallas_call x1, Pallas kernels, invert_diag(): pl.pallas_call(diag_kernel, out_shape=(out, out), in_specs=[pl.BlockSpec(...  3.81 us
  transfers between devices with their start and end apart: 29, of which 12 were waited for; matrix products, arithmetic and copies ran while one was open for 10% of the time, Pallas kernels for 25%

commit v1 on v0

--- a/solution.py
+++ b/solution.py
@@ -6,6 +6,7 @@
 from jax.experimental import pallas as pl
 from jax.experimental.pallas import tpu as pltpu
 from jax.sharding import PartitionSpec as P
+
 
 PANEL = 512
 BLK = 256
@@ -36,15 +37,6 @@
         & ((rows // step) % 2 == 1)
         & ((cols // step) % 2 == 0)
     )
-
-
-def invert_levels(inverse, lower, first, last):
-    step = first
-    while step < last:
-        below = jnp.where(level_mask(step), lower, 0.0)
-        inverse = inverse - mm3(inverse, mm3(below, inverse))
-        step *= 2
-    return inverse
 
 
 def diag_kernel(off_ref, strip_ref, high, low, square):
@@ -160,26 +152,13 @@
     )
 
 
-def apply_panel(raw, high, low, pt, q_ref):
-    width, size = pt.shape
-    span = min(256, size)
-    nt = ((1,), (1,))
-    for top in range(0, size, span):
-        end = top + span
-        value = mm(raw[:, :end], high[top:end, :end], nt) + mm(raw[:, :end], low[top:end, :end], nt)
-        pt[:, top:end] = value.astype(BF16)
-    for top in range(0, size, span):
-        end = top + span
-        part = pt[:, top:]
-        value = mm(part, high[top:, top:end]) + mm(part, low[top:, top:end])
-        q_ref[:width, top:end], q_ref[width:, top:end] = split(value)
-
-
-def apply_kernel(arcs, place_ref, *refs):
-    count = (len(refs) - 4) // arcs - 2
+def panel_kernel(arcs, place_ref, *refs):
+    count = (len(refs) - 3) // arcs - 2
     pieces = refs[: arcs * count]
     factors = refs[arcs * count : arcs * (count + 2)]
-    q_ref, block_ref, panel, pt = refs[arcs * (count + 2) :]
+    pt, block_ref, panel = refs[arcs * (count + 2) :]
+    size = panel.shape[0]
+    span = min(256, size)
     nt = ((1,), (1,))
     for arc in range(arcs):
         index = arc * pieces[0].shape[0] * count
@@ -190,27 +169,56 @@
                 panel[pl.ds(at, rows), :] = piece[z].astype(F32)
                 index += 1
         raw = panel[...].T.astype(BF16)
-        apply_panel(raw, factors[2 * arc], factors[2 * arc + 1], pt, q_ref.at[arc])
-        part = mm(pt[...], pt[...], nt)
+        high, low = factors[2 * arc], factors[2 * arc + 1]
+        for top in range(0, size, span):
+            end = top + span
+            value = mm(raw[:, :end], high[top:end, :end], nt) + mm(raw[:, :end], low[top:end, :end], nt)
+            pt[arc, :, top:end] = value.astype(BF16)
+        part = mm(pt[arc], pt[arc], nt)
         block_ref[...] = part if arc == 0 else block_ref[...] + part
 
 
-def apply_call(place, pieces, factors):
+def back_kernel(arcs, pt, *refs):
+    factors, q_ref = refs[: 2 * arcs], refs[2 * arcs]
+    _, width, size = pt.shape
+    span = min(256, size)
+    for arc in range(arcs):
+        high, low = factors[2 * arc], factors[2 * arc + 1]
+        for top in range(0, size, span):
+            end = top + span
+            part = pt[arc, :, top:]
+            value = mm(part, high[top:, top:end]) + mm(part, low[top:, top:end])
+            q_ref[arc, :width, top:end], q_ref[arc, width:, top:end] = split(value)
+
+
+def panel_call(place, pieces, factors):
     arcs = len(factors) // 2
     size = factors[0].shape[0]
     width = pieces[0].shape[2]
     return pl.pallas_call(
-        functools.partial(apply_kernel, arcs),
+        functools.partial(panel_kernel, arcs),
         out_shape=(
-            jax.ShapeDtypeStruct((arcs, 2 * width, size), BF16),
+            jax.ShapeDtypeStruct((arcs, width, size), BF16),
             jax.ShapeDtypeStruct((width, width), F32),
         ),
         in_specs=[SM] + [VM] * (len(pieces) + len(factors)),
         out_specs=(VM, VM),
-        scratch_shapes=[pltpu.VMEM((size, width), F32), pltpu.VMEM((width, size), BF16)],
-        compiler_params=grant(32),
-        name="apply_panel",
+        scratch_shapes=[pltpu.VMEM((size, width), F32)],
+        compiler_params=grant(26),
+        name="panel_block",
     )(place, *pieces, *factors)
+
+
+def back_call(pt, factors):
+    arcs, width, size = pt.shape
+    return pl.pallas_call(
+        functools.partial(back_kernel, arcs),
+        out_shape=jax.ShapeDtypeStruct((arcs, 2 * width, size), BF16),
+        in_specs=[VM] * (1 + len(factors)),
+        out_specs=VM,
+        compiler_params=grant(26),
+        name="back_solve",
+    )(pt, *factors)
 
 
 def normals_kernel(info, own, far, qown, qfar, inv_ref, reg_ref, out_ref, data, qs, acc, sems):
@@ -280,6 +288,7 @@
         compiler_params=grant(36),
         name="normals",
     )(info, own, far, qown, qfar, inverse, reg)
+
 
 SUB = 8
 
@@ -405,7 +414,8 @@
         call = invert_call(functools.partial(invert_dense_kernel, rows), observed, 1, [])
         factors += call(lower[arc])
     place = jnp.zeros((arcs,), jnp.int32)
-    qs, block = apply_call(place, [panel[arc : arc + 1] for arc in range(arcs)], factors)
+    pt, block = panel_call(place, [panel[arc : arc + 1] for arc in range(arcs)], factors)
+    qs = back_call(pt, factors)
     both = jnp.einsum("apo,aoc->pc", qs, masked, preferred_element_type=F32)
     gram = both[:PANEL] + both[PANEL:]
     share = columns // lax.axis_size("arc")
@@ -466,7 +476,9 @@
                 gone, at, quarter, 0
             )
 
-        value = piece(sides[second]) + hop(piece(1 - sides[second]), 1 << second)
+        again = piece(1 - sides[second])
+        again = hop(again, 1 << second)
+        value = piece(sides[second]) + again
         seeds.append(value.reshape(planes, rows, PANEL))
     seeds = jnp.stack(seeds, axis=1)
     chunk = lax.dynamic_index_in_dim(seeds, plane, 0, False)
@@ -474,7 +486,9 @@
         chunk += hop(lax.dynamic_index_in_dim(seeds, plane ^ k, 0, False), 4 * k)
 
     lower = factor_rows(cov_factor, me)
-    stack = [lower] + [hop(lower, 4 * k) for k in range(1, planes)]
+    stack = [lower]
+    for k in range(1, planes):
+        stack.append(hop(lower, 4 * k))
     packed = []
     for index in range(planes):
         width = LANE + 4 * rows * (index + 1)
@@ -501,7 +515,8 @@
         order = (bits[arc % 2] * 2 + bits[1 - arc % 2]) * planes + (source >> 2)
         place.append(order.reshape(-1) * rows)
     place = jnp.concatenate(place)
-    far = swap(lax.dynamic_slice_in_dim(design, (1 - core) * share, share, 2))
+    far = lax.dynamic_slice_in_dim(design, (1 - core) * share, share, 2)
+    far = swap(far)
     chunk, seats, info, reg, reg_panel, place = lax.optimization_barrier(
         (chunk, seats, info, reg, reg_panel, place)
     )
@@ -520,8 +535,11 @@
     for arc in range(arcs):
         found = spread(stack[arc], 1 + arc % 2)
         pieces += [found[k] for k in range(4)]
-    qs, block = apply_call(place, pieces, factors)
-    inverse = chol_inverse(block, swap(block), reg_panel)
+    pt, block = panel_call(place, pieces, factors)
+    other = swap(block)
+    qs = back_call(pt, factors)
+    qs, other = lax.optimization_barrier((qs, other))
+    inverse = chol_inverse(block, other, reg_panel)
     return normals_call(info, design, far, qs, swap(qs), inverse, reg)
 
 

time: 172 us -> 174 us (1.012)
  the two profiles are of different devices: /device:TPU:0 before, /device:TPU:22 now
where the time goes in v1:
time: 174 us; the launch traced here: 173 us
  waiting for transfers between devices  62.1 us (36%)
  Pallas kernels  61.4 us (35%)
  starting transfers between devices  26 us (15%)
  other arithmetic  13.2 us (8%)
  local copies, waits for them, and re-layouts  9.33 us (5%)
    ppermute x25, waiting for transfers between devices, hop(): return lax.ppermute(value, 'par', [(p, p ^ bits) for p in range(chips)])  62.1 us
    ppermute x25, starting transfers between devices, hop(): return lax.ppermute(value, 'par', [(p, p ^ bits) for p in range(chips)])  25.4 us
    pallas_call x1, Pallas kernels, chol_inverse(): pl.pallas_call(chol_kernel, out_shape=jax.ShapeDtypeStruct((size, size),...  23.7 us
    pallas_call x1, Pallas kernels, normals_call(): pl.pallas_call(normals_kernel, out_shape=jax.ShapeDtypeStruct((width, sha...  16.7 us
    pallas_call x2, Pallas kernels, paired(): factors += call(seats, *[pieces[k] for k in range(4)])  7.96 us
    pallas_call x1, Pallas kernels, panel_call(): pl.pallas_call(functools.partial(panel_kernel, arcs), out_shape=(jax.Shap...  6.42 us
    dynamic_slice x1, local copies, waits for them, and re-layouts, paired(): far = lax.dynamic_slice_in_dim(design, (1 - core) * share, share, 2)  5.15 us
    pallas_call x1, Pallas kernels, invert_diag(): pl.pallas_call(diag_kernel, out_shape=(out, out), in_specs=[pl.BlockSpec(...  3.78 us
  transfers between devices with their start and end apart: 29, of which 13 were waited for; matrix products, arithmetic and copies ran while one was open for 12% of the time, Pallas kernels for 22%

profile of v1, /device:TPU:22, one launch (start us, length us, event | category | flops | bytes accessed | tf_op | source)
XLA Modules:
  0.0 173.2 jit_solution(15633153089229194874)
XLA Ops:
  0.7 0.9 compare_reduce_fusion.1
  1.8 3.0 %bitcast_select_fusion = (bf16[512,512]{1,0:T(8,128)(2,1)S(1)}, bf16[512,512]{1,0:T(8,128)(2,1)S(1)}, bf16[512,512]{1,0:T(8,128)(2,1)S(1)}, bf16[512,512]{1,0:T(8,128)(2,1)S(1)}) fusion(bf16[2,1024,2560]{2,1,0:T(8,128)(2,1)} %own.1, s32[]{:T(128)S(6)} %select_n.177, s32[]{:T(128)S(6)} %min.4, pred[512]{0:T(512)(128)(4,1)S(1)} %broadcast_in_dim.55, ...), kind=kLoop, calls=%fused_computation.14 | loop fusion | flops 1048576 | bytes 4195348 | tf_op jit(solution)/shard_map/jit(_where)/select_n | solution.py:463
  4.9 0.6 constant_dynamic-slice_fusion.strip_ref
  5.5 3.8 %invert_diag.1 = (bf16[2,64,128]{2,1,0:T(8,128)(2,1)}, bf16[2,64,128]{2,1,0:T(8,128)(2,1)}) custom-call(s32[1]{0:T(128)} %bitcast.26.off_ref, f32[2,64,128]{2,1,0:T(8,128)} %constant_dynamic-slice_fusion.strip_ref), custom_call_target="tpu_custom_call" | custom-call | tf_op jit(solution)/shard_map/invert_diag/pallas_call | solution.py:70
  9.3 0.8 constant_dynamic-update-slice_fusion
  10.1 1.5 pad_maximum_fusion.1
  11.6 1.6 collective-permute-start.20
  13.3 1.7 %collective-permute-start.18 = (bf16[2,64,1152]{2,1,0:T(8,128)(2,1)}, bf16[2,64,1152]{2,1,0:T(8,128)(2,1)S(1)}, u32[]{:S(2)}, u32[]{:S(2)}) collective-permute-start(bf16[2,64,1152]{2,1,0:T(8,128)(2,1)} %pad_maximum_fusion.1), channel_id=1, source_target_pairs={{0,12},{1,13},{2,14},{3,15},{4,8},{5,9},{6,10},{7,11},{8,4},{9,5},... | collective-permute-start | bytes 884744 | tf_op jit(solution)/shard_map/ppermute | solution.py:448
  16.3 0.8 dynamic_slice.78
  17.0 0.8 dynamic_slice.77
  18.8 6.5 %collective-permute-done.20 = bf16[2,64,1152]{2,1,0:T(8,128)(2,1)S(1)} collective-permute-done((bf16[2,64,1152]{2,1,0:T(8,128)(2,1)}, bf16[2,64,1152]{2,1,0:T(8,128)(2,1)S(1)}, u32[]{:S(2)}, u32[]{:S(2)}) %collective-permute-start.20) | collective-permute-done | bytes 294944 | tf_op jit(solution)/shard_map/ppermute | solution.py:448
  25.3 8.3 %collective-permute-done.19 = bf16[2,64,1152]{2,1,0:T(8,128)(2,1)S(1)} collective-permute-done((bf16[2,64,1152]{2,1,0:T(8,128)(2,1)}, bf16[2,64,1152]{2,1,0:T(8,128)(2,1)S(1)}, u32[]{:S(2)}, u32[]{:S(2)}) %collective-permute-start.19) | collective-permute-done | bytes 294944 | tf_op jit(solution)/shard_map/ppermute | solution.py:448
  33.6 7.8 %collective-permute-done.18 = bf16[2,64,1152]{2,1,0:T(8,128)(2,1)S(1)} collective-permute-done((bf16[2,64,1152]{2,1,0:T(8,128)(2,1)}, bf16[2,64,1152]{2,1,0:T(8,128)(2,1)S(1)}, u32[]{:S(2)}, u32[]{:S(2)}) %collective-permute-start.18) | collective-permute-done | bytes 294944 | tf_op jit(solution)/shard_map/ppermute | solution.py:448
  41.4 0.8 fusion.7
  42.2 0.9 fusion.3
  43.4 1.0 dynamic-slice_add_fusion.1
  44.8 1.0 dynamic-slice_add_fusion
  45.8 0.6 collective-permute-start.3
  46.5 5.5 %collective-permute-done.1 = bf16[256,512]{1,0:T(8,128)(2,1)S(1)} collective-permute-done((bf16[256,512]{1,0:T(8,128)(2,1)S(1)}, bf16[256,512]{1,0:T(8,128)(2,1)S(1)}, u32[]{:S(2)}, u32[]{:S(2)}) %collective-permute-start.1) | collective-permute-done | bytes 262176 | tf_op jit(solution)/shard_map/ppermute | solution.py:448
  52.0 1.1 add_add_fusion.1
  53.2 1.1 add_add_fusion
  54.4 2.2 %collective-permute-start.5 = (bf16[2,64,512]{2,1,0:T(8,128)(2,1)S(1)}, bf16[2,64,512]{2,1,0:T(8,128)(2,1)S(1)}, u32[]{:S(2)}, u32[]{:S(2)}) collective-permute-start(bf16[2,64,512]{2,1,0:T(8,128)(2,1)S(1)} %get-tuple-element.54), channel_id=1, source_target_pairs={{0,8},{1,9},{2,10},{3,11},{4,12},{5,13},{6,14},{7,15},{8,0},{9,1},... | collective-permute-start | bytes 393224 | tf_op jit(solution)/shard_map/ppermute | solution.py:448
  56.5 1.3 collective-permute-start.6
  57.9 1.8 %collective-permute-start.25 = (bf16[64,3072]{1,0:T(8,128)(2,1)S(1)}, bf16[64,3072]{1,0:T(8,128)(2,1)S(1)}, u32[]{:S(2)}, u32[]{:S(2)}) collective-permute-start(bf16[64,3072]{1,0:T(8,128)(2,1)S(1)} %get-tuple-element.49.p0), channel_id=1, source_target_pairs={{0,2},{1,3},{2,0},{3,1},{4,6},{5,7},{6,4},{7,5},{8,10},{9,11},{10,... | collective-permute-start | bytes 1179656 | tf_op jit(solution)/shard_map/ppermute | solution.py:448
  60.7 3.9 %collective-permute-done.5 = bf16[2,64,512]{2,1,0:T(8,128)(2,1)S(1)} collective-permute-done((bf16[2,64,512]{2,1,0:T(8,128)(2,1)S(1)}, bf16[2,64,512]{2,1,0:T(8,128)(2,1)S(1)}, u32[]{:S(2)}, u32[]{:S(2)}) %collective-permute-start.5) | collective-permute-done | bytes 131104 | tf_op jit(solution)/shard_map/ppermute | solution.py:448
  64.6 4.6 %collective-permute-done.6 = bf16[2,64,512]{2,1,0:T(8,128)(2,1)S(1)} collective-permute-done((bf16[2,64,512]{2,1,0:T(8,128)(2,1)S(1)}, bf16[2,64,512]{2,1,0:T(8,128)(2,1)S(1)}, u32[]{:S(2)}, u32[]{:S(2)}) %collective-permute-start.6) | collective-permute-done | bytes 131104 | tf_op jit(solution)/shard_map/ppermute | solution.py:448
  69.2 0.8 collective-permute-start.11
  70.0 1.4 collective-permute-start.10
  71.4 1.4 collective-permute-start.9
  73.2 1.5 collective-permute-start.22
  74.6 4.4 %collective-permute-done.11 = bf16[2,64,512]{2,1,0:T(8,128)(2,1)S(1)} collective-permute-done((bf16[2,64,512]{2,1,0:T(8,128)(2,1)S(1)}, bf16[2,64,512]{2,1,0:T(8,128)(2,1)S(1)}, u32[]{:S(2)}, u32[]{:S(2)}) %collective-permute-start.11) | collective-permute-done | bytes 131104 | tf_op jit(solution)/shard_map/ppermute | solution.py:448
  79.6 1.5 collective-permute-start.26
  81.2 1.7 collective-permute-start.16
  82.9 1.9 %collective-permute-done.24.p1 = bf16[64,3072]{1,0:T(8,128)(2,1)S(1)} collective-permute-done((bf16[64,3072]{1,0:T(8,128)(2,1)S(1)}, bf16[64,3072]{1,0:T(8,128)(2,1)S(1)}, u32[]{:S(2)}, u32[]{:S(2)}) %collective-permute-start.24) | collective-permute-done | bytes 393248 | tf_op jit(solution)/shard_map/ppermute | solution.py:448
  85.1 8.1 %collective-permute-done.21.p1 = bf16[64,3072]{1,0:T(8,128)(2,1)S(1)} collective-permute-done((bf16[64,3072]{1,0:T(8,128)(2,1)S(1)}, bf16[64,3072]{1,0:T(8,128)(2,1)S(1)}, u32[]{:S(2)}, u32[]{:S(2)}) %collective-permute-start.21) | collective-permute-done | bytes 393248 | tf_op jit(solution)/shard_map/ppermute | solution.py:448
  93.2 1.5 collective-permute-start.23
  95.0 6.6 %collective-permute-done.26.p3 = bf16[64,3072]{1,0:T(8,128)(2,1)S(1)} collective-permute-done((bf16[64,3072]{1,0:T(8,128)(2,1)S(1)}, bf16[64,3072]{1,0:T(8,128)(2,1)S(1)}, u32[]{:S(2)}, u32[]{:S(2)}) %collective-permute-start.26) | collective-permute-done | bytes 393248 | tf_op jit(solution)/shard_map/ppermute | solution.py:448
  101.6 1.5 collective-permute-start.13
  103.5 3.9 %collective-permute-done.12.refs_1_ = bf16[4,64,512]{2,1,0:T(8,128)(2,1)} collective-permute-done((bf16[4,64,512]{2,1,0:T(8,128)(2,1)S(1)}, bf16[4,64,512]{2,1,0:T(8,128)(2,1)}, u32[]{:S(2)}, u32[]{:S(2)}) %collective-permute-start.12) | collective-permute-done | bytes 262176 | tf_op jit(solution)/shard_map/ppermute | solution.py:448
  107.3 1.5 collective-permute-start.14
  108.8 3.7 %invert_factor.3 = (bf16[1024,1024]{1,0:T(8,128)(2,1)S(1)}, bf16[1024,1024]{1,0:T(8,128)(2,1)S(1)}) custom-call(s32[4]{0:T(128)S(1)} %iota_xor_fusion.place_ref, bf16[64,3072]{1,0:T(8,128)(2,1)S(1)} %get-tuple-element.49.p0, bf16[64,3072]{1,0:T(8,128)(2,1)S(1)} %collective-permute-done.24.p1, bf16[64,3072]{1,0:T(8,128)(2,1)S(1)} %collective-permute-done.25.p2, ...), custom_call_target="tpu_custom_call" | custom-call | tf_op jit(solution)/shard_map/invert_factor/pallas_call | solution.py:531
  112.6 4.2 %invert_factor.2 = (bf16[1024,1024]{1,0:T(8,128)(2,1)S(1)}, bf16[1024,1024]{1,0:T(8,128)(2,1)S(1)}) custom-call(s32[4]{0:T(128)S(1)} %iota_xor_fusion.place_ref, bf16[64,3072]{1,0:T(8,128)(2,1)S(1)} %get-tuple-element.50.p0, bf16[64,3072]{1,0:T(8,128)(2,1)S(1)} %collective-permute-done.21.p1, bf16[64,3072]{1,0:T(8,128)(2,1)S(1)} %collective-permute-done.22.p2, ...), custom_call_target="tpu_custom_call" | custom-call | tf_op jit(solution)/shard_map/invert_factor/pallas_call | solution.py:531
  116.9 0.6 copy-done.1
  117.5 6.4 %panel_block.1 = (bf16[2,512,1024]{2,1,0:T(8,128)(2,1)S(1)}, f32[512,512]{1,0:T(8,128)S(1)}) custom-call(s32[32]{0:T(128)S(1)} %copy-done.1, bf16[4,64,512]{2,1,0:T(8,128)(2,1)S(1)} %get-tuple-element.52.refs_0_, bf16[4,64,512]{2,1,0:T(8,128)(2,1)} %collective-permute-done.12.refs_1_, bf16[4,64,512]{2,1,0:T(8,128)(2,1)} %collective-permute-done.13.refs_2_, ...), custom_call_target="tpu_custom_call" | custom-call | tf_op jit(solution)/shard_map/panel_block/pallas_call | solution.py:198
  124.0 5.1 %constant_dynamic-slice_fusion.1 = bf16[2,1024,1280]{2,1,0:T(8,128)(2,1)} fusion(bf16[2,1024,2560]{2,1,0:T(8,128)(2,1)} %own.1, s32[]{:T(128)S(6)} %select_n.188), kind=kLoop, calls=%fused_computation.56 | loop fusion | bytes 10485764 | tf_op jit(solution)/shard_map/dynamic_slice | solution.py:518
  129.6 2.9 %back_solve.1.qown = bf16[2,1024,1024]{2,1,0:T(8,128)(2,1)S(1)} custom-call(bf16[2,512,1024]{2,1,0:T(8,128)(2,1)S(1)} %get-tuple-element.37.pt, bf16[1024,1024]{1,0:T(8,128)(2,1)S(1)} %get-tuple-element.33.refs_8_.refs_0_, bf16[1024,1024]{1,0:T(8,128)(2,1)S(1)} %get-tuple-element.34.refs_9_.refs_1_, ...), custom_call_target="tpu_custom_call" | custom-call | tf_op jit(solution)/shard_map/back_solve/pallas_call | solution.py:214
  132.6 23.7 %chol_inverse.1.inv_ref = f32[512,512]{1,0:T(8,128)S(1)} custom-call(f32[512,512]{1,0:T(8,128)S(1)} %get-tuple-element.38.block_ref, f32[512,512]{1,0:T(8,128)S(1)} %collective-permute-done.27.other_ref, f32[1,512]{1,0:T(1,128)S(1)} %bitcast.53), custom_call_target="tpu_custom_call" | custom-call | tf_op jit(solution)/shard_map/chol_inverse/pallas_call | solution.py:368
  156.3 16.7 %normals.1 = f32[512,1280]{1,0:T(8,128)} custom-call(s32[22]{0:T(128)S(1)} %copy-done, bf16[2,1024,2560]{2,1,0:T(8,128)(2,1)} %own.1, bf16[2,1024,1280]{2,1,0:T(8,128)(2,1)S(1)} %collective-permute-done.8.far, bf16[2,1024,1024]{2,1,0:T(8,128)(2,1)S(1)} %back_solve.1.qown, bf16[2,1024,1024]{2,1,0:T(8,128)(2,1)S(1)} %collective-permute-done.28.qfar, ...), custom_call_target="tpu_custom_call" | custom-call | tf_op jit(solution)/shard_map/normals/pallas_call | solution.py:277
  (72 shorter events, 7.4 us)
Async XLA Ops:
  0.0 17.8 %collective-permute-start.7 = (s32[2,80]{1,0:T(2,128)}, s32[2,80]{1,0:T(2,128)S(1)}, u32[]{:S(2)}, u32[]{:S(2)}) collective-permute-start(s32[2,80]{1,0:T(2,128)} %param.7), channel_id=1, source_target_pairs={{0,16},{16,0},{1,17},{17,1},{2,18},{18,2},{3,19},{19,3},{4,20},{20... | collective-permute-start | bytes 1928 | tf_op jit(solution)/shard_map/ppermute | solution.py:445
  1.8 3.0 %copy-start.3 = (f32[2,64,1024]{2,1,0:T(8,128)S(1)}, f32[2,64,1024]{2,1,0:T(8,128)}, u32[]{:S(2)}) copy-start(f32[2,64,1024]{2,1,0:T(8,128)} %param.6) | copy-start | bytes 1572868
  1.8 16.6 %copy-start.4 = (s32[2,80]{1,0:T(2,128)S(1)}, s32[2,80]{1,0:T(2,128)}, u32[]{:S(2)}) copy-start(s32[2,80]{1,0:T(2,128)} %param.7) | copy-start | bytes 1924
  9.3 33.8 %copy-start.2 = (bf16[2,64,128]{2,1,0:T(8,128)(2,1)S(1)}, bf16[2,64,128]{2,1,0:T(8,128)(2,1)}, u32[]{:S(2)}) copy-start(bf16[2,64,128]{2,1,0:T(8,128)(2,1)} %get-tuple-element.31) | copy-start | bytes 98308
  11.6 13.7 %collective-permute-start.20 = (bf16[2,64,1152]{2,1,0:T(8,128)(2,1)}, bf16[2,64,1152]{2,1,0:T(8,128)(2,1)S(1)}, u32[]{:S(2)}, u32[]{:S(2)}) collective-permute-start(bf16[2,64,1152]{2,1,0:T(8,128)(2,1)} %pad_maximum_fusion.1), channel_id=1, source_target_pairs={{0,4},{1,5},{2,6},{3,7},{4,0},{5,1},{6,2},{7,3},{8,12},{9,13},{10,... | collective-permute-start | bytes 884744 | tf_op jit(solution)/shard_map/ppermute | solution.py:448
  13.1 20.4 %collective-permute-start.19 = (bf16[2,64,1152]{2,1,0:T(8,128)(2,1)}, bf16[2,64,1152]{2,1,0:T(8,128)(2,1)S(1)}, u32[]{:S(2)}, u32[]{:S(2)}) collective-permute-start(bf16[2,64,1152]{2,1,0:T(8,128)(2,1)} %pad_maximum_fusion.1), channel_id=1, source_target_pairs={{0,8},{1,9},{2,10},{3,11},{4,12},{5,13},{6,14},{7,15},{8,0},{9,1},... | collective-permute-start | bytes 884744 | tf_op jit(solution)/shard_map/ppermute | solution.py:448
  13.3 28.1 %collective-permute-start.18 = (bf16[2,64,1152]{2,1,0:T(8,128)(2,1)}, bf16[2,64,1152]{2,1,0:T(8,128)(2,1)S(1)}, u32[]{:S(2)}, u32[]{:S(2)}) collective-permute-start(bf16[2,64,1152]{2,1,0:T(8,128)(2,1)} %pad_maximum_fusion.1), channel_id=1, source_target_pairs={{0,12},{1,13},{2,14},{3,15},{4,8},{5,9},{6,10},{7,11},{8,4},{9,5},... | collective-permute-start | bytes 884744 | tf_op jit(solution)/shard_map/ppermute | solution.py:448
  15.1 28.3 %collective-permute-start = (bf16[512,512]{1,0:T(8,128)(2,1)S(1)}, bf16[512,512]{1,0:T(8,128)(2,1)}, u32[]{:S(2)}, u32[]{:S(2)}) collective-permute-start(bf16[512,512]{1,0:T(8,128)(2,1)S(1)} %get-tuple-element.24), channel_id=1, source_target_pairs={{0,1},{1,0},{2,3},{3,2},{4,5},{5,4},{6,7},{7,6},{8,9},{9,8},{10,11... | collective-permute-start | bytes 1572872 | tf_op jit(solution)/shard_map/ppermute | solution.py:448
  17.8 26.9 %collective-permute-start.2 = (bf16[512,512]{1,0:T(8,128)(2,1)S(1)}, bf16[512,512]{1,0:T(8,128)(2,1)}, u32[]{:S(2)}, u32[]{:S(2)}) collective-permute-start(bf16[512,512]{1,0:T(8,128)(2,1)S(1)} %get-tuple-element.25), channel_id=1, source_target_pairs={{0,2},{1,3},{2,0},{3,1},{4,6},{5,7},{6,4},{7,5},{8,10},{9,11},{10,... | collective-permute-start | bytes 1572872 | tf_op jit(solution)/shard_map/ppermute | solution.py:448
  44.4 7.6 %collective-permute-start.1 = (bf16[256,512]{1,0:T(8,128)(2,1)S(1)}, bf16[256,512]{1,0:T(8,128)(2,1)S(1)}, u32[]{:S(2)}, u32[]{:S(2)}) collective-permute-start(bf16[256,512]{1,0:T(8,128)(2,1)S(1)} %dynamic-slice_add_fusion.1), channel_id=1, source_target_pairs={{0,2},{1,3},{2,0},{3,1},{4,6},{5,7},{6,4},{7,5},{8,10},{9,11},{10,... | collective-permute-start | bytes 786440 | tf_op jit(solution)/shard_map/ppermute | solution.py:448
  45.8 7.4 %collective-permute-start.3 = (bf16[256,512]{1,0:T(8,128)(2,1)S(1)}, bf16[256,512]{1,0:T(8,128)(2,1)S(1)}, u32[]{:S(2)}, u32[]{:S(2)}) collective-permute-start(bf16[256,512]{1,0:T(8,128)(2,1)S(1)} %dynamic-slice_add_fusion), channel_id=1, source_target_pairs={{0,1},{1,0},{2,3},{3,2},{4,5},{5,4},{6,7},{7,6},{8,9},{9,8},{10,11... | collective-permute-start | bytes 786440 | tf_op jit(solution)/shard_map/ppermute | solution.py:448
  54.3 6.4 %collective-permute-start.4 = (bf16[2,64,512]{2,1,0:T(8,128)(2,1)S(1)}, bf16[2,64,512]{2,1,0:T(8,128)(2,1)S(1)}, u32[]{:S(2)}, u32[]{:S(2)}) collective-permute-start(bf16[2,64,512]{2,1,0:T(8,128)(2,1)S(1)} %get-tuple-element.53), channel_id=1, source_target_pairs={{0,4},{1,5},{2,6},{3,7},{4,0},{5,1},{6,2},{7,3},{8,12},{9,13},{10,... | collective-permute-start | bytes 393224 | tf_op jit(solution)/shard_map/ppermute | solution.py:448
  54.4 10.2 %collective-permute-start.5 = (bf16[2,64,512]{2,1,0:T(8,128)(2,1)S(1)}, bf16[2,64,512]{2,1,0:T(8,128)(2,1)S(1)}, u32[]{:S(2)}, u32[]{:S(2)}) collective-permute-start(bf16[2,64,512]{2,1,0:T(8,128)(2,1)S(1)} %get-tuple-element.54), channel_id=1, source_target_pairs={{0,8},{1,9},{2,10},{3,11},{4,12},{5,13},{6,14},{7,15},{8,0},{9,1},... | collective-permute-start | bytes 393224 | tf_op jit(solution)/shard_map/ppermute | solution.py:448
  56.5 12.7 %collective-permute-start.6 = (bf16[2,64,512]{2,1,0:T(8,128)(2,1)S(1)}, bf16[2,64,512]{2,1,0:T(8,128)(2,1)S(1)}, u32[]{:S(2)}, u32[]{:S(2)}) collective-permute-start(bf16[2,64,512]{2,1,0:T(8,128)(2,1)S(1)} %get-tuple-element.55), channel_id=1, source_target_pairs={{0,12},{1,13},{2,14},{3,15},{4,8},{5,9},{6,10},{7,11},{8,4},{9,5},... | collective-permute-start | bytes 393224 | tf_op jit(solution)/shard_map/ppermute | solution.py:448
  57.9 15.3 %collective-permute-start.25 = (bf16[64,3072]{1,0:T(8,128)(2,1)S(1)}, bf16[64,3072]{1,0:T(8,128)(2,1)S(1)}, u32[]{:S(2)}, u32[]{:S(2)}) collective-permute-start(bf16[64,3072]{1,0:T(8,128)(2,1)S(1)} %get-tuple-element.49.p0), channel_id=1, source_target_pairs={{0,2},{1,3},{2,0},{3,1},{4,6},{5,7},{6,4},{7,5},{8,10},{9,11},{10,... | collective-permute-start | bytes 1179656 | tf_op jit(solution)/shard_map/ppermute | solution.py:448
  69.2 9.8 %collective-permute-start.11 = (bf16[2,64,512]{2,1,0:T(8,128)(2,1)S(1)}, bf16[2,64,512]{2,1,0:T(8,128)(2,1)S(1)}, u32[]{:S(2)}, u32[]{:S(2)}) collective-permute-start(bf16[2,64,512]{2,1,0:T(8,128)(2,1)S(1)} %fusion.14), channel_id=1, source_target_pairs={{0,12},{1,13},{2,14},{3,15},{4,8},{5,9},{6,10},{7,11},{8,4},{9,5},... | collective-permute-start | bytes 393224 | tf_op jit(solution)/shard_map/ppermute | solution.py:448
  70.0 9.6 %collective-permute-start.10 = (bf16[2,64,512]{2,1,0:T(8,128)(2,1)S(1)}, bf16[2,64,512]{2,1,0:T(8,128)(2,1)S(1)}, u32[]{:S(2)}, u32[]{:S(2)}) collective-permute-start(bf16[2,64,512]{2,1,0:T(8,128)(2,1)S(1)} %fusion.14), channel_id=1, source_target_pairs={{0,8},{1,9},{2,10},{3,11},{4,12},{5,13},{6,14},{7,15},{8,0},{9,1},... | collective-permute-start | bytes 393224 | tf_op jit(solution)/shard_map/ppermute | solution.py:448
  71.4 9.7 %collective-permute-start.9 = (bf16[2,64,512]{2,1,0:T(8,128)(2,1)S(1)}, bf16[2,64,512]{2,1,0:T(8,128)(2,1)S(1)}, u32[]{:S(2)}, u32[]{:S(2)}) collective-permute-start(bf16[2,64,512]{2,1,0:T(8,128)(2,1)S(1)} %fusion.14), channel_id=1, source_target_pairs={{0,4},{1,5},{2,6},{3,7},{4,0},{5,1},{6,2},{7,3},{8,12},{9,13},{10,... | collective-permute-start | bytes 393224 | tf_op jit(solution)/shard_map/ppermute | solution.py:448
  72.8 12.0 %collective-permute-start.24 = (bf16[64,3072]{1,0:T(8,128)(2,1)S(1)}, bf16[64,3072]{1,0:T(8,128)(2,1)S(1)}, u32[]{:S(2)}, u32[]{:S(2)}) collective-permute-start(bf16[64,3072]{1,0:T(8,128)(2,1)S(1)} %get-tuple-element.49.p0), channel_id=1, source_target_pairs={{0,1},{1,0},{2,3},{3,2},{4,5},{5,4},{6,7},{7,6},{8,9},{9,8},{10,11... | collective-permute-start | bytes 1179656 | tf_op jit(solution)/shard_map/ppermute | solution.py:448
  73.2 21.5 %collective-permute-start.22 = (bf16[64,3072]{1,0:T(8,128)(2,1)S(1)}, bf16[64,3072]{1,0:T(8,128)(2,1)S(1)}, u32[]{:S(2)}, u32[]{:S(2)}) collective-permute-start(bf16[64,3072]{1,0:T(8,128)(2,1)S(1)} %get-tuple-element.50.p0), channel_id=1, source_target_pairs={{0,2},{1,3},{2,0},{3,1},{4,6},{5,7},{6,4},{7,5},{8,10},{9,11},{10,... | collective-permute-start | bytes 1179656 | tf_op jit(solution)/shard_map/ppermute | solution.py:448
  79.0 14.2 %collective-permute-start.21 = (bf16[64,3072]{1,0:T(8,128)(2,1)S(1)}, bf16[64,3072]{1,0:T(8,128)(2,1)S(1)}, u32[]{:S(2)}, u32[]{:S(2)}) collective-permute-start(bf16[64,3072]{1,0:T(8,128)(2,1)S(1)} %get-tuple-element.50.p0), channel_id=1, source_target_pairs={{0,1},{1,0},{2,3},{3,2},{4,5},{5,4},{6,7},{7,6},{8,9},{9,8},{10,11... | collective-permute-start | bytes 1179656 | tf_op jit(solution)/shard_map/ppermute | solution.py:448
  79.6 22.1 %collective-permute-start.26 = (bf16[64,3072]{1,0:T(8,128)(2,1)S(1)}, bf16[64,3072]{1,0:T(8,128)(2,1)S(1)}, u32[]{:S(2)}, u32[]{:S(2)}) collective-permute-start(bf16[64,3072]{1,0:T(8,128)(2,1)S(1)} %collective-permute-done.25.p2), channel_id=1, source_target_pairs={{0,1},{1,0},{2,3},{3,2},{4,5},{5,4},{6,7},{7,6},{8,9},{9,8},{10,11... | collective-permute-start | bytes 1179656 | tf_op jit(solution)/shard_map/ppermute | solution.py:448
  81.2 21.9 %collective-permute-start.16 = (bf16[4,64,512]{2,1,0:T(8,128)(2,1)S(1)}, bf16[4,64,512]{2,1,0:T(8,128)(2,1)S(1)}, u32[]{:S(2)}, u32[]{:S(2)}) collective-permute-start(bf16[4,64,512]{2,1,0:T(8,128)(2,1)S(1)} %get-tuple-element.51.refs_4_), channel_id=1, source_target_pairs={{0,2},{1,3},{2,0},{3,1},{4,6},{5,7},{6,4},{7,5},{8,10},{9,11},{10,... | collective-permute-start | bytes 786440 | tf_op jit(solution)/shard_map/ppermute | solution.py:448
  84.8 22.6 %collective-permute-start.12 = (bf16[4,64,512]{2,1,0:T(8,128)(2,1)S(1)}, bf16[4,64,512]{2,1,0:T(8,128)(2,1)}, u32[]{:S(2)}, u32[]{:S(2)}) collective-permute-start(bf16[4,64,512]{2,1,0:T(8,128)(2,1)S(1)} %get-tuple-element.52.refs_0_), channel_id=1, source_target_pairs={{0,1},{1,0},{2,3},{3,2},{4,5},{5,4},{6,7},{7,6},{8,9},{9,8},{10,11... | collective-permute-start | bytes 786440 | tf_op jit(solution)/shard_map/ppermute | solution.py:448
  93.2 19.4 %collective-permute-start.23 = (bf16[64,3072]{1,0:T(8,128)(2,1)S(1)}, bf16[64,3072]{1,0:T(8,128)(2,1)}, u32[]{:S(2)}, u32[]{:S(2)}) collective-permute-start(bf16[64,3072]{1,0:T(8,128)(2,1)S(1)} %collective-permute-done.21.p1), channel_id=1, source_target_pairs={{0,2},{1,3},{2,0},{3,1},{4,6},{5,7},{6,4},{7,5},{8,10},{9,11},{10,... | collective-permute-start | bytes 1179656 | tf_op jit(solution)/shard_map/ppermute | solution.py:448
  94.7 22.1 %collective-permute-start.15 = (bf16[4,64,512]{2,1,0:T(8,128)(2,1)S(1)}, bf16[4,64,512]{2,1,0:T(8,128)(2,1)}, u32[]{:S(2)}, u32[]{:S(2)}) collective-permute-start(bf16[4,64,512]{2,1,0:T(8,128)(2,1)S(1)} %get-tuple-element.51.refs_4_), channel_id=1, source_target_pairs={{0,1},{1,0},{2,3},{3,2},{4,5},{5,4},{6,7},{7,6},{8,9},{9,8},{10,11... | collective-permute-start | bytes 786440 | tf_op jit(solution)/shard_map/ppermute | solution.py:448
  101.6 15.2 %collective-permute-start.13 = (bf16[4,64,512]{2,1,0:T(8,128)(2,1)S(1)}, bf16[4,64,512]{2,1,0:T(8,128)(2,1)}, u32[]{:S(2)}, u32[]{:S(2)}) collective-permute-start(bf16[4,64,512]{2,1,0:T(8,128)(2,1)S(1)} %get-tuple-element.52.refs_0_), channel_id=1, source_target_pairs={{0,2},{1,3},{2,0},{3,1},{4,6},{5,7},{6,4},{7,5},{8,10},{9,11},{10,... | collective-permute-start | bytes 786440 | tf_op jit(solution)/shard_map/ppermute | solution.py:448
  103.1 13.7 %collective-permute-start.17 = (bf16[4,64,512]{2,1,0:T(8,128)(2,1)S(1)}, bf16[4,64,512]{2,1,0:T(8,128)(2,1)}, u32[]{:S(2)}, u32[]{:S(2)}) collective-permute-start(bf16[4,64,512]{2,1,0:T(8,128)(2,1)S(1)} %collective-permute-done.16.refs_6_), channel_id=1, source_target_pairs={{0,1},{1,0},{2,3},{3,2},{4,5},{5,4},{6,7},{7,6},{8,9},{9,8},{10,11... | collective-permute-start | bytes 786440 | tf_op jit(solution)/shard_map/ppermute | solution.py:448
  107.3 9.5 %collective-permute-start.14 = (bf16[4,64,512]{2,1,0:T(8,128)(2,1)}, bf16[4,64,512]{2,1,0:T(8,128)(2,1)}, u32[]{:S(2)}, u32[]{:S(2)}) collective-permute-start(bf16[4,64,512]{2,1,0:T(8,128)(2,1)} %collective-permute-done.12.refs_1_), channel_id=1, source_target_pairs={{0,2},{1,3},{2,0},{3,1},{4,6},{5,7},{6,4},{7,5},{8,10},{9,11},{10,... | collective-permute-start | bytes 786440 | tf_op jit(solution)/shard_map/ppermute | solution.py:448
  116.9 0.6 copy-start.1
  123.9 8.6 %collective-permute-start.27 = (f32[512,512]{1,0:T(8,128)S(1)}, f32[512,512]{1,0:T(8,128)S(1)}, u32[]{:S(2)}, u32[]{:S(2)}) collective-permute-start(f32[512,512]{1,0:T(8,128)S(1)} %get-tuple-element.38.block_ref), channel_id=1, source_target_pairs={{0,16},{16,0},{1,17},{17,1},{2,18},{18,2},{3,19},{19,3},{4,20},{20... | collective-permute-start | bytes 3145736 | tf_op jit(solution)/shard_map/ppermute | solution.py:445
  129.1 27.2 %collective-permute-start.8 = (bf16[2,1024,1280]{2,1,0:T(8,128)(2,1)}, bf16[2,1024,1280]{2,1,0:T(8,128)(2,1)S(1)}, u32[]{:S(2)}, u32[]{:S(2)}) collective-permute-start(bf16[2,1024,1280]{2,1,0:T(8,128)(2,1)} %constant_dynamic-slice_fusion.1), channel_id=1, source_target_pairs={{0,16},{16,0},{1,17},{17,1},{2,18},{18,2},{3,19},{19,3},{4,20},{20... | collective-permute-start | bytes 15728648 | tf_op jit(solution)/shard_map/ppermute | solution.py:445
  132.5 23.8 %copy-start = (s32[22]{0:T(128)S(1)}, s32[22]{0:T(128)}, u32[]{:S(2)}) copy-start(s32[22]{0:T(128)} %pad_add_fusion.1.info) | copy-start | bytes 268
  132.5 23.8 %collective-permute-start.28 = (bf16[2,1024,1024]{2,1,0:T(8,128)(2,1)S(1)}, bf16[2,1024,1024]{2,1,0:T(8,128)(2,1)S(1)}, u32[]{:S(2)}, u32[]{:S(2)}) collective-permute-start(bf16[2,1024,1024]{2,1,0:T(8,128)(2,1)S(1)} %back_solve.1.qown), channel_id=1, source_target_pairs={{0,16},{16,0},{1,17},{17,1},{2,18},{18,2},{3,19},{19,3},{4,20},{20... | collective-permute-start | bytes 12582920 | tf_op jit(solution)/shard_map/ppermute | solution.py:445

commit v2 on v1

--- a/solution.py
+++ b/solution.py
@@ -449,8 +449,9 @@
 
     def spread(value, first):
         second = 3 - first
-        direct = hop(value, first)
-        return {0: value, first: direct, second: hop(value, second), 3: hop(direct, second)}
+        direct, other = hop(value, first), hop(value, second)
+        corner = hop(direct, second)
+        return {0: value, first: direct, second: other, 3: corner}
 
     offset = start - me * columns
     inside = (offset >= 0) & (offset < columns)
@@ -483,7 +484,8 @@
     seeds = jnp.stack(seeds, axis=1)
     chunk = lax.dynamic_index_in_dim(seeds, plane, 0, False)
     for k in range(1, planes):
-        chunk += hop(lax.dynamic_index_in_dim(seeds, plane ^ k, 0, False), 4 * k)
+        gone = hop(lax.dynamic_index_in_dim(seeds, plane ^ k, 0, False), 4 * k)
+        chunk += gone
 
     lower = factor_rows(cov_factor, me)
     stack = [lower]
@@ -530,7 +532,8 @@
         )
         factors += call(seats, *[pieces[k] for k in range(4)])
 
-    stack = jnp.stack([chunk] + [hop(chunk, 4 * k) for k in range(1, planes)], axis=1)
+    stack = [chunk] + [hop(chunk, 4 * k) for k in range(1, planes)]
+    stack = jnp.stack(stack, axis=1)
     pieces = []
     for arc in range(arcs):
         found = spread(stack[arc], 1 + arc % 2)

time: 174 us -> 174 us (level)
  no operation moved by 1% of the time
where the time goes in v2:
time: 174 us; the launch traced here: 173 us
  waiting for transfers between devices  62.1 us (36%)
  Pallas kernels  61.4 us (35%)
  starting transfers between devices  26 us (15%)
  other arithmetic  13.2 us (8%)
  local copies, waits for them, and re-layouts  9.33 us (5%)
    ppermute x25, waiting for transfers between devices, hop(): return lax.ppermute(value, 'par', [(p, p ^ bits) for p in range(chips)])  62.1 us
    ppermute x25, starting transfers between devices, hop(): return lax.ppermute(value, 'par', [(p, p ^ bits) for p in range(chips)])  25.4 us
    pallas_call x1, Pallas kernels, chol_inverse(): pl.pallas_call(chol_kernel, out_shape=jax.ShapeDtypeStruct((size, size),...  23.7 us
    pallas_call x1, Pallas kernels, normals_call(): pl.pallas_call(normals_kernel, out_shape=jax.ShapeDtypeStruct((width, sha...  16.7 us
    pallas_call x2, Pallas kernels, paired(): factors += call(seats, *[pieces[k] for k in range(4)])  7.96 us
    pallas_call x1, Pallas kernels, panel_call(): pl.pallas_call(functools.partial(panel_kernel, arcs), out_shape=(jax.Shap...  6.42 us
    dynamic_slice x1, local copies, waits for them, and re-layouts, paired(): far = lax.dynamic_slice_in_dim(design, (1 - core) * share, share, 2)  5.15 us
    pallas_call x1, Pallas kernels, invert_diag(): pl.pallas_call(diag_kernel, out_shape=(out, out), in_specs=[pl.BlockSpec(...  3.78 us
  transfers between devices with their start and end apart: 29, of which 13 were waited for; matrix products, arithmetic and copies ran while one was open for 12% of the time, Pallas kernels for 22%

profile of v2, /device:TPU:22, one launch (start us, length us, event | category | flops | bytes accessed | tf_op | source)
XLA Modules:
  0.0 173.2 jit_solution(15633153089229194874)
XLA Ops:
  0.7 0.9 compare_reduce_fusion.1
  1.8 3.0 %bitcast_select_fusion = (bf16[512,512]{1,0:T(8,128)(2,1)S(1)}, bf16[512,512]{1,0:T(8,128)(2,1)S(1)}, bf16[512,512]{1,0:T(8,128)(2,1)S(1)}, bf16[512,512]{1,0:T(8,128)(2,1)S(1)}) fusion(bf16[2,1024,2560]{2,1,0:T(8,128)(2,1)} %own.1, s32[]{:T(128)S(6)} %select_n.177, s32[]{:T(128)S(6)} %min.4, pred[512]{0:T(512)(128)(4,1)S(1)} %broadcast_in_dim.55, ...), kind=kLoop, calls=%fused_computation.14 | loop fusion | flops 1048576 | bytes 4195348 | tf_op jit(solution)/shard_map/jit(_where)/select_n | solution.py:464
  4.9 0.6 constant_dynamic-slice_fusion.strip_ref
  5.5 3.8 %invert_diag.1 = (bf16[2,64,128]{2,1,0:T(8,128)(2,1)}, bf16[2,64,128]{2,1,0:T(8,128)(2,1)}) custom-call(s32[1]{0:T(128)} %bitcast.26.off_ref, f32[2,64,128]{2,1,0:T(8,128)} %constant_dynamic-slice_fusion.strip_ref), custom_call_target="tpu_custom_call" | custom-call | tf_op jit(solution)/shard_map/invert_diag/pallas_call | solution.py:70
  9.3 0.8 constant_dynamic-update-slice_fusion
  10.1 1.5 pad_maximum_fusion.1
  11.6 1.6 collective-permute-start.20
  13.3 1.7 %collective-permute-start.18 = (bf16[2,64,1152]{2,1,0:T(8,128)(2,1)}, bf16[2,64,1152]{2,1,0:T(8,128)(2,1)S(1)}, u32[]{:S(2)}, u32[]{:S(2)}) collective-permute-start(bf16[2,64,1152]{2,1,0:T(8,128)(2,1)} %pad_maximum_fusion.1), channel_id=1, source_target_pairs={{0,12},{1,13},{2,14},{3,15},{4,8},{5,9},{6,10},{7,11},{8,4},{9,5},... | collective-permute-start | bytes 884744 | tf_op jit(solution)/shard_map/ppermute | solution.py:448
  16.3 0.8 dynamic_slice.78
  17.0 0.8 dynamic_slice.77
  18.8 6.5 %collective-permute-done.20 = bf16[2,64,1152]{2,1,0:T(8,128)(2,1)S(1)} collective-permute-done((bf16[2,64,1152]{2,1,0:T(8,128)(2,1)}, bf16[2,64,1152]{2,1,0:T(8,128)(2,1)S(1)}, u32[]{:S(2)}, u32[]{:S(2)}) %collective-permute-start.20) | collective-permute-done | bytes 294944 | tf_op jit(solution)/shard_map/ppermute | solution.py:448
  25.3 8.3 %collective-permute-done.19 = bf16[2,64,1152]{2,1,0:T(8,128)(2,1)S(1)} collective-permute-done((bf16[2,64,1152]{2,1,0:T(8,128)(2,1)}, bf16[2,64,1152]{2,1,0:T(8,128)(2,1)S(1)}, u32[]{:S(2)}, u32[]{:S(2)}) %collective-permute-start.19) | collective-permute-done | bytes 294944 | tf_op jit(solution)/shard_map/ppermute | solution.py:448
  33.6 7.8 %collective-permute-done.18 = bf16[2,64,1152]{2,1,0:T(8,128)(2,1)S(1)} collective-permute-done((bf16[2,64,1152]{2,1,0:T(8,128)(2,1)}, bf16[2,64,1152]{2,1,0:T(8,128)(2,1)S(1)}, u32[]{:S(2)}, u32[]{:S(2)}) %collective-permute-start.18) | collective-permute-done | bytes 294944 | tf_op jit(solution)/shard_map/ppermute | solution.py:448
  41.4 0.8 fusion.7
  42.2 0.9 fusion.3
  43.4 1.0 dynamic-slice_add_fusion.1
  44.8 1.0 dynamic-slice_add_fusion
  45.8 0.6 collective-permute-start.3
  46.5 5.5 %collective-permute-done.1 = bf16[256,512]{1,0:T(8,128)(2,1)S(1)} collective-permute-done((bf16[256,512]{1,0:T(8,128)(2,1)S(1)}, bf16[256,512]{1,0:T(8,128)(2,1)S(1)}, u32[]{:S(2)}, u32[]{:S(2)}) %collective-permute-start.1) | collective-permute-done | bytes 262176 | tf_op jit(solution)/shard_map/ppermute | solution.py:448
  52.0 1.1 add_add_fusion.1
  53.2 1.1 add_add_fusion
  54.4 2.2 %collective-permute-start.5 = (bf16[2,64,512]{2,1,0:T(8,128)(2,1)S(1)}, bf16[2,64,512]{2,1,0:T(8,128)(2,1)S(1)}, u32[]{:S(2)}, u32[]{:S(2)}) collective-permute-start(bf16[2,64,512]{2,1,0:T(8,128)(2,1)S(1)} %get-tuple-element.54), channel_id=1, source_target_pairs={{0,8},{1,9},{2,10},{3,11},{4,12},{5,13},{6,14},{7,15},{8,0},{9,1},... | collective-permute-start | bytes 393224 | tf_op jit(solution)/shard_map/ppermute | solution.py:448
  56.5 1.3 collective-permute-start.6
  57.9 1.8 %collective-permute-start.25 = (bf16[64,3072]{1,0:T(8,128)(2,1)S(1)}, bf16[64,3072]{1,0:T(8,128)(2,1)S(1)}, u32[]{:S(2)}, u32[]{:S(2)}) collective-permute-start(bf16[64,3072]{1,0:T(8,128)(2,1)S(1)} %get-tuple-element.49.p0), channel_id=1, source_target_pairs={{0,2},{1,3},{2,0},{3,1},{4,6},{5,7},{6,4},{7,5},{8,10},{9,11},{10,... | collective-permute-start | bytes 1179656 | tf_op jit(solution)/shard_map/ppermute | solution.py:448
  60.7 3.9 %collective-permute-done.5 = bf16[2,64,512]{2,1,0:T(8,128)(2,1)S(1)} collective-permute-done((bf16[2,64,512]{2,1,0:T(8,128)(2,1)S(1)}, bf16[2,64,512]{2,1,0:T(8,128)(2,1)S(1)}, u32[]{:S(2)}, u32[]{:S(2)}) %collective-permute-start.5) | collective-permute-done | bytes 131104 | tf_op jit(solution)/shard_map/ppermute | solution.py:448
  64.6 4.6 %collective-permute-done.6 = bf16[2,64,512]{2,1,0:T(8,128)(2,1)S(1)} collective-permute-done((bf16[2,64,512]{2,1,0:T(8,128)(2,1)S(1)}, bf16[2,64,512]{2,1,0:T(8,128)(2,1)S(1)}, u32[]{:S(2)}, u32[]{:S(2)}) %collective-permute-start.6) | collective-permute-done | bytes 131104 | tf_op jit(solution)/shard_map/ppermute | solution.py:448
  69.2 0.8 collective-permute-start.11
  70.0 1.4 collective-permute-start.10
  71.4 1.4 collective-permute-start.9
  73.2 1.5 collective-permute-start.22
  74.6 4.4 %collective-permute-done.11 = bf16[2,64,512]{2,1,0:T(8,128)(2,1)S(1)} collective-permute-done((bf16[2,64,512]{2,1,0:T(8,128)(2,1)S(1)}, bf16[2,64,512]{2,1,0:T(8,128)(2,1)S(1)}, u32[]{:S(2)}, u32[]{:S(2)}) %collective-permute-start.11) | collective-permute-done | bytes 131104 | tf_op jit(solution)/shard_map/ppermute | solution.py:448
  79.6 1.5 collective-permute-start.26
  81.2 1.7 collective-permute-start.16
  82.9 1.9 %collective-permute-done.24.p1 = bf16[64,3072]{1,0:T(8,128)(2,1)S(1)} collective-permute-done((bf16[64,3072]{1,0:T(8,128)(2,1)S(1)}, bf16[64,3072]{1,0:T(8,128)(2,1)S(1)}, u32[]{:S(2)}, u32[]{:S(2)}) %collective-permute-start.24) | collective-permute-done | bytes 393248 | tf_op jit(solution)/shard_map/ppermute | solution.py:448
  85.1 8.1 %collective-permute-done.21.p1 = bf16[64,3072]{1,0:T(8,128)(2,1)S(1)} collective-permute-done((bf16[64,3072]{1,0:T(8,128)(2,1)S(1)}, bf16[64,3072]{1,0:T(8,128)(2,1)S(1)}, u32[]{:S(2)}, u32[]{:S(2)}) %collective-permute-start.21) | collective-permute-done | bytes 393248 | tf_op jit(solution)/shard_map/ppermute | solution.py:448
  93.2 1.5 collective-permute-start.23
  95.0 6.6 %collective-permute-done.26.p3 = bf16[64,3072]{1,0:T(8,128)(2,1)S(1)} collective-permute-done((bf16[64,3072]{1,0:T(8,128)(2,1)S(1)}, bf16[64,3072]{1,0:T(8,128)(2,1)S(1)}, u32[]{:S(2)}, u32[]{:S(2)}) %collective-permute-start.26) | collective-permute-done | bytes 393248 | tf_op jit(solution)/shard_map/ppermute | solution.py:448
  101.6 1.5 collective-permute-start.13
  103.5 3.9 %collective-permute-done.12.refs_1_ = bf16[4,64,512]{2,1,0:T(8,128)(2,1)} collective-permute-done((bf16[4,64,512]{2,1,0:T(8,128)(2,1)S(1)}, bf16[4,64,512]{2,1,0:T(8,128)(2,1)}, u32[]{:S(2)}, u32[]{:S(2)}) %collective-permute-start.12) | collective-permute-done | bytes 262176 | tf_op jit(solution)/shard_map/ppermute | solution.py:448
  107.3 1.5 collective-permute-start.14
  108.8 3.7 %invert_factor.3 = (bf16[1024,1024]{1,0:T(8,128)(2,1)S(1)}, bf16[1024,1024]{1,0:T(8,128)(2,1)S(1)}) custom-call(s32[4]{0:T(128)S(1)} %iota_xor_fusion.place_ref, bf16[64,3072]{1,0:T(8,128)(2,1)S(1)} %get-tuple-element.49.p0, bf16[64,3072]{1,0:T(8,128)(2,1)S(1)} %collective-permute-done.24.p1, bf16[64,3072]{1,0:T(8,128)(2,1)S(1)} %collective-permute-done.25.p2, ...), custom_call_target="tpu_custom_call" | custom-call | tf_op jit(solution)/shard_map/invert_factor/pallas_call | solution.py:533
  112.6 4.2 %invert_factor.2 = (bf16[1024,1024]{1,0:T(8,128)(2,1)S(1)}, bf16[1024,1024]{1,0:T(8,128)(2,1)S(1)}) custom-call(s32[4]{0:T(128)S(1)} %iota_xor_fusion.place_ref, bf16[64,3072]{1,0:T(8,128)(2,1)S(1)} %get-tuple-element.50.p0, bf16[64,3072]{1,0:T(8,128)(2,1)S(1)} %collective-permute-done.21.p1, bf16[64,3072]{1,0:T(8,128)(2,1)S(1)} %collective-permute-done.22.p2, ...), custom_call_target="tpu_custom_call" | custom-call | tf_op jit(solution)/shard_map/invert_factor/pallas_call | solution.py:533
  116.9 0.6 copy-done.1
  117.5 6.4 %panel_block.1 = (bf16[2,512,1024]{2,1,0:T(8,128)(2,1)S(1)}, f32[512,512]{1,0:T(8,128)S(1)}) custom-call(s32[32]{0:T(128)S(1)} %copy-done.1, bf16[4,64,512]{2,1,0:T(8,128)(2,1)S(1)} %get-tuple-element.52.refs_0_, bf16[4,64,512]{2,1,0:T(8,128)(2,1)} %collective-permute-done.12.refs_1_, bf16[4,64,512]{2,1,0:T(8,128)(2,1)} %collective-permute-done.13.refs_2_, ...), custom_call_target="tpu_custom_call" | custom-call | tf_op jit(solution)/shard_map/panel_block/pallas_call | solution.py:198
  124.0 5.1 %constant_dynamic-slice_fusion.1 = bf16[2,1024,1280]{2,1,0:T(8,128)(2,1)} fusion(bf16[2,1024,2560]{2,1,0:T(8,128)(2,1)} %own.1, s32[]{:T(128)S(6)} %select_n.188), kind=kLoop, calls=%fused_computation.56 | loop fusion | bytes 10485764 | tf_op jit(solution)/shard_map/dynamic_slice | solution.py:520
  129.6 2.9 %back_solve.1.qown = bf16[2,1024,1024]{2,1,0:T(8,128)(2,1)S(1)} custom-call(bf16[2,512,1024]{2,1,0:T(8,128)(2,1)S(1)} %get-tuple-element.37.pt, bf16[1024,1024]{1,0:T(8,128)(2,1)S(1)} %get-tuple-element.33.refs_8_.refs_0_, bf16[1024,1024]{1,0:T(8,128)(2,1)S(1)} %get-tuple-element.34.refs_9_.refs_1_, ...), custom_call_target="tpu_custom_call" | custom-call | tf_op jit(solution)/shard_map/back_solve/pallas_call | solution.py:214
  132.6 23.7 %chol_inverse.1.inv_ref = f32[512,512]{1,0:T(8,128)S(1)} custom-call(f32[512,512]{1,0:T(8,128)S(1)} %get-tuple-element.38.block_ref, f32[512,512]{1,0:T(8,128)S(1)} %collective-permute-done.27.other_ref, f32[1,512]{1,0:T(1,128)S(1)} %bitcast.53), custom_call_target="tpu_custom_call" | custom-call | tf_op jit(solution)/shard_map/chol_inverse/pallas_call | solution.py:368
  156.3 16.7 %normals.1 = f32[512,1280]{1,0:T(8,128)} custom-call(s32[22]{0:T(128)S(1)} %copy-done, bf16[2,1024,2560]{2,1,0:T(8,128)(2,1)} %own.1, bf16[2,1024,1280]{2,1,0:T(8,128)(2,1)S(1)} %collective-permute-done.8.far, bf16[2,1024,1024]{2,1,0:T(8,128)(2,1)S(1)} %back_solve.1.qown, bf16[2,1024,1024]{2,1,0:T(8,128)(2,1)S(1)} %collective-permute-done.28.qfar, ...), custom_call_target="tpu_custom_call" | custom-call | tf_op jit(solution)/shard_map/normals/pallas_call | solution.py:277
  (72 shorter events, 7.4 us)
Async XLA Ops:
  0.0 17.8 %collective-permute-start.7 = (s32[2,80]{1,0:T(2,128)}, s32[2,80]{1,0:T(2,128)S(1)}, u32[]{:S(2)}, u32[]{:S(2)}) collective-permute-start(s32[2,80]{1,0:T(2,128)} %param.7), channel_id=1, source_target_pairs={{0,16},{16,0},{1,17},{17,1},{2,18},{18,2},{3,19},{19,3},{4,20},{20... | collective-permute-start | bytes 1928 | tf_op jit(solution)/shard_map/ppermute | solution.py:445
  1.8 3.0 %copy-start.3 = (f32[2,64,1024]{2,1,0:T(8,128)S(1)}, f32[2,64,1024]{2,1,0:T(8,128)}, u32[]{:S(2)}) copy-start(f32[2,64,1024]{2,1,0:T(8,128)} %param.6) | copy-start | bytes 1572868
  1.8 16.6 %copy-start.4 = (s32[2,80]{1,0:T(2,128)S(1)}, s32[2,80]{1,0:T(2,128)}, u32[]{:S(2)}) copy-start(s32[2,80]{1,0:T(2,128)} %param.7) | copy-start | bytes 1924
  9.3 33.8 %copy-start.2 = (bf16[2,64,128]{2,1,0:T(8,128)(2,1)S(1)}, bf16[2,64,128]{2,1,0:T(8,128)(2,1)}, u32[]{:S(2)}) copy-start(bf16[2,64,128]{2,1,0:T(8,128)(2,1)} %get-tuple-element.31) | copy-start | bytes 98308
  11.6 13.7 %collective-permute-start.20 = (bf16[2,64,1152]{2,1,0:T(8,128)(2,1)}, bf16[2,64,1152]{2,1,0:T(8,128)(2,1)S(1)}, u32[]{:S(2)}, u32[]{:S(2)}) collective-permute-start(bf16[2,64,1152]{2,1,0:T(8,128)(2,1)} %pad_maximum_fusion.1), channel_id=1, source_target_pairs={{0,4},{1,5},{2,6},{3,7},{4,0},{5,1},{6,2},{7,3},{8,12},{9,13},{10,... | collective-permute-start | bytes 884744 | tf_op jit(solution)/shard_map/ppermute | solution.py:448
  13.1 20.4 %collective-permute-start.19 = (bf16[2,64,1152]{2,1,0:T(8,128)(2,1)}, bf16[2,64,1152]{2,1,0:T(8,128)(2,1)S(1)}, u32[]{:S(2)}, u32[]{:S(2)}) collective-permute-start(bf16[2,64,1152]{2,1,0:T(8,128)(2,1)} %pad_maximum_fusion.1), channel_id=1, source_target_pairs={{0,8},{1,9},{2,10},{3,11},{4,12},{5,13},{6,14},{7,15},{8,0},{9,1},... | collective-permute-start | bytes 884744 | tf_op jit(solution)/shard_map/ppermute | solution.py:448
  13.3 28.1 %collective-permute-start.18 = (bf16[2,64,1152]{2,1,0:T(8,128)(2,1)}, bf16[2,64,1152]{2,1,0:T(8,128)(2,1)S(1)}, u32[]{:S(2)}, u32[]{:S(2)}) collective-permute-start(bf16[2,64,1152]{2,1,0:T(8,128)(2,1)} %pad_maximum_fusion.1), channel_id=1, source_target_pairs={{0,12},{1,13},{2,14},{3,15},{4,8},{5,9},{6,10},{7,11},{8,4},{9,5},... | collective-permute-start | bytes 884744 | tf_op jit(solution)/shard_map/ppermute | solution.py:448
  15.1 28.3 %collective-permute-start = (bf16[512,512]{1,0:T(8,128)(2,1)S(1)}, bf16[512,512]{1,0:T(8,128)(2,1)}, u32[]{:S(2)}, u32[]{:S(2)}) collective-permute-start(bf16[512,512]{1,0:T(8,128)(2,1)S(1)} %get-tuple-element.24), channel_id=1, source_target_pairs={{0,1},{1,0},{2,3},{3,2},{4,5},{5,4},{6,7},{7,6},{8,9},{9,8},{10,11... | collective-permute-start | bytes 1572872 | tf_op jit(solution)/shard_map/ppermute | solution.py:448
  17.8 26.9 %collective-permute-start.2 = (bf16[512,512]{1,0:T(8,128)(2,1)S(1)}, bf16[512,512]{1,0:T(8,128)(2,1)}, u32[]{:S(2)}, u32[]{:S(2)}) collective-permute-start(bf16[512,512]{1,0:T(8,128)(2,1)S(1)} %get-tuple-element.25), channel_id=1, source_target_pairs={{0,2},{1,3},{2,0},{3,1},{4,6},{5,7},{6,4},{7,5},{8,10},{9,11},{10,... | collective-permute-start | bytes 1572872 | tf_op jit(solution)/shard_map/ppermute | solution.py:448
  44.4 7.6 %collective-permute-start.1 = (bf16[256,512]{1,0:T(8,128)(2,1)S(1)}, bf16[256,512]{1,0:T(8,128)(2,1)S(1)}, u32[]{:S(2)}, u32[]{:S(2)}) collective-permute-start(bf16[256,512]{1,0:T(8,128)(2,1)S(1)} %dynamic-slice_add_fusion.1), channel_id=1, source_target_pairs={{0,2},{1,3},{2,0},{3,1},{4,6},{5,7},{6,4},{7,5},{8,10},{9,11},{10,... | collective-permute-start | bytes 786440 | tf_op jit(solution)/shard_map/ppermute | solution.py:448
  45.8 7.4 %collective-permute-start.3 = (bf16[256,512]{1,0:T(8,128)(2,1)S(1)}, bf16[256,512]{1,0:T(8,128)(2,1)S(1)}, u32[]{:S(2)}, u32[]{:S(2)}) collective-permute-start(bf16[256,512]{1,0:T(8,128)(2,1)S(1)} %dynamic-slice_add_fusion), channel_id=1, source_target_pairs={{0,1},{1,0},{2,3},{3,2},{4,5},{5,4},{6,7},{7,6},{8,9},{9,8},{10,11... | collective-permute-start | bytes 786440 | tf_op jit(solution)/shard_map/ppermute | solution.py:448
  54.3 6.4 %collective-permute-start.4 = (bf16[2,64,512]{2,1,0:T(8,128)(2,1)S(1)}, bf16[2,64,512]{2,1,0:T(8,128)(2,1)S(1)}, u32[]{:S(2)}, u32[]{:S(2)}) collective-permute-start(bf16[2,64,512]{2,1,0:T(8,128)(2,1)S(1)} %get-tuple-element.53), channel_id=1, source_target_pairs={{0,4},{1,5},{2,6},{3,7},{4,0},{5,1},{6,2},{7,3},{8,12},{9,13},{10,... | collective-permute-start | bytes 393224 | tf_op jit(solution)/shard_map/ppermute | solution.py:448
  54.4 10.2 %collective-permute-start.5 = (bf16[2,64,512]{2,1,0:T(8,128)(2,1)S(1)}, bf16[2,64,512]{2,1,0:T(8,128)(2,1)S(1)}, u32[]{:S(2)}, u32[]{:S(2)}) collective-permute-start(bf16[2,64,512]{2,1,0:T(8,128)(2,1)S(1)} %get-tuple-element.54), channel_id=1, source_target_pairs={{0,8},{1,9},{2,10},{3,11},{4,12},{5,13},{6,14},{7,15},{8,0},{9,1},... | collective-permute-start | bytes 393224 | tf_op jit(solution)/shard_map/ppermute | solution.py:448
  56.5 12.7 %collective-permute-start.6 = (bf16[2,64,512]{2,1,0:T(8,128)(2,1)S(1)}, bf16[2,64,512]{2,1,0:T(8,128)(2,1)S(1)}, u32[]{:S(2)}, u32[]{:S(2)}) collective-permute-start(bf16[2,64,512]{2,1,0:T(8,128)(2,1)S(1)} %get-tuple-element.55), channel_id=1, source_target_pairs={{0,12},{1,13},{2,14},{3,15},{4,8},{5,9},{6,10},{7,11},{8,4},{9,5},... | collective-permute-start | bytes 393224 | tf_op jit(solution)/shard_map/ppermute | solution.py:448
  57.9 15.3 %collective-permute-start.25 = (bf16[64,3072]{1,0:T(8,128)(2,1)S(1)}, bf16[64,3072]{1,0:T(8,128)(2,1)S(1)}, u32[]{:S(2)}, u32[]{:S(2)}) collective-permute-start(bf16[64,3072]{1,0:T(8,128)(2,1)S(1)} %get-tuple-element.49.p0), channel_id=1, source_target_pairs={{0,2},{1,3},{2,0},{3,1},{4,6},{5,7},{6,4},{7,5},{8,10},{9,11},{10,... | collective-permute-start | bytes 1179656 | tf_op jit(solution)/shard_map/ppermute | solution.py:448
  69.2 9.8 %collective-permute-start.11 = (bf16[2,64,512]{2,1,0:T(8,128)(2,1)S(1)}, bf16[2,64,512]{2,1,0:T(8,128)(2,1)S(1)}, u32[]{:S(2)}, u32[]{:S(2)}) collective-permute-start(bf16[2,64,512]{2,1,0:T(8,128)(2,1)S(1)} %fusion.14), channel_id=1, source_target_pairs={{0,12},{1,13},{2,14},{3,15},{4,8},{5,9},{6,10},{7,11},{8,4},{9,5},... | collective-permute-start | bytes 393224 | tf_op jit(solution)/shard_map/ppermute | solution.py:448
  70.0 9.6 %collective-permute-start.10 = (bf16[2,64,512]{2,1,0:T(8,128)(2,1)S(1)}, bf16[2,64,512]{2,1,0:T(8,128)(2,1)S(1)}, u32[]{:S(2)}, u32[]{:S(2)}) collective-permute-start(bf16[2,64,512]{2,1,0:T(8,128)(2,1)S(1)} %fusion.14), channel_id=1, source_target_pairs={{0,8},{1,9},{2,10},{3,11},{4,12},{5,13},{6,14},{7,15},{8,0},{9,1},... | collective-permute-start | bytes 393224 | tf_op jit(solution)/shard_map/ppermute | solution.py:448
  71.4 9.7 %collective-permute-start.9 = (bf16[2,64,512]{2,1,0:T(8,128)(2,1)S(1)}, bf16[2,64,512]{2,1,0:T(8,128)(2,1)S(1)}, u32[]{:S(2)}, u32[]{:S(2)}) collective-permute-start(bf16[2,64,512]{2,1,0:T(8,128)(2,1)S(1)} %fusion.14), channel_id=1, source_target_pairs={{0,4},{1,5},{2,6},{3,7},{4,0},{5,1},{6,2},{7,3},{8,12},{9,13},{10,... | collective-permute-start | bytes 393224 | tf_op jit(solution)/shard_map/ppermute | solution.py:448
  72.8 12.0 %collective-permute-start.24 = (bf16[64,3072]{1,0:T(8,128)(2,1)S(1)}, bf16[64,3072]{1,0:T(8,128)(2,1)S(1)}, u32[]{:S(2)}, u32[]{:S(2)}) collective-permute-start(bf16[64,3072]{1,0:T(8,128)(2,1)S(1)} %get-tuple-element.49.p0), channel_id=1, source_target_pairs={{0,1},{1,0},{2,3},{3,2},{4,5},{5,4},{6,7},{7,6},{8,9},{9,8},{10,11... | collective-permute-start | bytes 1179656 | tf_op jit(solution)/shard_map/ppermute | solution.py:448
  73.2 21.5 %collective-permute-start.22 = (bf16[64,3072]{1,0:T(8,128)(2,1)S(1)}, bf16[64,3072]{1,0:T(8,128)(2,1)S(1)}, u32[]{:S(2)}, u32[]{:S(2)}) collective-permute-start(bf16[64,3072]{1,0:T(8,128)(2,1)S(1)} %get-tuple-element.50.p0), channel_id=1, source_target_pairs={{0,2},{1,3},{2,0},{3,1},{4,6},{5,7},{6,4},{7,5},{8,10},{9,11},{10,... | collective-permute-start | bytes 1179656 | tf_op jit(solution)/shard_map/ppermute | solution.py:448
  79.0 14.2 %collective-permute-start.21 = (bf16[64,3072]{1,0:T(8,128)(2,1)S(1)}, bf16[64,3072]{1,0:T(8,128)(2,1)S(1)}, u32[]{:S(2)}, u32[]{:S(2)}) collective-permute-start(bf16[64,3072]{1,0:T(8,128)(2,1)S(1)} %get-tuple-element.50.p0), channel_id=1, source_target_pairs={{0,1},{1,0},{2,3},{3,2},{4,5},{5,4},{6,7},{7,6},{8,9},{9,8},{10,11... | collective-permute-start | bytes 1179656 | tf_op jit(solution)/shard_map/ppermute | solution.py:448
  79.6 22.1 %collective-permute-start.26 = (bf16[64,3072]{1,0:T(8,128)(2,1)S(1)}, bf16[64,3072]{1,0:T(8,128)(2,1)S(1)}, u32[]{:S(2)}, u32[]{:S(2)}) collective-permute-start(bf16[64,3072]{1,0:T(8,128)(2,1)S(1)} %collective-permute-done.25.p2), channel_id=1, source_target_pairs={{0,1},{1,0},{2,3},{3,2},{4,5},{5,4},{6,7},{7,6},{8,9},{9,8},{10,11... | collective-permute-start | bytes 1179656 | tf_op jit(solution)/shard_map/ppermute | solution.py:448
  81.2 21.9 %collective-permute-start.16 = (bf16[4,64,512]{2,1,0:T(8,128)(2,1)S(1)}, bf16[4,64,512]{2,1,0:T(8,128)(2,1)S(1)}, u32[]{:S(2)}, u32[]{:S(2)}) collective-permute-start(bf16[4,64,512]{2,1,0:T(8,128)(2,1)S(1)} %get-tuple-element.51.refs_4_), channel_id=1, source_target_pairs={{0,2},{1,3},{2,0},{3,1},{4,6},{5,7},{6,4},{7,5},{8,10},{9,11},{10,... | collective-permute-start | bytes 786440 | tf_op jit(solution)/shard_map/ppermute | solution.py:448
  84.8 22.6 %collective-permute-start.12 = (bf16[4,64,512]{2,1,0:T(8,128)(2,1)S(1)}, bf16[4,64,512]{2,1,0:T(8,128)(2,1)}, u32[]{:S(2)}, u32[]{:S(2)}) collective-permute-start(bf16[4,64,512]{2,1,0:T(8,128)(2,1)S(1)} %get-tuple-element.52.refs_0_), channel_id=1, source_target_pairs={{0,1},{1,0},{2,3},{3,2},{4,5},{5,4},{6,7},{7,6},{8,9},{9,8},{10,11... | collective-permute-start | bytes 786440 | tf_op jit(solution)/shard_map/ppermute | solution.py:448
  93.2 19.4 %collective-permute-start.23 = (bf16[64,3072]{1,0:T(8,128)(2,1)S(1)}, bf16[64,3072]{1,0:T(8,128)(2,1)}, u32[]{:S(2)}, u32[]{:S(2)}) collective-permute-start(bf16[64,3072]{1,0:T(8,128)(2,1)S(1)} %collective-permute-done.21.p1), channel_id=1, source_target_pairs={{0,2},{1,3},{2,0},{3,1},{4,6},{5,7},{6,4},{7,5},{8,10},{9,11},{10,... | collective-permute-start | bytes 1179656 | tf_op jit(solution)/shard_map/ppermute | solution.py:448
  94.7 22.1 %collective-permute-start.15 = (bf16[4,64,512]{2,1,0:T(8,128)(2,1)S(1)}, bf16[4,64,512]{2,1,0:T(8,128)(2,1)}, u32[]{:S(2)}, u32[]{:S(2)}) collective-permute-start(bf16[4,64,512]{2,1,0:T(8,128)(2,1)S(1)} %get-tuple-element.51.refs_4_), channel_id=1, source_target_pairs={{0,1},{1,0},{2,3},{3,2},{4,5},{5,4},{6,7},{7,6},{8,9},{9,8},{10,11... | collective-permute-start | bytes 786440 | tf_op jit(solution)/shard_map/ppermute | solution.py:448
  101.6 15.2 %collective-permute-start.13 = (bf16[4,64,512]{2,1,0:T(8,128)(2,1)S(1)}, bf16[4,64,512]{2,1,0:T(8,128)(2,1)}, u32[]{:S(2)}, u32[]{:S(2)}) collective-permute-start(bf16[4,64,512]{2,1,0:T(8,128)(2,1)S(1)} %get-tuple-element.52.refs_0_), channel_id=1, source_target_pairs={{0,2},{1,3},{2,0},{3,1},{4,6},{5,7},{6,4},{7,5},{8,10},{9,11},{10,... | collective-permute-start | bytes 786440 | tf_op jit(solution)/shard_map/ppermute | solution.py:448
  103.1 13.7 %collective-permute-start.17 = (bf16[4,64,512]{2,1,0:T(8,128)(2,1)S(1)}, bf16[4,64,512]{2,1,0:T(8,128)(2,1)}, u32[]{:S(2)}, u32[]{:S(2)}) collective-permute-start(bf16[4,64,512]{2,1,0:T(8,128)(2,1)S(1)} %collective-permute-done.16.refs_6_), channel_id=1, source_target_pairs={{0,1},{1,0},{2,3},{3,2},{4,5},{5,4},{6,7},{7,6},{8,9},{9,8},{10,11... | collective-permute-start | bytes 786440 | tf_op jit(solution)/shard_map/ppermute | solution.py:448
  107.3 9.5 %collective-permute-start.14 = (bf16[4,64,512]{2,1,0:T(8,128)(2,1)}, bf16[4,64,512]{2,1,0:T(8,128)(2,1)}, u32[]{:S(2)}, u32[]{:S(2)}) collective-permute-start(bf16[4,64,512]{2,1,0:T(8,128)(2,1)} %collective-permute-done.12.refs_1_), channel_id=1, source_target_pairs={{0,2},{1,3},{2,0},{3,1},{4,6},{5,7},{6,4},{7,5},{8,10},{9,11},{10,... | collective-permute-start | bytes 786440 | tf_op jit(solution)/shard_map/ppermute | solution.py:448
  116.9 0.6 copy-start.1
  123.9 8.6 %collective-permute-start.27 = (f32[512,512]{1,0:T(8,128)S(1)}, f32[512,512]{1,0:T(8,128)S(1)}, u32[]{:S(2)}, u32[]{:S(2)}) collective-permute-start(f32[512,512]{1,0:T(8,128)S(1)} %get-tuple-element.38.block_ref), channel_id=1, source_target_pairs={{0,16},{16,0},{1,17},{17,1},{2,18},{18,2},{3,19},{19,3},{4,20},{20... | collective-permute-start | bytes 3145736 | tf_op jit(solution)/shard_map/ppermute | solution.py:445
  129.1 27.2 %collective-permute-start.8 = (bf16[2,1024,1280]{2,1,0:T(8,128)(2,1)}, bf16[2,1024,1280]{2,1,0:T(8,128)(2,1)S(1)}, u32[]{:S(2)}, u32[]{:S(2)}) collective-permute-start(bf16[2,1024,1280]{2,1,0:T(8,128)(2,1)} %constant_dynamic-slice_fusion.1), channel_id=1, source_target_pairs={{0,16},{16,0},{1,17},{17,1},{2,18},{18,2},{3,19},{19,3},{4,20},{20... | collective-permute-start | bytes 15728648 | tf_op jit(solution)/shard_map/ppermute | solution.py:445
  132.5 23.8 %copy-start = (s32[22]{0:T(128)S(1)}, s32[22]{0:T(128)}, u32[]{:S(2)}) copy-start(s32[22]{0:T(128)} %pad_add_fusion.1.info) | copy-start | bytes 268
  132.5 23.8 %collective-permute-start.28 = (bf16[2,1024,1024]{2,1,0:T(8,128)(2,1)S(1)}, bf16[2,1024,1024]{2,1,0:T(8,128)(2,1)S(1)}, u32[]{:S(2)}, u32[]{:S(2)}) collective-permute-start(bf16[2,1024,1024]{2,1,0:T(8,128)(2,1)S(1)} %back_solve.1.qown), channel_id=1, source_target_pairs={{0,16},{16,0},{1,17},{17,1},{2,18},{18,2},{3,19},{19,3},{4,20},{20... | collective-permute-start | bytes 12582920 | tf_op jit(solution)/shard_map/ppermute | solution.py:445

commit v3 on v2

--- a/solution.py
+++ b/solution.py
@@ -120,44 +120,54 @@
     return pltpu.CompilerParams(vmem_limit_bytes=mib * MIB)
 
 
-def invert_dense_kernel(first, rows_ref, high, low):
-    invert_factor(rows_ref.at[:, LANE:], rows_ref.at[:, :LANE], high, low, first)
-
-
-def invert_pieces_kernel(first, place_ref, p0, p1, p2, p3, high, low, rest, fine):
-    rows = p0.shape[0]
-    planes = rest.shape[0] // (4 * rows)
-    for k, piece in enumerate((p0, p1, p2, p3)):
-        seat = place_ref[k]
+def invert_pieces_kernel(first, place_ref, *refs):
+    pieces, (high, low, rest, fine) = refs[:-4], refs[-4:]
+    arcs, size, _ = high.shape
+    rows = pieces[0].shape[0]
+    planes = size // (4 * rows)
+    for index, piece in enumerate(pieces):
+        arc, seat = index // 4, place_ref[index % 4]
         left = 0
         for plane in range(planes):
             width = 4 * rows * (plane + 1)
             at = pl.multiple_of((4 * plane + seat) * rows, 16)
-            fine[pl.ds(at, rows), :] = piece[:, left : left + LANE]
-            rest[pl.ds(at, rows), :width] = piece[:, left + LANE : left + LANE + width]
+            fine[arc, pl.ds(at, rows), :] = piece[:, left : left + LANE]
+            rest[arc, pl.ds(at, rows), :width] = piece[:, left + LANE : left + LANE + width]
             left += LANE + width
-    invert_factor(rest, fine, high, low, first)
-
-
-def invert_call(kernel, size, count, scratch):
-    out = jax.ShapeDtypeStruct((size, size), BF16)
+
+    def one(arc, _):
+        invert_factor(rest.at[arc], fine.at[arc], high.at[arc], low.at[arc], first)
+        return 0
+
+    lax.fori_loop(0, arcs, one, 0)
+
+
+def invert_dense_kernel(first, rows_ref, high, low):
+    def one(arc, _):
+        both = rows_ref.at[arc]
+        invert_factor(both.at[:, LANE:], both.at[:, :LANE], high.at[arc], low.at[arc], first)
+        return 0
+
+    lax.fori_loop(0, rows_ref.shape[0], one, 0)
+
+
+def invert_call(kernel, arcs, size, operands, scratch):
+    out = jax.ShapeDtypeStruct((arcs, size, size), BF16)
     return pl.pallas_call(
         kernel,
         out_shape=(out, out),
-        in_specs=[SM] * (count > 1) + [VM] * count,
+        in_specs=[SM if value.dtype == jnp.int32 else VM for value in operands],
         out_specs=(VM, VM),
         scratch_shapes=scratch,
-        compiler_params=grant(20),
+        compiler_params=grant(28),
         name="invert_factor",
-    )
+    )(*operands)
 
 
 def panel_kernel(arcs, place_ref, *refs):
-    count = (len(refs) - 3) // arcs - 2
-    pieces = refs[: arcs * count]
-    factors = refs[arcs * count : arcs * (count + 2)]
-    pt, block_ref, panel = refs[arcs * (count + 2) :]
-    size = panel.shape[0]
+    pieces, (high, low, pt, block_ref, panel) = refs[:-5], refs[-5:]
+    count = len(pieces) // arcs
+    size = panel.shape[1]
     span = min(256, size)
     nt = ((1,), (1,))
     for arc in range(arcs):
@@ -166,34 +176,40 @@
             rows = piece.shape[1]
             for z in range(piece.shape[0]):
                 at = pl.multiple_of(place_ref[index], 16)
-                panel[pl.ds(at, rows), :] = piece[z].astype(F32)
+                panel[arc, pl.ds(at, rows), :] = piece[z].astype(F32)
                 index += 1
-        raw = panel[...].T.astype(BF16)
-        high, low = factors[2 * arc], factors[2 * arc + 1]
+    block_ref[...] = jnp.zeros_like(block_ref)
+
+    def one(arc, _):
+        raw = panel[arc].T.astype(BF16)
         for top in range(0, size, span):
             end = top + span
-            value = mm(raw[:, :end], high[top:end, :end], nt) + mm(raw[:, :end], low[top:end, :end], nt)
+            value = mm(raw[:, :end], high[arc, top:end, :end], nt)
+            value += mm(raw[:, :end], low[arc, top:end, :end], nt)
             pt[arc, :, top:end] = value.astype(BF16)
-        part = mm(pt[arc], pt[arc], nt)
-        block_ref[...] = part if arc == 0 else block_ref[...] + part
-
-
-def back_kernel(arcs, pt, *refs):
-    factors, q_ref = refs[: 2 * arcs], refs[2 * arcs]
-    _, width, size = pt.shape
+        block_ref[...] += mm(pt[arc], pt[arc], nt)
+        return 0
+
+    lax.fori_loop(0, arcs, one, 0)
+
+
+def back_kernel(pt, high, low, q_ref):
+    arcs, width, size = pt.shape
     span = min(256, size)
-    for arc in range(arcs):
-        high, low = factors[2 * arc], factors[2 * arc + 1]
+
+    def one(arc, _):
         for top in range(0, size, span):
             end = top + span
             part = pt[arc, :, top:]
-            value = mm(part, high[top:, top:end]) + mm(part, low[top:, top:end])
+            value = mm(part, high[arc, top:, top:end]) + mm(part, low[arc, top:, top:end])
             q_ref[arc, :width, top:end], q_ref[arc, width:, top:end] = split(value)
+        return 0
+
+    lax.fori_loop(0, arcs, one, 0)
 
 
 def panel_call(place, pieces, factors):
-    arcs = len(factors) // 2
-    size = factors[0].shape[0]
+    arcs, size, _ = factors[0].shape
     width = pieces[0].shape[2]
     return pl.pallas_call(
         functools.partial(panel_kernel, arcs),
@@ -203,7 +219,7 @@
         ),
         in_specs=[SM] + [VM] * (len(pieces) + len(factors)),
         out_specs=(VM, VM),
-        scratch_shapes=[pltpu.VMEM((size, width), F32)],
+        scratch_shapes=[pltpu.VMEM((arcs, size, width), F32)],
         compiler_params=grant(26),
         name="panel_block",
     )(place, *pieces, *factors)
@@ -212,7 +228,7 @@
 def back_call(pt, factors):
     arcs, width, size = pt.shape
     return pl.pallas_call(
-        functools.partial(back_kernel, arcs),
+        back_kernel,
         out_shape=jax.ShapeDtypeStruct((arcs, 2 * width, size), BF16),
         in_specs=[VM] * (1 + len(factors)),
         out_specs=VM,
@@ -221,73 +237,59 @@
     )(pt, *factors)
 
 
-def normals_kernel(info, own, far, qown, qfar, inv_ref, reg_ref, out_ref, data, qs, acc, sems):
-    near = own.shape[0]
-    arcs = 2 * near
-    size, share = acc.shape
+def normals_kernel(info, far, qs, sums, inv_ref, reg_ref, out_ref, data, acc, sems):
+    arcs, _, share = far.shape
+    width = inv_ref.shape[0]
     blocks = share // BLK
-    half = size // 2
-    left = pl.multiple_of(info[0] * BLK, BLK)
+    half = width // 2
     copies = []
     for arc in range(arcs):
-        if arc < near:
-            source, q = own.at[arc, :, pl.ds(left, share)], qown.at[arc]
-        else:
-            source, q = far.at[arc - near], qfar.at[arc - near]
-        pair = (
-            pltpu.make_async_copy(q, qs.at[arc], sems.at[2 * arc]),
-            pltpu.make_async_copy(source, data.at[arc], sems.at[2 * arc + 1]),
-        )
-        for copy in pair:
-            copy.start()
-        copies.append(pair)
-    acc[...] = jnp.zeros_like(acc)
-    for arc in range(arcs):
-        for copy in copies[arc]:
-            copy.wait()
+        copies.append(pltpu.make_async_copy(far.at[arc], data.at[arc], sems.at[arc]))
+        copies[arc].start()
+    for block in range(blocks):
+        acc[block] = sums[block]
+    for arc in range(arcs):
+        copies[arc].wait()
 
         def add(block, _):
-            @pl.when(info[2 + block * arcs + arc] > 0)
+            @pl.when(info[2 + block * 2 * arcs + arcs + arc] > 0)
             def _():
                 at = pl.ds(pl.multiple_of(block * BLK, BLK), BLK)
                 both = mm(qs[arc], data[arc, :, at])
-                acc[:, at] += both[:size] + both[size:]
+                acc[block] += both[:width] + both[width:]
 
             return 0
 
         lax.fori_loop(0, blocks, add, 0)
     ih, il = split(inv_ref[...])
-    row = lax.broadcasted_iota(jnp.int32, (size, BLK), 0) + info[1]
-    col = lax.broadcasted_iota(jnp.int32, (size, BLK), 1)
+    row = lax.broadcasted_iota(jnp.int32, (width, BLK), 0) + info[1]
+    col = lax.broadcasted_iota(jnp.int32, (width, BLK), 1)
     for block in range(blocks):
         at = slice(block * BLK, (block + 1) * BLK)
         hit = row == col + block * BLK
-        th, tl = split(acc[:, at] + jnp.where(hit, reg_ref[:, at], 0.0))
-        for top, end in ((0, half), (half, size)):
+        th, tl = split(acc[block] + jnp.where(hit, reg_ref[:, at], 0.0))
+        for top, end in ((0, half), (half, width)):
             value = mm(ih[top:end, :end], th[:end]) + mm(ih[top:end, :end], tl[:end])
             out_ref[top:end, at] = value + mm(il[top:end, :end], th[:end])
 
 
-def normals_call(info, own, far, qown, qfar, inverse, reg):
-    near, size, _ = own.shape
-    arcs = 2 * near
-    share = far.shape[2]
+def normals_call(info, far, qfar, sums, inverse, reg):
+    arcs, size, share = far.shape
     width = inverse.shape[0]
-    hbm = pl.BlockSpec(memory_space=pl.ANY)
+    hbm = pl.BlockSpec(memory_space=pltpu.HBM)
     return pl.pallas_call(
         normals_kernel,
         out_shape=jax.ShapeDtypeStruct((width, share), F32),
-        in_specs=[SM, hbm, hbm, hbm, hbm, VM, VM],
+        in_specs=[SM, hbm, VM, VM, VM, VM],
         out_specs=VM,
         scratch_shapes=[
             pltpu.VMEM((arcs, size, share), BF16),
-            pltpu.VMEM((arcs, 2 * width, size), BF16),
-            pltpu.VMEM((width, share), F32),
-            pltpu.SemaphoreType.DMA((2 * arcs,)),
+            pltpu.VMEM((share // BLK, width, BLK), F32),
+            pltpu.SemaphoreType.DMA((arcs,)),
         ],
-        compiler_params=grant(36),
+        compiler_params=grant(28),
         name="normals",
-    )(info, own, far, qown, qfar, inverse, reg)
+    )(info, far, qfar, sums, inverse, reg)
 
 
 SUB = 8
@@ -300,7 +302,7 @@
     return high, mid, (rest - mid.astype(F32)).astype(BF16)
 
 
-def factor_diag(work):
+def factor_diag(work, between):
     tn = ((0,), (0,))
     wide = work.shape[1]
     for top in range(0, LANE, SUB):
@@ -330,9 +332,10 @@
             rhs = jnp.concatenate([h, m, h, m, l, h], axis=0)
             gone = mm(lhs, rhs, tn)
             work[end:, :] = work[end:, :] - gone[end:, :]
-
-
-def chol_kernel(block_ref, other_ref, reg_ref, out_ref, full, work, upper):
+        between()
+
+
+def chol_body(block_ref, other_ref, reg_ref, out_ref, full, work, upper, between):
     size = block_ref.shape[0]
     row = lax.broadcasted_iota(jnp.int32, (size, size), 0)
     col = lax.broadcasted_iota(jnp.int32, (size, size), 1)
@@ -344,7 +347,7 @@
         end = top + LANE
         work[:, :LANE] = full[top:end, top:end]
         work[:, LANE:] = (r1 == c1).astype(F32)
-        factor_diag(work)
+        factor_diag(work, between)
         inverse = jnp.where(r1 >= c1, work[:, LANE:], 0.0)
         out_ref[top:end, top:end] = inverse
         if end < size:
@@ -360,6 +363,72 @@
             low = upper[left, second].T
             out_ref[second, left] = -mm3(out_ref[second, second], mm3(low, out_ref[left, left]))
         step *= 2
+
+
+def chol_kernel(*refs):
+    chol_body(*refs, lambda: None)
+
+
+def chol_normals_kernel(info, block_ref, other_ref, reg_ref, own, qs, out_ref, sums, full, work, upper, data, sems):
+    arcs, size, share = data.shape
+    width = block_ref.shape[0]
+    blocks = share // BLK
+    left = pl.multiple_of(info[0] * BLK, BLK)
+    copies = []
+    for arc in range(arcs):
+        source = own.at[arc, :, pl.ds(left, share)]
+        copies.append(pltpu.make_async_copy(source, data.at[arc], sems.at[arc]))
+    for copy in copies:
+        copy.start()
+    for block in range(blocks + 1):
+        sums[block] = jnp.zeros((width, BLK), F32)
+    span = min(256, size)
+    slices = [(arc, block, top) for arc in range(arcs) for block in range(blocks) for top in range(0, size, span)]
+    panels = width // SUB
+    delay = panels // 4
+    state = [0, 0]
+
+    def between():
+        state[0] += 1
+        if state[0] == delay:
+            for copy in copies:
+                copy.wait()
+        goal = len(slices) * max(state[0] - delay, 0) // (panels - delay)
+        while state[1] < goal:
+            arc, block, top = slices[state[1]]
+            state[1] += 1
+            target = jnp.where(info[2 + block * 2 * arcs + arc] > 0, block, blocks)
+            at = slice(block * BLK, (block + 1) * BLK)
+            rows = slice(top, top + span)
+            value = mm(qs[arc, :, rows], data[arc, rows, at])
+            sums[target] += value[:width] + value[width:]
+
+    chol_body(block_ref, other_ref, reg_ref, out_ref, full, work, upper, between)
+
+
+def chol_normals(info, block, other, reg, own, qown):
+    arcs, observed, _ = own.shape
+    size = block.shape[0]
+    share = own.shape[2] // 2
+    hbm = pl.BlockSpec(memory_space=pltpu.HBM)
+    return pl.pallas_call(
+        chol_normals_kernel,
+        out_shape=(
+            jax.ShapeDtypeStruct((size, size), F32),
+            jax.ShapeDtypeStruct((share // BLK + 1, size, BLK), F32),
+        ),
+        in_specs=[SM, VM, VM, VM, hbm, VM],
+        out_specs=(VM, VM),
+        scratch_shapes=[
+            pltpu.VMEM((size, size), F32),
+            pltpu.VMEM((LANE, 2 * LANE), F32),
+            pltpu.VMEM((size, size), F32),
+            pltpu.VMEM((arcs, observed, share), BF16),
+            pltpu.SemaphoreType.DMA((arcs,)),
+        ],
+        compiler_params=grant(28),
+        name="chol_normals",
+    )(info, block, other, reg, own, qown)
 
 
 def chol_inverse(block, other, reg):
@@ -409,10 +478,7 @@
         padded, jnp.clip(start - par_id * columns + PANEL, 0, columns + PANEL), PANEL, 2
     )
     panel = lax.psum(window.astype(F32).astype(BF16), "par")
-    factors = []
-    for arc in range(arcs):
-        call = invert_call(functools.partial(invert_dense_kernel, rows), observed, 1, [])
-        factors += call(lower[arc])
+    factors = invert_call(functools.partial(invert_dense_kernel, rows), arcs, observed, [lower], [])
     place = jnp.zeros((arcs,), jnp.int32)
     pt, block = panel_call(place, [panel[arc : arc + 1] for arc in range(arcs)], factors)
     qs = back_call(pt, factors)
@@ -523,14 +589,14 @@
         (chunk, seats, info, reg, reg_panel, place)
     )
 
-    factors = []
+    shares = [seats]
     for arc in range(arcs):
         pieces = spread(packed[arc], 1 + arc % 2)
-        call = invert_call(
-            functools.partial(invert_pieces_kernel, rows), observed, 4,
-            [pltpu.VMEM((observed, observed), BF16), pltpu.VMEM((observed, LANE), BF16)],
-        )
-        factors += call(seats, *[pieces[k] for k in range(4)])
+        shares += [pieces[k] for k in range(4)]
+    factors = invert_call(
+        functools.partial(invert_pieces_kernel, rows), arcs, observed, shares,
+        [pltpu.VMEM((arcs, observed, observed), BF16), pltpu.VMEM((arcs, observed, LANE), BF16)],
+    )
 
     stack = [chunk] + [hop(chunk, 4 * k) for k in range(1, planes)]
     stack = jnp.stack(stack, axis=1)
@@ -542,8 +608,8 @@
     other = swap(block)
     qs = back_call(pt, factors)
     qs, other = lax.optimization_barrier((qs, other))
-    inverse = chol_inverse(block, other, reg_panel)
-    return normals_call(info, design, far, qs, swap(qs), inverse, reg)
+    inverse, sums = chol_normals(info, block, other, reg_panel, design, qs)
+    return normals_call(info, far, swap(qs), sums, inverse, reg)
 
 
 def whole(design, cov_factor, *rest):

time: 174 us -> 175 us (level)
  the two profiles are of different devices: /device:TPU:22 before, /device:TPU:0 now
where the time goes in v3:
time: 175 us; the launch traced here: 172 us
  Pallas kernels  57.5 us (33%)
  waiting for transfers between devices  51.3 us (29%)
  starting transfers between devices  34.1 us (19%)
  local copies, waits for them, and re-layouts  13.9 us (8%)
  other arithmetic  13.9 us (8%)
    ppermute x25, waiting for transfers between devices, hop(): return lax.ppermute(value, 'par', [(p, p ^ bits) for p in range(chips)])  51.2 us
    ppermute x25, starting transfers between devices, hop(): return lax.ppermute(value, 'par', [(p, p ^ bits) for p in range(chips)])  33.3 us
    pallas_call x1, Pallas kernels, chol_normals(): pl.pallas_call(chol_normals_kernel, out_shape=(jax.ShapeDtypeStruct((size...  27.4 us
    pallas_call x1, Pallas kernels, panel_call(): pl.pallas_call(functools.partial(panel_kernel, arcs), out_shape=(jax.Shap...  8.28 us
    pallas_call x1, Pallas kernels, invert_call(): pl.pallas_call(kernel, out_shape=(out, out), in_specs=[SM if value.dtype...  7.63 us
    pallas_call x1, Pallas kernels, normals_call(): pl.pallas_call(normals_kernel, out_shape=jax.ShapeDtypeStruct((width, sha...  7.35 us
    dynamic_slice x1, local copies, waits for them, and re-layouts, paired(): far = lax.dynamic_slice_in_dim(design, (1 - core) * share, share, 2)  5.64 us
    unnamed x22, local copies, waits for them, and re-layouts  4.24 us
  transfers between devices with their start and end apart: 29, of which 11 were waited for; matrix products, arithmetic and copies ran while one was open for 9% of the time, Pallas kernels for 22%

profile of v3, /device:TPU:0, one launch (start us, length us, event | category | flops | bytes accessed | tf_op | source)
XLA Modules:
  0.0 171.9 jit_solution(10949441192600986573)
XLA Ops:
  0.8 0.9 compare_reduce_fusion.1
  1.9 3.7 %bitcast_select_fusion = (bf16[512,512]{1,0:T(8,128)(2,1)S(1)}, bf16[512,512]{1,0:T(8,128)(2,1)}, bf16[512,512]{1,0:T(8,128)(2,1)}, bf16[512,512]{1,0:T(8,128)(2,1)S(1)}) fusion(bf16[2,1024,2560]{2,1,0:T(8,128)(2,1)} %own.1, s32[]{:T(128)S(6)} %select_n.177, s32[]{:T(128)S(6)} %min.4, pred[512]{0:T(512)(128)(4,1)S(1)} %broadcast_in_dim.55, ...), kind=kLoop, calls=%fused_computation.14 | loop fusion | flops 1048576 | bytes 4195348 | tf_op jit(solution)/shard_map/jit(_where)/select_n | solution.py:530
  6.3 3.8 %invert_diag.1 = (bf16[2,64,128]{2,1,0:T(8,128)(2,1)}, bf16[2,64,128]{2,1,0:T(8,128)(2,1)}) custom-call(s32[1]{0:T(128)} %bitcast.26.off_ref, f32[2,64,128]{2,1,0:T(8,128)} %constant_dynamic-slice_fusion.strip_ref), custom_call_target="tpu_custom_call" | custom-call | tf_op jit(solution)/shard_map/invert_diag/pallas_call | solution.py:70
  10.1 0.8 constant_dynamic-update-slice_fusion
  10.8 0.8 pad_maximum_fusion.1
  11.6 5.4 %collective-permute-start.18 = (bf16[2,64,1152]{2,1,0:T(8,128)(2,1)S(1)}, bf16[2,64,1152]{2,1,0:T(8,128)(2,1)S(1)}, u32[]{:S(2)}, u32[]{:S(2)}) collective-permute-start(bf16[2,64,1152]{2,1,0:T(8,128)(2,1)S(1)} %pad_maximum_fusion.1), channel_id=1, source_target_pairs={{0,12},{1,13},{2,14},{3,15},{4,8},{5,9},{6,10},{7,11},{8,4},{9,5},... | collective-permute-start | bytes 884744 | tf_op jit(solution)/shard_map/ppermute | solution.py:514
  17.7 1.5 collective-permute-start.2
  20.7 0.8 dynamic_slice.77
  21.5 0.8 dynamic_slice.78
  22.3 1.5 collective-permute-start
  25.1 16.8 %collective-permute-done.19 = bf16[2,64,1152]{2,1,0:T(8,128)(2,1)S(1)} collective-permute-done((bf16[2,64,1152]{2,1,0:T(8,128)(2,1)S(1)}, bf16[2,64,1152]{2,1,0:T(8,128)(2,1)S(1)}, u32[]{:S(2)}, u32[]{:S(2)}) %collective-permute-start.19) | collective-permute-done | bytes 294944 | tf_op jit(solution)/shard_map/ppermute | solution.py:514
  41.9 0.8 fusion.7
  42.7 0.9 fusion.3
  43.6 0.8 fusion.22
  44.4 0.9 select_select_fusion
  45.5 1.6 collective-permute-start.3
  47.0 1.0 dynamic-slice_add_fusion.1
  48.1 1.6 collective-permute-start.1
  49.7 3.0 %collective-permute-done.3 = bf16[256,512]{1,0:T(8,128)(2,1)S(1)} collective-permute-done((bf16[256,512]{1,0:T(8,128)(2,1)S(1)}, bf16[256,512]{1,0:T(8,128)(2,1)S(1)}, u32[]{:S(2)}, u32[]{:S(2)}) %collective-permute-start.3) | collective-permute-done | bytes 262176 | tf_op jit(solution)/shard_map/ppermute | solution.py:514
  52.7 1.1 add_add_fusion
  53.8 1.3 collective-permute-done.1
  55.0 1.1 add_add_fusion.1
  56.2 3.0 %collective-permute-start.5 = (bf16[2,64,512]{2,1,0:T(8,128)(2,1)S(1)}, bf16[2,64,512]{2,1,0:T(8,128)(2,1)S(1)}, u32[]{:S(2)}, u32[]{:S(2)}) collective-permute-start(bf16[2,64,512]{2,1,0:T(8,128)(2,1)S(1)} %get-tuple-element.54), channel_id=1, source_target_pairs={{0,8},{1,9},{2,10},{3,11},{4,12},{5,13},{6,14},{7,15},{8,0},{9,1},... | collective-permute-start | bytes 393224 | tf_op jit(solution)/shard_map/ppermute | solution.py:514
  59.2 1.4 collective-permute-start.6
  61.3 1.4 collective-permute-done.4
  62.7 4.8 %collective-permute-done.5 = bf16[2,64,512]{2,1,0:T(8,128)(2,1)S(1)} collective-permute-done((bf16[2,64,512]{2,1,0:T(8,128)(2,1)S(1)}, bf16[2,64,512]{2,1,0:T(8,128)(2,1)S(1)}, u32[]{:S(2)}, u32[]{:S(2)}) %collective-permute-start.5) | collective-permute-done | bytes 131104 | tf_op jit(solution)/shard_map/ppermute | solution.py:514
  67.6 2.0 %collective-permute-start.9 = (bf16[2,64,512]{2,1,0:T(8,128)(2,1)S(1)}, bf16[2,64,512]{2,1,0:T(8,128)(2,1)S(1)}, u32[]{:S(2)}, u32[]{:S(2)}) collective-permute-start(bf16[2,64,512]{2,1,0:T(8,128)(2,1)S(1)} %fusion.14), channel_id=1, source_target_pairs={{0,4},{1,5},{2,6},{3,7},{4,0},{5,1},{6,2},{7,3},{8,12},{9,13},{10,... | collective-permute-start | bytes 393224 | tf_op jit(solution)/shard_map/ppermute | solution.py:514
  69.6 1.1 collective-permute-start.10
  70.7 1.4 collective-permute-start.11
  72.0 1.7 collective-permute-start.25
  74.6 6.3 %collective-permute-done.10 = bf16[2,64,512]{2,1,0:T(8,128)(2,1)S(1)} collective-permute-done((bf16[2,64,512]{2,1,0:T(8,128)(2,1)S(1)}, bf16[2,64,512]{2,1,0:T(8,128)(2,1)S(1)}, u32[]{:S(2)}, u32[]{:S(2)}) %collective-permute-start.10) | collective-permute-done | bytes 131104 | tf_op jit(solution)/shard_map/ppermute | solution.py:514
  81.0 1.6 collective-permute-start.23
  82.7 0.7 collective-permute-start.12
  84.0 1.7 collective-permute-start.16
  85.7 6.7 %collective-permute-done.22.refs_2_ = bf16[64,3072]{1,0:T(8,128)(2,1)S(1)} collective-permute-done((bf16[64,3072]{1,0:T(8,128)(2,1)S(1)}, bf16[64,3072]{1,0:T(8,128)(2,1)S(1)}, u32[]{:S(2)}, u32[]{:S(2)}) %collective-permute-start.22) | collective-permute-done | bytes 393248 | tf_op jit(solution)/shard_map/ppermute | solution.py:514
  93.0 1.7 collective-permute-start.13
  94.7 6.2 %collective-permute-done.23.refs_3_ = bf16[64,3072]{1,0:T(8,128)(2,1)S(1)} collective-permute-done((bf16[64,3072]{1,0:T(8,128)(2,1)S(1)}, bf16[64,3072]{1,0:T(8,128)(2,1)S(1)}, u32[]{:S(2)}, u32[]{:S(2)}) %collective-permute-start.23) | collective-permute-done | bytes 393248 | tf_op jit(solution)/shard_map/ppermute | solution.py:514
  101.4 1.7 collective-permute-start.14
  103.1 3.5 %collective-permute-done.16.refs_6_ = bf16[4,64,512]{2,1,0:T(8,128)(2,1)} collective-permute-done((bf16[4,64,512]{2,1,0:T(8,128)(2,1)S(1)}, bf16[4,64,512]{2,1,0:T(8,128)(2,1)}, u32[]{:S(2)}, u32[]{:S(2)}) %collective-permute-start.16) | collective-permute-done | bytes 262176 | tf_op jit(solution)/shard_map/ppermute | solution.py:514
  107.8 7.6 %invert_factor.1 = (bf16[2,1024,1024]{2,1,0:T(8,128)(2,1)S(1)}, bf16[2,1024,1024]{2,1,0:T(8,128)(2,1)S(1)}) custom-call(s32[4]{0:T(128)S(1)} %copy-done.2, bf16[64,3072]{1,0:T(8,128)(2,1)S(1)} %get-tuple-element.50.refs_0_, bf16[64,3072]{1,0:T(8,128)(2,1)S(1)} %collective-permute-done.21.refs_1_, bf16[64,3072]{1,0:T(8,128)(2,1)S(1)} %collective-permute-done.22.refs_2_, ...), custom_call_target="tpu_custom_call" | custom-call | tf_op jit(solution)/shard_map/invert_factor/pallas_call | solution.py:156
  115.5 0.7 copy-done.3
  116.1 8.3 %panel_block.1 = (bf16[2,512,1024]{2,1,0:T(8,128)(2,1)S(1)}, f32[512,512]{1,0:T(8,128)}) custom-call(s32[32]{0:T(128)S(1)} %copy-done.3, bf16[4,64,512]{2,1,0:T(8,128)(2,1)S(1)} %get-tuple-element.52.refs_0_, bf16[4,64,512]{2,1,0:T(8,128)(2,1)S(1)} %collective-permute-done.12.refs_1_, bf16[4,64,512]{2,1,0:T(8,128)(2,1)} %collective-permute-done.13.refs_2_, ...), custom_call_target="tpu_custom_call" | custom-call | tf_op jit(solution)/shard_map/panel_block/pallas_call | solution.py:214
  124.4 1.3 copy-done
  125.8 5.6 %constant_dynamic-slice_fusion.1 = bf16[2,1024,1280]{2,1,0:T(8,128)(2,1)} fusion(bf16[2,1024,2560]{2,1,0:T(8,128)(2,1)} %own.1, s32[]{:T(128)S(6)} %select_n.188), kind=kLoop, calls=%fused_computation.56 | loop fusion | bytes 10485764 | tf_op jit(solution)/shard_map/dynamic_slice | solution.py:586
  131.9 1.6 copy-done.1
  133.5 3.0 %back_solve.1.qs = bf16[2,1024,1024]{2,1,0:T(8,128)(2,1)S(1)} custom-call(bf16[2,512,1024]{2,1,0:T(8,128)(2,1)S(1)} %copy-done.1, bf16[2,1024,1024]{2,1,0:T(8,128)(2,1)S(1)} %get-tuple-element.33.refs_8_.high, bf16[2,1024,1024]{2,1,0:T(8,128)(2,1)S(1)} %get-tuple-element.34.refs_9_.low), custom_call_target="tpu_custom_call" | custom-call | tf_op jit(solution)/shard_map/back_solve/pallas_call | solution.py:230
  136.9 27.4 %chol_normals.1 = (f32[512,512]{1,0:T(8,128)S(1)}, f32[6,512,256]{2,1,0:T(8,128)S(1)}) custom-call(s32[22]{0:T(128)S(1)} %pad_add_fusion.1.info, f32[512,512]{1,0:T(8,128)} %get-tuple-element.36.block_ref, f32[512,512]{1,0:T(8,128)} %collective-permute-done.27.other_ref, f32[1,512]{1,0:T(1,128)S(1)} %bitcast.55, bf16[2,1024,2560]{2,1,0:T(8,128)(2,1)S(1)} %bitcast.54, ...), custom_call_target="tpu_custom_call" | custom-call | tf_op jit(solution)/shard_map/chol_normals/pallas_call | solution.py:414
  164.4 7.4 %normals.1 = f32[512,1280]{1,0:T(8,128)} custom-call(s32[22]{0:T(128)S(1)} %pad_add_fusion.1.info, bf16[2,1024,1280]{2,1,0:T(8,128)(2,1)S(1)} %collective-permute-done.8.far, bf16[2,1024,1024]{2,1,0:T(8,128)(2,1)S(1)} %collective-permute-done.28.qs, f32[6,512,256]{2,1,0:T(8,128)S(1)} %get-tuple-element.40.sums, f32[512,512]{1,0:T(8,128)S(1)} %get-tuple-element.41.inv_ref, ...), custom_call_target="tpu_custom_call" | custom-call | tf_op jit(solution)/shard_map/normals/pallas_call | solution.py:280
  (84 shorter events, 10.1 us)
Async XLA Ops:
  0.0 17.7 %copy-start.6 = (s32[2,80]{1,0:T(2,128)S(1)}, s32[2,80]{1,0:T(2,128)}, u32[]{:S(2)}) copy-start(s32[2,80]{1,0:T(2,128)} %param.7) | copy-start | bytes 1924
  0.0 5.6 %copy-start.4 = (f32[2,64,1024]{2,1,0:T(8,128)S(1)}, f32[2,64,1024]{2,1,0:T(8,128)}, u32[]{:S(2)}) copy-start(f32[2,64,1024]{2,1,0:T(8,128)} %param.6) | copy-start | bytes 1572868
  11.6 13.4 %collective-permute-start.18 = (bf16[2,64,1152]{2,1,0:T(8,128)(2,1)S(1)}, bf16[2,64,1152]{2,1,0:T(8,128)(2,1)S(1)}, u32[]{:S(2)}, u32[]{:S(2)}) collective-permute-start(bf16[2,64,1152]{2,1,0:T(8,128)(2,1)S(1)} %pad_maximum_fusion.1), channel_id=1, source_target_pairs={{0,12},{1,13},{2,14},{3,15},{4,8},{5,9},{6,10},{7,11},{8,4},{9,5},... | collective-permute-start | bytes 884744 | tf_op jit(solution)/shard_map/ppermute | solution.py:514
  17.1 24.8 %collective-permute-start.19 = (bf16[2,64,1152]{2,1,0:T(8,128)(2,1)S(1)}, bf16[2,64,1152]{2,1,0:T(8,128)(2,1)S(1)}, u32[]{:S(2)}, u32[]{:S(2)}) collective-permute-start(bf16[2,64,1152]{2,1,0:T(8,128)(2,1)S(1)} %pad_maximum_fusion.1), channel_id=1, source_target_pairs={{0,8},{1,9},{2,10},{3,11},{4,12},{5,13},{6,14},{7,15},{8,0},{9,1},... | collective-permute-start | bytes 884744 | tf_op jit(solution)/shard_map/ppermute | solution.py:514
  17.1 24.8 %collective-permute-start.20 = (bf16[2,64,1152]{2,1,0:T(8,128)(2,1)S(1)}, bf16[2,64,1152]{2,1,0:T(8,128)(2,1)S(1)}, u32[]{:S(2)}, u32[]{:S(2)}) collective-permute-start(bf16[2,64,1152]{2,1,0:T(8,128)(2,1)S(1)} %pad_maximum_fusion.1), channel_id=1, source_target_pairs={{0,4},{1,5},{2,6},{3,7},{4,0},{5,1},{6,2},{7,3},{8,12},{9,13},{10,... | collective-permute-start | bytes 884744 | tf_op jit(solution)/shard_map/ppermute | solution.py:514
  17.7 4.6 %collective-permute-start.7 = (s32[2,80]{1,0:T(2,128)S(1)}, s32[2,80]{1,0:T(2,128)S(1)}, u32[]{:S(2)}, u32[]{:S(2)}) collective-permute-start(s32[2,80]{1,0:T(2,128)S(1)} %copy-done.6), channel_id=1, source_target_pairs={{0,16},{16,0},{1,17},{17,1},{2,18},{18,2},{3,19},{19,3},{4,20},{20... | collective-permute-start | bytes 1928 | tf_op jit(solution)/shard_map/ppermute | solution.py:511
  17.7 27.7 %collective-permute-start.2 = (bf16[512,512]{1,0:T(8,128)(2,1)}, bf16[512,512]{1,0:T(8,128)(2,1)S(1)}, u32[]{:S(2)}, u32[]{:S(2)}) collective-permute-start(bf16[512,512]{1,0:T(8,128)(2,1)} %get-tuple-element.25), channel_id=1, source_target_pairs={{0,2},{1,3},{2,0},{3,1},{4,6},{5,7},{6,4},{7,5},{8,10},{9,11},{10,... | collective-permute-start | bytes 1572872 | tf_op jit(solution)/shard_map/ppermute | solution.py:514
  22.3 24.8 %collective-permute-start = (bf16[512,512]{1,0:T(8,128)(2,1)}, bf16[512,512]{1,0:T(8,128)(2,1)}, u32[]{:S(2)}, u32[]{:S(2)}) collective-permute-start(bf16[512,512]{1,0:T(8,128)(2,1)} %get-tuple-element.24), channel_id=1, source_target_pairs={{0,1},{1,0},{2,3},{3,2},{4,5},{5,4},{6,7},{7,6},{8,9},{9,8},{10,11... | collective-permute-start | bytes 1572872 | tf_op jit(solution)/shard_map/ppermute | solution.py:514
  45.4 15.9 %copy-start.7 = (s32[20]{0:T(128)S(1)}, s32[20]{0:T(128)}, u32[]{:S(2)}) copy-start(s32[20]{0:T(128)} %reshape.46) | copy-start | bytes 244
  45.4 2.7 %copy-start.5 = (bf16[512,512]{1,0:T(8,128)(2,1)}, bf16[512,512]{1,0:T(8,128)(2,1)S(1)}, u32[]{:S(2)}) copy-start(bf16[512,512]{1,0:T(8,128)(2,1)S(1)} %collective-permute-done.2) | copy-start | bytes 1572868
  45.5 7.3 %collective-permute-start.3 = (bf16[256,512]{1,0:T(8,128)(2,1)S(1)}, bf16[256,512]{1,0:T(8,128)(2,1)S(1)}, u32[]{:S(2)}, u32[]{:S(2)}) collective-permute-start(bf16[256,512]{1,0:T(8,128)(2,1)S(1)} %dynamic-slice_add_fusion), channel_id=1, source_target_pairs={{0,1},{1,0},{2,3},{3,2},{4,5},{5,4},{6,7},{7,6},{8,9},{9,8},{10,11... | collective-permute-start | bytes 786440 | tf_op jit(solution)/shard_map/ppermute | solution.py:514
  48.1 7.0 %collective-permute-start.1 = (bf16[256,512]{1,0:T(8,128)(2,1)S(1)}, bf16[256,512]{1,0:T(8,128)(2,1)S(1)}, u32[]{:S(2)}, u32[]{:S(2)}) collective-permute-start(bf16[256,512]{1,0:T(8,128)(2,1)S(1)} %dynamic-slice_add_fusion.1), channel_id=1, source_target_pairs={{0,2},{1,3},{2,0},{3,1},{4,6},{5,7},{6,4},{7,5},{8,10},{9,11},{10,... | collective-permute-start | bytes 786440 | tf_op jit(solution)/shard_map/ppermute | solution.py:514
  56.1 6.6 %collective-permute-start.4 = (bf16[2,64,512]{2,1,0:T(8,128)(2,1)S(1)}, bf16[2,64,512]{2,1,0:T(8,128)(2,1)S(1)}, u32[]{:S(2)}, u32[]{:S(2)}) collective-permute-start(bf16[2,64,512]{2,1,0:T(8,128)(2,1)S(1)} %get-tuple-element.53), channel_id=1, source_target_pairs={{0,4},{1,5},{2,6},{3,7},{4,0},{5,1},{6,2},{7,3},{8,12},{9,13},{10,... | collective-permute-start | bytes 393224 | tf_op jit(solution)/shard_map/ppermute | solution.py:514
  56.2 11.3 %collective-permute-start.5 = (bf16[2,64,512]{2,1,0:T(8,128)(2,1)S(1)}, bf16[2,64,512]{2,1,0:T(8,128)(2,1)S(1)}, u32[]{:S(2)}, u32[]{:S(2)}) collective-permute-start(bf16[2,64,512]{2,1,0:T(8,128)(2,1)S(1)} %get-tuple-element.54), channel_id=1, source_target_pairs={{0,8},{1,9},{2,10},{3,11},{4,12},{5,13},{6,14},{7,15},{8,0},{9,1},... | collective-permute-start | bytes 393224 | tf_op jit(solution)/shard_map/ppermute | solution.py:514
  59.2 8.3 %collective-permute-start.6 = (bf16[2,64,512]{2,1,0:T(8,128)(2,1)S(1)}, bf16[2,64,512]{2,1,0:T(8,128)(2,1)S(1)}, u32[]{:S(2)}, u32[]{:S(2)}) collective-permute-start(bf16[2,64,512]{2,1,0:T(8,128)(2,1)S(1)} %get-tuple-element.55), channel_id=1, source_target_pairs={{0,12},{1,13},{2,14},{3,15},{4,8},{5,9},{6,10},{7,11},{8,4},{9,5},... | collective-permute-start | bytes 393224 | tf_op jit(solution)/shard_map/ppermute | solution.py:514
  60.7 13.1 %collective-permute-start.21 = (bf16[64,3072]{1,0:T(8,128)(2,1)S(1)}, bf16[64,3072]{1,0:T(8,128)(2,1)S(1)}, u32[]{:S(2)}, u32[]{:S(2)}) collective-permute-start(bf16[64,3072]{1,0:T(8,128)(2,1)S(1)} %get-tuple-element.50.refs_0_), channel_id=1, source_target_pairs={{0,1},{1,0},{2,3},{3,2},{4,5},{5,4},{6,7},{7,6},{8,9},{9,8},{10,11... | collective-permute-start | bytes 1179656 | tf_op jit(solution)/shard_map/ppermute | solution.py:514
  67.6 6.5 %collective-permute-start.9 = (bf16[2,64,512]{2,1,0:T(8,128)(2,1)S(1)}, bf16[2,64,512]{2,1,0:T(8,128)(2,1)S(1)}, u32[]{:S(2)}, u32[]{:S(2)}) collective-permute-start(bf16[2,64,512]{2,1,0:T(8,128)(2,1)S(1)} %fusion.14), channel_id=1, source_target_pairs={{0,4},{1,5},{2,6},{3,7},{4,0},{5,1},{6,2},{7,3},{8,12},{9,13},{10,... | collective-permute-start | bytes 393224 | tf_op jit(solution)/shard_map/ppermute | solution.py:514
  69.6 11.4 %collective-permute-start.10 = (bf16[2,64,512]{2,1,0:T(8,128)(2,1)S(1)}, bf16[2,64,512]{2,1,0:T(8,128)(2,1)S(1)}, u32[]{:S(2)}, u32[]{:S(2)}) collective-permute-start(bf16[2,64,512]{2,1,0:T(8,128)(2,1)S(1)} %fusion.14), channel_id=1, source_target_pairs={{0,8},{1,9},{2,10},{3,11},{4,12},{5,13},{6,14},{7,15},{8,0},{9,1},... | collective-permute-start | bytes 393224 | tf_op jit(solution)/shard_map/ppermute | solution.py:514
  70.7 11.9 %collective-permute-start.11 = (bf16[2,64,512]{2,1,0:T(8,128)(2,1)S(1)}, bf16[2,64,512]{2,1,0:T(8,128)(2,1)S(1)}, u32[]{:S(2)}, u32[]{:S(2)}) collective-permute-start(bf16[2,64,512]{2,1,0:T(8,128)(2,1)S(1)} %fusion.14), channel_id=1, source_target_pairs={{0,12},{1,13},{2,14},{3,15},{4,8},{5,9},{6,10},{7,11},{8,4},{9,5},... | collective-permute-start | bytes 393224 | tf_op jit(solution)/shard_map/ppermute | solution.py:514
  72.0 12.0 %collective-permute-start.25 = (bf16[64,3072]{1,0:T(8,128)(2,1)S(1)}, bf16[64,3072]{1,0:T(8,128)(2,1)S(1)}, u32[]{:S(2)}, u32[]{:S(2)}) collective-permute-start(bf16[64,3072]{1,0:T(8,128)(2,1)S(1)} %get-tuple-element.49.refs_4_), channel_id=1, source_target_pairs={{0,2},{1,3},{2,0},{3,1},{4,6},{5,7},{6,4},{7,5},{8,10},{9,11},{10,... | collective-permute-start | bytes 1179656 | tf_op jit(solution)/shard_map/ppermute | solution.py:514
  73.7 18.7 %collective-permute-start.22 = (bf16[64,3072]{1,0:T(8,128)(2,1)S(1)}, bf16[64,3072]{1,0:T(8,128)(2,1)S(1)}, u32[]{:S(2)}, u32[]{:S(2)}) collective-permute-start(bf16[64,3072]{1,0:T(8,128)(2,1)S(1)} %get-tuple-element.50.refs_0_), channel_id=1, source_target_pairs={{0,2},{1,3},{2,0},{3,1},{4,6},{5,7},{6,4},{7,5},{8,10},{9,11},{10,... | collective-permute-start | bytes 1179656 | tf_op jit(solution)/shard_map/ppermute | solution.py:514
  74.1 18.9 %collective-permute-start.24 = (bf16[64,3072]{1,0:T(8,128)(2,1)S(1)}, bf16[64,3072]{1,0:T(8,128)(2,1)S(1)}, u32[]{:S(2)}, u32[]{:S(2)}) collective-permute-start(bf16[64,3072]{1,0:T(8,128)(2,1)S(1)} %get-tuple-element.49.refs_4_), channel_id=1, source_target_pairs={{0,1},{1,0},{2,3},{3,2},{4,5},{5,4},{6,7},{7,6},{8,9},{9,8},{10,11... | collective-permute-start | bytes 1179656 | tf_op jit(solution)/shard_map/ppermute | solution.py:514
  81.0 19.9 %collective-permute-start.23 = (bf16[64,3072]{1,0:T(8,128)(2,1)S(1)}, bf16[64,3072]{1,0:T(8,128)(2,1)S(1)}, u32[]{:S(2)}, u32[]{:S(2)}) collective-permute-start(bf16[64,3072]{1,0:T(8,128)(2,1)S(1)} %collective-permute-done.21.refs_1_), channel_id=1, source_target_pairs={{0,2},{1,3},{2,0},{3,1},{4,6},{5,7},{6,4},{7,5},{8,10},{9,11},{10,... | collective-permute-start | bytes 1179656 | tf_op jit(solution)/shard_map/ppermute | solution.py:514
  82.7 18.7 %collective-permute-start.12 = (bf16[4,64,512]{2,1,0:T(8,128)(2,1)S(1)}, bf16[4,64,512]{2,1,0:T(8,128)(2,1)S(1)}, u32[]{:S(2)}, u32[]{:S(2)}) collective-permute-start(bf16[4,64,512]{2,1,0:T(8,128)(2,1)S(1)} %get-tuple-element.52.refs_0_), channel_id=1, source_target_pairs={{0,1},{1,0},{2,3},{3,2},{4,5},{5,4},{6,7},{7,6},{8,9},{9,8},{10,11... | collective-permute-start | bytes 786440 | tf_op jit(solution)/shard_map/ppermute | solution.py:514
  84.0 22.6 %collective-permute-start.16 = (bf16[4,64,512]{2,1,0:T(8,128)(2,1)S(1)}, bf16[4,64,512]{2,1,0:T(8,128)(2,1)}, u32[]{:S(2)}, u32[]{:S(2)}) collective-permute-start(bf16[4,64,512]{2,1,0:T(8,128)(2,1)S(1)} %get-tuple-element.51.refs_4_), channel_id=1, source_target_pairs={{0,2},{1,3},{2,0},{3,1},{4,6},{5,7},{6,4},{7,5},{8,10},{9,11},{10,... | collective-permute-start | bytes 786440 | tf_op jit(solution)/shard_map/ppermute | solution.py:514
  92.5 14.7 %collective-permute-start.26 = (bf16[64,3072]{1,0:T(8,128)(2,1)S(1)}, bf16[64,3072]{1,0:T(8,128)(2,1)}, u32[]{:S(2)}, u32[]{:S(2)}) collective-permute-start(bf16[64,3072]{1,0:T(8,128)(2,1)S(1)} %collective-permute-done.25.refs_6_), channel_id=1, source_target_pairs={{0,1},{1,0},{2,3},{3,2},{4,5},{5,4},{6,7},{7,6},{8,9},{9,8},{10,11... | collective-permute-start | bytes 1179656 | tf_op jit(solution)/shard_map/ppermute | solution.py:514
  93.0 22.4 %collective-permute-start.13 = (bf16[4,64,512]{2,1,0:T(8,128)(2,1)S(1)}, bf16[4,64,512]{2,1,0:T(8,128)(2,1)}, u32[]{:S(2)}, u32[]{:S(2)}) collective-permute-start(bf16[4,64,512]{2,1,0:T(8,128)(2,1)S(1)} %get-tuple-element.52.refs_0_), channel_id=1, source_target_pairs={{0,2},{1,3},{2,0},{3,1},{4,6},{5,7},{6,4},{7,5},{8,10},{9,11},{10,... | collective-permute-start | bytes 786440 | tf_op jit(solution)/shard_map/ppermute | solution.py:514
  100.9 14.5 %collective-permute-start.15 = (bf16[4,64,512]{2,1,0:T(8,128)(2,1)S(1)}, bf16[4,64,512]{2,1,0:T(8,128)(2,1)}, u32[]{:S(2)}, u32[]{:S(2)}) collective-permute-start(bf16[4,64,512]{2,1,0:T(8,128)(2,1)S(1)} %get-tuple-element.51.refs_4_), channel_id=1, source_target_pairs={{0,1},{1,0},{2,3},{3,2},{4,5},{5,4},{6,7},{7,6},{8,9},{9,8},{10,11... | collective-permute-start | bytes 786440 | tf_op jit(solution)/shard_map/ppermute | solution.py:514
  101.4 14.0 %collective-permute-start.14 = (bf16[4,64,512]{2,1,0:T(8,128)(2,1)S(1)}, bf16[4,64,512]{2,1,0:T(8,128)(2,1)}, u32[]{:S(2)}, u32[]{:S(2)}) collective-permute-start(bf16[4,64,512]{2,1,0:T(8,128)(2,1)S(1)} %collective-permute-done.12.refs_1_), channel_id=1, source_target_pairs={{0,2},{1,3},{2,0},{3,1},{4,6},{5,7},{6,4},{7,5},{8,10},{9,11},{10,... | collective-permute-start | bytes 786440 | tf_op jit(solution)/shard_map/ppermute | solution.py:514
  106.6 8.8 %collective-permute-start.17 = (bf16[4,64,512]{2,1,0:T(8,128)(2,1)}, bf16[4,64,512]{2,1,0:T(8,128)(2,1)}, u32[]{:S(2)}, u32[]{:S(2)}) collective-permute-start(bf16[4,64,512]{2,1,0:T(8,128)(2,1)} %collective-permute-done.16.refs_6_), channel_id=1, source_target_pairs={{0,1},{1,0},{2,3},{3,2},{4,5},{5,4},{6,7},{7,6},{8,9},{9,8},{10,11... | collective-permute-start | bytes 786440 | tf_op jit(solution)/shard_map/ppermute | solution.py:514
  107.2 0.6 copy-start.2
  115.5 0.7 copy-start.3
  124.4 1.3 copy-start
  125.7 10.8 %collective-permute-start.27 = (f32[512,512]{1,0:T(8,128)}, f32[512,512]{1,0:T(8,128)}, u32[]{:S(2)}, u32[]{:S(2)}) collective-permute-start(f32[512,512]{1,0:T(8,128)} %get-tuple-element.36.block_ref), channel_id=1, source_target_pairs={{0,16},{16,0},{1,17},{17,1},{2,18},{18,2},{3,19},{19,3},{4,20},{20... | collective-permute-start | bytes 3145736 | tf_op jit(solution)/shard_map/ppermute | solution.py:511
  125.8 11.1 %slice-start = ((s8[10485760]{0:T(1024)(128)(4,1)}), s8[4194304]{0:T(1024)(128)(4,1)S(1)}, s32[]{:S(2)}) async-start(s8[10485760]{0:T(1024)(128)(4,1)} %bitcast.53), calls=%async_computation | async-start | bytes 8388608
  125.8 11.1 %slice-start.1 = ((s8[10485760]{0:T(1024)(128)(4,1)}), s8[4194304]{0:T(1024)(128)(4,1)S(1)}, s32[]{:S(2)}) async-start(s8[10485760]{0:T(1024)(128)(4,1)} %bitcast.53), calls=%async_computation.1 | async-start | bytes 8388608
  131.4 33.0 %collective-permute-start.8 = (bf16[2,1024,1280]{2,1,0:T(8,128)(2,1)}, bf16[2,1024,1280]{2,1,0:T(8,128)(2,1)S(1)}, u32[]{:S(2)}, u32[]{:S(2)}) collective-permute-start(bf16[2,1024,1280]{2,1,0:T(8,128)(2,1)} %constant_dynamic-slice_fusion.1), channel_id=1, source_target_pairs={{0,16},{16,0},{1,17},{17,1},{2,18},{18,2},{3,19},{19,3},{4,20},{20... | collective-permute-start | bytes 15728648 | tf_op jit(solution)/shard_map/ppermute | solution.py:511
  131.9 1.6 copy-start.1
  133.5 3.4 %slice-start.2 = ((s8[10485760]{0:T(1024)(128)(4,1)}), s8[2097152]{0:T(1024)(128)(4,1)S(1)}, s32[]{:S(2)}) async-start(s8[10485760]{0:T(1024)(128)(4,1)} %bitcast.53), calls=%async_computation.2 | async-start | bytes 4194304
  136.6 27.8 %collective-permute-start.28 = (bf16[2,1024,1024]{2,1,0:T(8,128)(2,1)S(1)}, bf16[2,1024,1024]{2,1,0:T(8,128)(2,1)S(1)}, u32[]{:S(2)}, u32[]{:S(2)}) collective-permute-start(bf16[2,1024,1024]{2,1,0:T(8,128)(2,1)S(1)} %back_solve.1.qs), channel_id=1, source_target_pairs={{0,16},{16,0},{1,17},{17,1},{2,18},{18,2},{3,19},{19,3},{4,20},{20... | collective-permute-start | bytes 12582920 | tf_op jit(solution)/shard_map/ppermute | solution.py:511

commit v4 on v3

--- a/solution.py
+++ b/solution.py
@@ -39,17 +39,20 @@
     )
 
 
-def diag_kernel(off_ref, strip_ref, high, low, square):
-    arcs, rows, _ = strip_ref.shape
-    off = pl.multiple_of(off_ref[0], 8)
+def rows_kernel(place_ref, rows_ref, out_ref, square):
+    arcs, rows, _ = rows_ref.shape
+    at = pl.multiple_of(place_ref[0], LANE)
+    off = pl.multiple_of(place_ref[1], 16)
     r = lax.broadcasted_iota(jnp.int32, (LANE, LANE), 0)
     c = lax.broadcasted_iota(jnp.int32, (LANE, LANE), 1)
     eye = r == c
     sub = lax.broadcasted_iota(jnp.int32, (rows, LANE), 1)
     own = (sub >= off) & (sub < off + rows)
-    for arc in range(arcs):
+    strips = [rows_ref[arc, :, pl.ds(at, LANE)] for arc in range(arcs)]
+    for arc in range(arcs):
+        out_ref[arc, :, LANE:] = rows_ref[arc].astype(BF16)
         square[arc] = eye.astype(F32)
-        square[arc, pl.ds(off, rows), :] = jnp.where(own, strip_ref[arc], 0.0)
+        square[arc, pl.ds(off, rows), :] = jnp.where(own, strips[arc], 0.0)
     lowers = [square[arc] for arc in range(arcs)]
     invs = [jnp.where(eye, 1.0 / jnp.where(eye, low, 1.0), 0.0) for low in lowers]
     step = 1
@@ -60,21 +63,25 @@
         step *= 2
     for arc in range(arcs):
         square[arc] = invs[arc]
-        value = jnp.where(own, square[arc, pl.ds(off, rows), :], strip_ref[arc])
-        high[arc], low[arc] = split(value)
-
-
-def invert_diag(strip, off):
-    arcs = strip.shape[0]
-    out = jax.ShapeDtypeStruct(strip.shape, BF16)
+        value = jnp.where(own, square[arc, pl.ds(off, rows), :], strips[arc])
+        high, low = split(value)
+        out_ref[arc, :, pl.ds(at + LANE, LANE)] = high
+        out_ref[arc, :, :LANE] = low
+
+
+def factor_rows(cov_factor, me):
+    arcs, rows, size = cov_factor.shape
+    at = me * rows // LANE * LANE
+    place = jnp.stack([at, me * rows - at]).astype(jnp.int32)
     return pl.pallas_call(
-        diag_kernel,
-        out_shape=(out, out),
+        rows_kernel,
+        out_shape=jax.ShapeDtypeStruct((arcs, rows, LANE + size), BF16),
         in_specs=[pl.BlockSpec(memory_space=pltpu.SMEM), pl.BlockSpec(memory_space=pltpu.VMEM)],
-        out_specs=(pl.BlockSpec(memory_space=pltpu.VMEM), pl.BlockSpec(memory_space=pltpu.VMEM)),
+        out_specs=pl.BlockSpec(memory_space=pltpu.VMEM),
         scratch_shapes=[pltpu.VMEM((arcs, LANE, LANE), F32)],
-        name="invert_diag",
-    )(off, strip)
+        compiler_params=pltpu.CompilerParams(vmem_limit_bytes=8 << 20),
+        name="factor_rows",
+    )(place, cov_factor)
 
 
 def invert_factor(rest, fine, high, low, first):
@@ -454,15 +461,6 @@
     return jnp.any(active[:, :, None] == ids[None, None, :], axis=1)
 
 
-def factor_rows(cov_factor, me):
-    rows = cov_factor.shape[1]
-    at = me * rows // LANE * LANE
-    strip = lax.dynamic_slice_in_dim(cov_factor, at, LANE, 2)
-    high, low = invert_diag(strip, (me * rows % LANE).astype(jnp.int32)[None])
-    rest = lax.dynamic_update_slice_in_dim(cov_factor.astype(BF16), high, at, 2)
-    return jnp.concatenate([low, rest], axis=2)
-
-
 def general(design, cov_factor, active_blocks, panel_index, reg_diag):
     arcs, observed, columns = design.shape
     rows = cov_factor.shape[1]
@@ -554,15 +552,21 @@
         chunk += gone
 
     lower = factor_rows(cov_factor, me)
-    stack = [lower]
-    for k in range(1, planes):
-        stack.append(hop(lower, 4 * k))
+    near = {0: lower}
+    for sign in (1, -1):
+        value = lower
+        for k in range(1, planes):
+            low, top = (k - 1, planes - 1) if sign > 0 else (1, planes - k + 1)
+            pairs = [(p, p + 4 * sign) for p in range(4 * low, 4 * top)]
+            value = lax.ppermute(value, "par", pairs)
+            near[sign * k] = value
     packed = []
     for index in range(planes):
         width = LANE + 4 * rows * (index + 1)
-        value = stack[0][:, :, :width]
-        for k in range(1, planes):
-            value = jnp.where(plane == (index ^ k), stack[k][:, :, :width], value)
+        value = lower[:, :, :width]
+        for source in range(planes):
+            if source != index:
+                value = jnp.where(plane == source, near[source - index][:, :, :width], value)
         packed.append(value)
     packed = jnp.concatenate(packed, axis=2)
     seats = (me & 3) ^ jnp.arange(4, dtype=jnp.int32)

time: 175 us -> 163 us (0.931); the launches traced: 172 us -> 162 us
  waiting for transfers between devices: 51.3 us -> 40.3 us
  starting transfers between devices: 34.1 us -> 42 us
  other arithmetic: 13.9 us -> 9.79 us
  local copies, waits for them, and re-layouts: 13.9 us -> 12 us
    ppermute x25 -> x22, waiting for transfers between devices: 51.2 us -> 39.4 us  [hop(): return lax.ppermute(value, 'par', [(p, p ^ bits) for p in range(chips)])]
    ppermute x0 -> x6, starting transfers between devices: none -> 11 us  [paired(): value = lax.ppermute(value, 'par', pairs)]
    select_n x4, other arithmetic: 3.45 us -> 0.18 us  [paired(): jnp.where(plane == source, near[source - index][:, :, :width], value)]
    ppermute x25 -> x22, starting transfers between devices: 33.3 us -> 30.1 us  [hop(): return lax.ppermute(value, 'par', [(p, p ^ bits) for p in range(chips)])]
    unnamed x22 -> x20, local copies, waits for them, and re-layouts: 4.24 us -> 4.17 us
  transfers between devices with their start and end apart: 29 -> 32, of which waited for: 11 -> 10; matrix products, arithmetic and copies ran while one was open for 9% -> 8% of each run, Pallas kernels for 22% -> 23%
where the time goes in v4:
time: 163 us; the launch traced here: 162 us
  Pallas kernels  56.5 us (35%)
  starting transfers between devices  42 us (26%)
  waiting for transfers between devices  40.3 us (25%)
  local copies, waits for them, and re-layouts  12 us (7%)
  other arithmetic  9.79 us (6%)
    ppermute x22, waiting for transfers between devices, hop(): return lax.ppermute(value, 'par', [(p, p ^ bits) for p in range(chips)])  39.4 us
    ppermute x22, starting transfers between devices, hop(): return lax.ppermute(value, 'par', [(p, p ^ bits) for p in range(chips)])  30.1 us
    pallas_call x1, Pallas kernels, chol_normals(): pl.pallas_call(chol_normals_kernel, out_shape=(jax.ShapeDtypeStruct((size...  27.4 us
    ppermute x6, starting transfers between devices, paired(): value = lax.ppermute(value, 'par', pairs)  11 us
    pallas_call x1, Pallas kernels, panel_call(): pl.pallas_call(functools.partial(panel_kernel, arcs), out_shape=(jax.Shap...  8.29 us
    pallas_call x1, Pallas kernels, invert_call(): pl.pallas_call(kernel, out_shape=(out, out), in_specs=[SM if value.dtype...  7.45 us
    pallas_call x1, Pallas kernels, normals_call(): pl.pallas_call(normals_kernel, out_shape=jax.ShapeDtypeStruct((width, sha...  7.35 us
    dynamic_slice x1, local copies, waits for them, and re-layouts, paired(): far = lax.dynamic_slice_in_dim(design, (1 - core) * share, share, 2)  5.64 us
  transfers between devices with their start and end apart: 32, of which 10 were waited for; matrix products, arithmetic and copies ran while one was open for 8% of the time, Pallas kernels for 23%

profile of v4, /device:TPU:0, one launch (start us, length us, event | category | flops | bytes accessed | tf_op | source)
XLA Modules:
  0.0 161.8 jit_solution(16388208037545250470)
XLA Ops:
  0.8 0.9 compare_reduce_fusion.1
  1.9 3.7 %bitcast_select_fusion = (bf16[512,512]{1,0:T(8,128)(2,1)S(1)}, bf16[512,512]{1,0:T(8,128)(2,1)}, bf16[512,512]{1,0:T(8,128)(2,1)}, bf16[512,512]{1,0:T(8,128)(2,1)S(1)}) fusion(bf16[2,1024,2560]{2,1,0:T(8,128)(2,1)} %own.1, s32[]{:T(128)S(6)} %select_n.167, s32[]{:T(128)S(6)} %min.4, pred[512]{0:T(512)(128)(4,1)S(1)} %broadcast_in_dim.52, ...), kind=kLoop, calls=%fused_computation.10 | loop fusion | flops 1048576 | bytes 4195348 | tf_op jit(solution)/shard_map/jit(_where)/select_n | solution.py:528
  5.7 2.9 %factor_rows.1 = bf16[2,64,1152]{2,1,0:T(8,128)(2,1)S(1)} custom-call(s32[2]{0:T(128)S(1)} %pad_add_fusion.3.place_ref, f32[2,64,1024]{2,1,0:T(8,128)S(1)} %copy-done.2), custom_call_target="tpu_custom_call" | custom-call | tf_op jit(solution)/shard_map/factor_rows/pallas_call | solution.py:76
  8.5 1.3 collective-permute-start.21
  9.8 5.6 %collective-permute-start.18 = (bf16[2,64,1152]{2,1,0:T(8,128)(2,1)S(1)}, bf16[2,64,1152]{2,1,0:T(8,128)(2,1)S(1)}, u32[]{:S(2)}, u32[]{:S(2)}) collective-permute-start(bf16[2,64,1152]{2,1,0:T(8,128)(2,1)S(1)} %factor_rows.1), channel_id=1, source_target_pairs={{0,4},{1,5},{2,6},{3,7},{4,8},{5,9},{6,10},{7,11},{8,12},{9,13},{1... | collective-permute-start | bytes 884744 | tf_op jit(solution)/shard_map/ppermute | solution.py:561
  15.5 2.0 %collective-permute-start.2 = (bf16[512,512]{1,0:T(8,128)(2,1)}, bf16[512,512]{1,0:T(8,128)(2,1)}, u32[]{:S(2)}, u32[]{:S(2)}) collective-permute-start(bf16[512,512]{1,0:T(8,128)(2,1)} %get-tuple-element.23), channel_id=1, source_target_pairs={{0,2},{1,3},{2,0},{3,1},{4,6},{5,7},{6,4},{7,5},{8,10},{9,11},{10,... | collective-permute-start | bytes 1572872 | tf_op jit(solution)/shard_map/ppermute | solution.py:512
  17.6 1.5 collective-permute-start
  20.5 0.8 dynamic_slice.74
  21.3 0.8 dynamic_slice.75
  22.4 1.3 collective-permute-start.22
  23.7 0.7 collective-permute-start.19
  24.5 5.9 %collective-permute-done.2 = bf16[512,512]{1,0:T(8,128)(2,1)} collective-permute-done((bf16[512,512]{1,0:T(8,128)(2,1)}, bf16[512,512]{1,0:T(8,128)(2,1)}, u32[]{:S(2)}, u32[]{:S(2)}) %collective-permute-start.2) | collective-permute-done | bytes 524320 | tf_op jit(solution)/shard_map/ppermute | solution.py:512
  30.4 1.0 dynamic-slice_add_fusion
  31.4 1.8 %collective-permute-start.3 = (bf16[256,512]{1,0:T(8,128)(2,1)S(1)}, bf16[256,512]{1,0:T(8,128)(2,1)S(1)}, u32[]{:S(2)}, u32[]{:S(2)}) collective-permute-start(bf16[256,512]{1,0:T(8,128)(2,1)S(1)} %dynamic-slice_add_fusion), channel_id=1, source_target_pairs={{0,1},{1,0},{2,3},{3,2},{4,5},{5,4},{6,7},{7,6},{8,9},{9,8},{10,11... | collective-permute-start | bytes 786440 | tf_op jit(solution)/shard_map/ppermute | solution.py:512
  33.3 1.6 collective-permute-start.1
  34.9 1.3 collective-permute-start.23
  36.2 0.9 collective-permute-start.20
  37.1 2.3 %collective-permute-done.3 = bf16[256,512]{1,0:T(8,128)(2,1)S(1)} collective-permute-done((bf16[256,512]{1,0:T(8,128)(2,1)S(1)}, bf16[256,512]{1,0:T(8,128)(2,1)S(1)}, u32[]{:S(2)}, u32[]{:S(2)}) %collective-permute-start.3) | collective-permute-done | bytes 262176 | tf_op jit(solution)/shard_map/ppermute | solution.py:512
  39.5 1.1 add_add_fusion
  40.8 1.1 add_add_fusion.1
  41.9 1.6 %collective-permute-start.4 = (bf16[2,64,512]{2,1,0:T(8,128)(2,1)S(1)}, bf16[2,64,512]{2,1,0:T(8,128)(2,1)S(1)}, u32[]{:S(2)}, u32[]{:S(2)}) collective-permute-start(bf16[2,64,512]{2,1,0:T(8,128)(2,1)S(1)} %get-tuple-element.49), channel_id=1, source_target_pairs={{0,4},{1,5},{2,6},{3,7},{4,0},{5,1},{6,2},{7,3},{8,12},{9,13},{10,... | collective-permute-start | bytes 393224 | tf_op jit(solution)/shard_map/ppermute | solution.py:512
  43.6 1.1 collective-permute-start.5
  44.7 1.7 %collective-permute-start.6 = (bf16[2,64,512]{2,1,0:T(8,128)(2,1)S(1)}, bf16[2,64,512]{2,1,0:T(8,128)(2,1)S(1)}, u32[]{:S(2)}, u32[]{:S(2)}) collective-permute-start(bf16[2,64,512]{2,1,0:T(8,128)(2,1)S(1)} %get-tuple-element.51), channel_id=1, source_target_pairs={{0,12},{1,13},{2,14},{3,15},{4,8},{5,9},{6,10},{7,11},{8,4},{9,5},... | collective-permute-start | bytes 393224 | tf_op jit(solution)/shard_map/ppermute | solution.py:512
  46.4 1.0 collective-permute-done.23
  47.9 2.8 %collective-permute-done.4 = bf16[2,64,512]{2,1,0:T(8,128)(2,1)S(1)} collective-permute-done((bf16[2,64,512]{2,1,0:T(8,128)(2,1)S(1)}, bf16[2,64,512]{2,1,0:T(8,128)(2,1)S(1)}, u32[]{:S(2)}, u32[]{:S(2)}) %collective-permute-start.4) | collective-permute-done | bytes 131104 | tf_op jit(solution)/shard_map/ppermute | solution.py:512
  50.7 4.4 %collective-permute-done.5 = bf16[2,64,512]{2,1,0:T(8,128)(2,1)S(1)} collective-permute-done((bf16[2,64,512]{2,1,0:T(8,128)(2,1)S(1)}, bf16[2,64,512]{2,1,0:T(8,128)(2,1)S(1)}, u32[]{:S(2)}, u32[]{:S(2)}) %collective-permute-start.5) | collective-permute-done | bytes 131104 | tf_op jit(solution)/shard_map/ppermute | solution.py:512
  55.1 2.0 %collective-permute-start.9 = (bf16[2,64,512]{2,1,0:T(8,128)(2,1)S(1)}, bf16[2,64,512]{2,1,0:T(8,128)(2,1)S(1)}, u32[]{:S(2)}, u32[]{:S(2)}) collective-permute-start(bf16[2,64,512]{2,1,0:T(8,128)(2,1)S(1)} %fusion.10), channel_id=1, source_target_pairs={{0,4},{1,5},{2,6},{3,7},{4,0},{5,1},{6,2},{7,3},{8,12},{9,13},{10,... | collective-permute-start | bytes 393224 | tf_op jit(solution)/shard_map/ppermute | solution.py:512
  57.2 1.1 collective-permute-start.10
  58.3 1.4 collective-permute-start.11
  59.7 1.6 collective-permute-start.28
  61.6 1.5 collective-permute-start.25
  63.1 6.2 %collective-permute-done.10 = bf16[2,64,512]{2,1,0:T(8,128)(2,1)S(1)} collective-permute-done((bf16[2,64,512]{2,1,0:T(8,128)(2,1)S(1)}, bf16[2,64,512]{2,1,0:T(8,128)(2,1)S(1)}, u32[]{:S(2)}, u32[]{:S(2)}) %collective-permute-start.10) | collective-permute-done | bytes 131104 | tf_op jit(solution)/shard_map/ppermute | solution.py:512
  69.2 1.5 collective-permute-start.27
  70.8 1.7 %collective-permute-start.26 = (bf16[64,3072]{1,0:T(8,128)(2,1)S(1)}, bf16[64,3072]{1,0:T(8,128)(2,1)S(1)}, u32[]{:S(2)}, u32[]{:S(2)}) collective-permute-start(bf16[64,3072]{1,0:T(8,128)(2,1)S(1)} %collective-permute-done.24.refs_1_), channel_id=1, source_target_pairs={{0,2},{1,3},{2,0},{3,1},{4,6},{5,7},{6,4},{7,5},{8,10},{9,11},{10,... | collective-permute-start | bytes 1179656 | tf_op jit(solution)/shard_map/ppermute | solution.py:512
  73.5 6.5 %collective-permute-done.25.refs_2_ = bf16[64,3072]{1,0:T(8,128)(2,1)S(1)} collective-permute-done((bf16[64,3072]{1,0:T(8,128)(2,1)S(1)}, bf16[64,3072]{1,0:T(8,128)(2,1)S(1)}, u32[]{:S(2)}, u32[]{:S(2)}) %collective-permute-start.25) | collective-permute-done | bytes 393248 | tf_op jit(solution)/shard_map/ppermute | solution.py:512
  80.1 1.4 collective-permute-start.29
  81.5 1.6 collective-permute-start.13
  83.7 10.5 %collective-permute-done.16.refs_6_ = bf16[4,64,512]{2,1,0:T(8,128)(2,1)} collective-permute-done((bf16[4,64,512]{2,1,0:T(8,128)(2,1)S(1)}, bf16[4,64,512]{2,1,0:T(8,128)(2,1)}, u32[]{:S(2)}, u32[]{:S(2)}) %collective-permute-start.16) | collective-permute-done | bytes 262176 | tf_op jit(solution)/shard_map/ppermute | solution.py:512
  94.2 1.6 collective-permute-start.14
  95.8 1.5 collective-permute-start.17
  97.9 7.5 %invert_factor.1 = (bf16[2,1024,1024]{2,1,0:T(8,128)(2,1)S(1)}, bf16[2,1024,1024]{2,1,0:T(8,128)(2,1)S(1)}) custom-call(s32[4]{0:T(128)S(1)} %copy-done.3, bf16[64,3072]{1,0:T(8,128)(2,1)S(1)} %get-tuple-element.46.refs_0_, bf16[64,3072]{1,0:T(8,128)(2,1)S(1)} %collective-permute-done.24.refs_1_, bf16[64,3072]{1,0:T(8,128)(2,1)S(1)} %collective-permute-done.25.refs_2_, ...), custom_call_target="tpu_custom_call" | custom-call | tf_op jit(solution)/shard_map/invert_factor/pallas_call | solution.py:163
  106.0 8.3 %panel_block.1 = (bf16[2,512,1024]{2,1,0:T(8,128)(2,1)S(1)}, f32[512,512]{1,0:T(8,128)}) custom-call(s32[32]{0:T(128)S(1)} %copy-done.4, bf16[4,64,512]{2,1,0:T(8,128)(2,1)S(1)} %get-tuple-element.48.refs_0_, bf16[4,64,512]{2,1,0:T(8,128)(2,1)S(1)} %collective-permute-done.12.refs_1_, bf16[4,64,512]{2,1,0:T(8,128)(2,1)} %collective-permute-done.13.refs_2_, ...), custom_call_target="tpu_custom_call" | custom-call | tf_op jit(solution)/shard_map/panel_block/pallas_call | solution.py:221
  114.3 1.3 copy-done
  115.7 5.6 %constant_dynamic-slice_fusion = bf16[2,1024,1280]{2,1,0:T(8,128)(2,1)} fusion(bf16[2,1024,2560]{2,1,0:T(8,128)(2,1)} %own.1, s32[]{:T(128)S(6)} %select_n.178), kind=kLoop, calls=%fused_computation.44 | loop fusion | bytes 10485764 | tf_op jit(solution)/shard_map/dynamic_slice | solution.py:590
  121.8 1.6 copy-done.1
  123.4 3.0 %back_solve.1.qs = bf16[2,1024,1024]{2,1,0:T(8,128)(2,1)S(1)} custom-call(bf16[2,512,1024]{2,1,0:T(8,128)(2,1)S(1)} %copy-done.1, bf16[2,1024,1024]{2,1,0:T(8,128)(2,1)S(1)} %get-tuple-element.29.refs_8_.high, bf16[2,1024,1024]{2,1,0:T(8,128)(2,1)S(1)} %get-tuple-element.30.refs_9_.low), custom_call_target="tpu_custom_call" | custom-call | tf_op jit(solution)/shard_map/back_solve/pallas_call | solution.py:237
  126.8 27.4 %chol_normals.1 = (f32[512,512]{1,0:T(8,128)S(1)}, f32[6,512,256]{2,1,0:T(8,128)S(1)}) custom-call(s32[22]{0:T(128)S(1)} %pad_add_fusion.1.info, f32[512,512]{1,0:T(8,128)} %get-tuple-element.32.block_ref, f32[512,512]{1,0:T(8,128)} %collective-permute-done.30.other_ref, f32[1,512]{1,0:T(1,128)S(1)} %bitcast.56, bf16[2,1024,2560]{2,1,0:T(8,128)(2,1)S(1)} %bitcast.55, ...), custom_call_target="tpu_custom_call" | custom-call | tf_op jit(solution)/shard_map/chol_normals/pallas_call | solution.py:421
  154.3 7.4 %normals.1 = f32[512,1280]{1,0:T(8,128)} custom-call(s32[22]{0:T(128)S(1)} %pad_add_fusion.1.info, bf16[2,1024,1280]{2,1,0:T(8,128)(2,1)S(1)} %collective-permute-done.8.far, bf16[2,1024,1024]{2,1,0:T(8,128)(2,1)S(1)} %collective-permute-done.31.qs, f32[6,512,256]{2,1,0:T(8,128)S(1)} %get-tuple-element.36.sums, f32[512,512]{1,0:T(8,128)S(1)} %get-tuple-element.37.inv_ref, ...), custom_call_target="tpu_custom_call" | custom-call | tf_op jit(solution)/shard_map/normals/pallas_call | solution.py:287
  (85 shorter events, 7.4 us)
Async XLA Ops:
  0.0 15.4 %copy-start.6 = (s32[2,80]{1,0:T(2,128)S(1)}, s32[2,80]{1,0:T(2,128)}, u32[]{:S(2)}) copy-start(s32[2,80]{1,0:T(2,128)} %param.7) | copy-start | bytes 1924
  0.0 5.7 %copy-start.2 = (f32[2,64,1024]{2,1,0:T(8,128)S(1)}, f32[2,64,1024]{2,1,0:T(8,128)}, u32[]{:S(2)}) copy-start(f32[2,64,1024]{2,1,0:T(8,128)} %rows_ref) | copy-start | bytes 1572868
  8.5 13.8 %collective-permute-start.21 = (bf16[2,64,1152]{2,1,0:T(8,128)(2,1)S(1)}, bf16[2,64,1152]{2,1,0:T(8,128)(2,1)S(1)}, u32[]{:S(2)}, u32[]{:S(2)}) collective-permute-start(bf16[2,64,1152]{2,1,0:T(8,128)(2,1)S(1)} %factor_rows.1), channel_id=1, source_target_pairs={{4,0},{5,1},{6,2},{7,3},{8,4},{9,5},{10,6},{11,7},{12,8},{13,9},{1... | collective-permute-start | bytes 884744 | tf_op jit(solution)/shard_map/ppermute | solution.py:561
  9.8 13.9 %collective-permute-start.18 = (bf16[2,64,1152]{2,1,0:T(8,128)(2,1)S(1)}, bf16[2,64,1152]{2,1,0:T(8,128)(2,1)S(1)}, u32[]{:S(2)}, u32[]{:S(2)}) collective-permute-start(bf16[2,64,1152]{2,1,0:T(8,128)(2,1)S(1)} %factor_rows.1), channel_id=1, source_target_pairs={{0,4},{1,5},{2,6},{3,7},{4,8},{5,9},{6,10},{7,11},{8,12},{9,13},{1... | collective-permute-start | bytes 884744 | tf_op jit(solution)/shard_map/ppermute | solution.py:561
  15.5 6.6 %collective-permute-start.7 = (s32[2,80]{1,0:T(2,128)S(1)}, s32[2,80]{1,0:T(2,128)S(1)}, u32[]{:S(2)}, u32[]{:S(2)}) collective-permute-start(s32[2,80]{1,0:T(2,128)S(1)} %copy-done.6), channel_id=1, source_target_pairs={{0,16},{16,0},{1,17},{17,1},{2,18},{18,2},{3,19},{19,3},{4,20},{20... | collective-permute-start | bytes 1928 | tf_op jit(solution)/shard_map/ppermute | solution.py:509
  15.5 14.9 %collective-permute-start.2 = (bf16[512,512]{1,0:T(8,128)(2,1)}, bf16[512,512]{1,0:T(8,128)(2,1)}, u32[]{:S(2)}, u32[]{:S(2)}) collective-permute-start(bf16[512,512]{1,0:T(8,128)(2,1)} %get-tuple-element.23), channel_id=1, source_target_pairs={{0,2},{1,3},{2,0},{3,1},{4,6},{5,7},{6,4},{7,5},{8,10},{9,11},{10,... | collective-permute-start | bytes 1572872 | tf_op jit(solution)/shard_map/ppermute | solution.py:512
  17.6 15.6 %collective-permute-start = (bf16[512,512]{1,0:T(8,128)(2,1)}, bf16[512,512]{1,0:T(8,128)(2,1)S(1)}, u32[]{:S(2)}, u32[]{:S(2)}) collective-permute-start(bf16[512,512]{1,0:T(8,128)(2,1)} %get-tuple-element.22), channel_id=1, source_target_pairs={{0,1},{1,0},{2,3},{3,2},{4,5},{5,4},{6,7},{7,6},{8,9},{9,8},{10,11... | collective-permute-start | bytes 1572872 | tf_op jit(solution)/shard_map/ppermute | solution.py:512
  22.4 12.5 %collective-permute-start.22 = (bf16[2,64,1152]{2,1,0:T(8,128)(2,1)S(1)}, bf16[2,64,1152]{2,1,0:T(8,128)(2,1)S(1)}, u32[]{:S(2)}, u32[]{:S(2)}) collective-permute-start(bf16[2,64,1152]{2,1,0:T(8,128)(2,1)S(1)} %collective-permute-done.21), channel_id=1, source_target_pairs={{4,0},{5,1},{6,2},{7,3},{8,4},{9,5},{10,6},{11,7},{20,16},{21,17},... | collective-permute-start | bytes 884744 | tf_op jit(solution)/shard_map/ppermute | solution.py:561
  23.7 12.5 %collective-permute-start.19 = (bf16[2,64,1152]{2,1,0:T(8,128)(2,1)S(1)}, bf16[2,64,1152]{2,1,0:T(8,128)(2,1)S(1)}, u32[]{:S(2)}, u32[]{:S(2)}) collective-permute-start(bf16[2,64,1152]{2,1,0:T(8,128)(2,1)S(1)} %collective-permute-done.18), channel_id=1, source_target_pairs={{4,8},{5,9},{6,10},{7,11},{8,12},{9,13},{10,14},{11,15},{20,24},{2... | collective-permute-start | bytes 884744 | tf_op jit(solution)/shard_map/ppermute | solution.py:561
  31.4 8.1 %collective-permute-start.3 = (bf16[256,512]{1,0:T(8,128)(2,1)S(1)}, bf16[256,512]{1,0:T(8,128)(2,1)S(1)}, u32[]{:S(2)}, u32[]{:S(2)}) collective-permute-start(bf16[256,512]{1,0:T(8,128)(2,1)S(1)} %dynamic-slice_add_fusion), channel_id=1, source_target_pairs={{0,1},{1,0},{2,3},{3,2},{4,5},{5,4},{6,7},{7,6},{8,9},{9,8},{10,11... | collective-permute-start | bytes 786440 | tf_op jit(solution)/shard_map/ppermute | solution.py:512
  33.2 3.8 %copy-start.5 = (bf16[512,512]{1,0:T(8,128)(2,1)}, bf16[512,512]{1,0:T(8,128)(2,1)S(1)}, u32[]{:S(2)}) copy-start(bf16[512,512]{1,0:T(8,128)(2,1)S(1)} %collective-permute-done) | copy-start | bytes 1572868
  33.3 7.6 %collective-permute-start.1 = (bf16[256,512]{1,0:T(8,128)(2,1)S(1)}, bf16[256,512]{1,0:T(8,128)(2,1)S(1)}, u32[]{:S(2)}, u32[]{:S(2)}) collective-permute-start(bf16[256,512]{1,0:T(8,128)(2,1)S(1)} %dynamic-slice_add_fusion.1), channel_id=1, source_target_pairs={{0,2},{1,3},{2,0},{3,1},{4,6},{5,7},{6,4},{7,5},{8,10},{9,11},{10,... | collective-permute-start | bytes 786440 | tf_op jit(solution)/shard_map/ppermute | solution.py:512
  34.9 12.5 %collective-permute-start.23 = (bf16[2,64,1152]{2,1,0:T(8,128)(2,1)S(1)}, bf16[2,64,1152]{2,1,0:T(8,128)(2,1)S(1)}, u32[]{:S(2)}, u32[]{:S(2)}) collective-permute-start(bf16[2,64,1152]{2,1,0:T(8,128)(2,1)S(1)} %collective-permute-done.22), channel_id=1, source_target_pairs={{4,0},{5,1},{6,2},{7,3},{20,16},{21,17},{22,18},{23,19}} | collective-permute-start | bytes 884744 | tf_op jit(solution)/shard_map/ppermute | solution.py:561
  36.2 11.3 %collective-permute-start.20 = (bf16[2,64,1152]{2,1,0:T(8,128)(2,1)S(1)}, bf16[2,64,1152]{2,1,0:T(8,128)(2,1)S(1)}, u32[]{:S(2)}, u32[]{:S(2)}) collective-permute-start(bf16[2,64,1152]{2,1,0:T(8,128)(2,1)S(1)} %collective-permute-done.19), channel_id=1, source_target_pairs={{8,12},{9,13},{10,14},{11,15},{24,28},{25,29},{26,30},{27,31}} | collective-permute-start | bytes 884744 | tf_op jit(solution)/shard_map/ppermute | solution.py:561
  41.9 8.8 %collective-permute-start.4 = (bf16[2,64,512]{2,1,0:T(8,128)(2,1)S(1)}, bf16[2,64,512]{2,1,0:T(8,128)(2,1)S(1)}, u32[]{:S(2)}, u32[]{:S(2)}) collective-permute-start(bf16[2,64,512]{2,1,0:T(8,128)(2,1)S(1)} %get-tuple-element.49), channel_id=1, source_target_pairs={{0,4},{1,5},{2,6},{3,7},{4,0},{5,1},{6,2},{7,3},{8,12},{9,13},{10,... | collective-permute-start | bytes 393224 | tf_op jit(solution)/shard_map/ppermute | solution.py:512
  43.6 11.5 %collective-permute-start.5 = (bf16[2,64,512]{2,1,0:T(8,128)(2,1)S(1)}, bf16[2,64,512]{2,1,0:T(8,128)(2,1)S(1)}, u32[]{:S(2)}, u32[]{:S(2)}) collective-permute-start(bf16[2,64,512]{2,1,0:T(8,128)(2,1)S(1)} %get-tuple-element.50), channel_id=1, source_target_pairs={{0,8},{1,9},{2,10},{3,11},{4,12},{5,13},{6,14},{7,15},{8,0},{9,1},... | collective-permute-start | bytes 393224 | tf_op jit(solution)/shard_map/ppermute | solution.py:512
  44.7 10.4 %collective-permute-start.6 = (bf16[2,64,512]{2,1,0:T(8,128)(2,1)S(1)}, bf16[2,64,512]{2,1,0:T(8,128)(2,1)S(1)}, u32[]{:S(2)}, u32[]{:S(2)}) collective-permute-start(bf16[2,64,512]{2,1,0:T(8,128)(2,1)S(1)} %get-tuple-element.51), channel_id=1, source_target_pairs={{0,12},{1,13},{2,14},{3,15},{4,8},{5,9},{6,10},{7,11},{8,4},{9,5},... | collective-permute-start | bytes 393224 | tf_op jit(solution)/shard_map/ppermute | solution.py:512
  47.6 23.2 %collective-permute-start.24 = (bf16[64,3072]{1,0:T(8,128)(2,1)S(1)}, bf16[64,3072]{1,0:T(8,128)(2,1)S(1)}, u32[]{:S(2)}, u32[]{:S(2)}) collective-permute-start(bf16[64,3072]{1,0:T(8,128)(2,1)S(1)} %get-tuple-element.46.refs_0_), channel_id=1, source_target_pairs={{0,1},{1,0},{2,3},{3,2},{4,5},{5,4},{6,7},{7,6},{8,9},{9,8},{10,11... | collective-permute-start | bytes 1179656 | tf_op jit(solution)/shard_map/ppermute | solution.py:512
  55.1 6.4 %collective-permute-start.9 = (bf16[2,64,512]{2,1,0:T(8,128)(2,1)S(1)}, bf16[2,64,512]{2,1,0:T(8,128)(2,1)S(1)}, u32[]{:S(2)}, u32[]{:S(2)}) collective-permute-start(bf16[2,64,512]{2,1,0:T(8,128)(2,1)S(1)} %fusion.10), channel_id=1, source_target_pairs={{0,4},{1,5},{2,6},{3,7},{4,0},{5,1},{6,2},{7,3},{8,12},{9,13},{10,... | collective-permute-start | bytes 393224 | tf_op jit(solution)/shard_map/ppermute | solution.py:512
  57.2 12.1 %collective-permute-start.10 = (bf16[2,64,512]{2,1,0:T(8,128)(2,1)S(1)}, bf16[2,64,512]{2,1,0:T(8,128)(2,1)S(1)}, u32[]{:S(2)}, u32[]{:S(2)}) collective-permute-start(bf16[2,64,512]{2,1,0:T(8,128)(2,1)S(1)} %fusion.10), channel_id=1, source_target_pairs={{0,8},{1,9},{2,10},{3,11},{4,12},{5,13},{6,14},{7,15},{8,0},{9,1},... | collective-permute-start | bytes 393224 | tf_op jit(solution)/shard_map/ppermute | solution.py:512
  58.3 12.5 %collective-permute-start.11 = (bf16[2,64,512]{2,1,0:T(8,128)(2,1)S(1)}, bf16[2,64,512]{2,1,0:T(8,128)(2,1)S(1)}, u32[]{:S(2)}, u32[]{:S(2)}) collective-permute-start(bf16[2,64,512]{2,1,0:T(8,128)(2,1)S(1)} %fusion.10), channel_id=1, source_target_pairs={{0,12},{1,13},{2,14},{3,15},{4,8},{5,9},{6,10},{7,11},{8,4},{9,5},... | collective-permute-start | bytes 393224 | tf_op jit(solution)/shard_map/ppermute | solution.py:512
  59.7 13.5 %collective-permute-start.28 = (bf16[64,3072]{1,0:T(8,128)(2,1)S(1)}, bf16[64,3072]{1,0:T(8,128)(2,1)S(1)}, u32[]{:S(2)}, u32[]{:S(2)}) collective-permute-start(bf16[64,3072]{1,0:T(8,128)(2,1)S(1)} %get-tuple-element.45.refs_4_), channel_id=1, source_target_pairs={{0,2},{1,3},{2,0},{3,1},{4,6},{5,7},{6,4},{7,5},{8,10},{9,11},{10,... | collective-permute-start | bytes 1179656 | tf_op jit(solution)/shard_map/ppermute | solution.py:512
  61.6 18.5 %collective-permute-start.25 = (bf16[64,3072]{1,0:T(8,128)(2,1)S(1)}, bf16[64,3072]{1,0:T(8,128)(2,1)S(1)}, u32[]{:S(2)}, u32[]{:S(2)}) collective-permute-start(bf16[64,3072]{1,0:T(8,128)(2,1)S(1)} %get-tuple-element.46.refs_0_), channel_id=1, source_target_pairs={{0,2},{1,3},{2,0},{3,1},{4,6},{5,7},{6,4},{7,5},{8,10},{9,11},{10,... | collective-permute-start | bytes 1179656 | tf_op jit(solution)/shard_map/ppermute | solution.py:512
  69.2 12.3 %collective-permute-start.27 = (bf16[64,3072]{1,0:T(8,128)(2,1)S(1)}, bf16[64,3072]{1,0:T(8,128)(2,1)S(1)}, u32[]{:S(2)}, u32[]{:S(2)}) collective-permute-start(bf16[64,3072]{1,0:T(8,128)(2,1)S(1)} %get-tuple-element.45.refs_4_), channel_id=1, source_target_pairs={{0,1},{1,0},{2,3},{3,2},{4,5},{5,4},{6,7},{7,6},{8,9},{9,8},{10,11... | collective-permute-start | bytes 1179656 | tf_op jit(solution)/shard_map/ppermute | solution.py:512
  70.8 25.0 %collective-permute-start.26 = (bf16[64,3072]{1,0:T(8,128)(2,1)S(1)}, bf16[64,3072]{1,0:T(8,128)(2,1)S(1)}, u32[]{:S(2)}, u32[]{:S(2)}) collective-permute-start(bf16[64,3072]{1,0:T(8,128)(2,1)S(1)} %collective-permute-done.24.refs_1_), channel_id=1, source_target_pairs={{0,2},{1,3},{2,0},{3,1},{4,6},{5,7},{6,4},{7,5},{8,10},{9,11},{10,... | collective-permute-start | bytes 1179656 | tf_op jit(solution)/shard_map/ppermute | solution.py:512
  72.5 10.6 %collective-permute-start.12 = (bf16[4,64,512]{2,1,0:T(8,128)(2,1)S(1)}, bf16[4,64,512]{2,1,0:T(8,128)(2,1)S(1)}, u32[]{:S(2)}, u32[]{:S(2)}) collective-permute-start(bf16[4,64,512]{2,1,0:T(8,128)(2,1)S(1)} %get-tuple-element.48.refs_0_), channel_id=1, source_target_pairs={{0,1},{1,0},{2,3},{3,2},{4,5},{5,4},{6,7},{7,6},{8,9},{9,8},{10,11... | collective-permute-start | bytes 786440 | tf_op jit(solution)/shard_map/ppermute | solution.py:512
  73.1 21.1 %collective-permute-start.16 = (bf16[4,64,512]{2,1,0:T(8,128)(2,1)S(1)}, bf16[4,64,512]{2,1,0:T(8,128)(2,1)}, u32[]{:S(2)}, u32[]{:S(2)}) collective-permute-start(bf16[4,64,512]{2,1,0:T(8,128)(2,1)S(1)} %get-tuple-element.47.refs_4_), channel_id=1, source_target_pairs={{0,2},{1,3},{2,0},{3,1},{4,6},{5,7},{6,4},{7,5},{8,10},{9,11},{10,... | collective-permute-start | bytes 786440 | tf_op jit(solution)/shard_map/ppermute | solution.py:512
  80.1 17.2 %collective-permute-start.29 = (bf16[64,3072]{1,0:T(8,128)(2,1)S(1)}, bf16[64,3072]{1,0:T(8,128)(2,1)}, u32[]{:S(2)}, u32[]{:S(2)}) collective-permute-start(bf16[64,3072]{1,0:T(8,128)(2,1)S(1)} %collective-permute-done.28.refs_6_), channel_id=1, source_target_pairs={{0,1},{1,0},{2,3},{3,2},{4,5},{5,4},{6,7},{7,6},{8,9},{9,8},{10,11... | collective-permute-start | bytes 1179656 | tf_op jit(solution)/shard_map/ppermute | solution.py:512
  81.5 23.9 %collective-permute-start.13 = (bf16[4,64,512]{2,1,0:T(8,128)(2,1)S(1)}, bf16[4,64,512]{2,1,0:T(8,128)(2,1)}, u32[]{:S(2)}, u32[]{:S(2)}) collective-permute-start(bf16[4,64,512]{2,1,0:T(8,128)(2,1)S(1)} %get-tuple-element.48.refs_0_), channel_id=1, source_target_pairs={{0,2},{1,3},{2,0},{3,1},{4,6},{5,7},{6,4},{7,5},{8,10},{9,11},{10,... | collective-permute-start | bytes 786440 | tf_op jit(solution)/shard_map/ppermute | solution.py:512
  83.1 22.2 %collective-permute-start.15 = (bf16[4,64,512]{2,1,0:T(8,128)(2,1)S(1)}, bf16[4,64,512]{2,1,0:T(8,128)(2,1)}, u32[]{:S(2)}, u32[]{:S(2)}) collective-permute-start(bf16[4,64,512]{2,1,0:T(8,128)(2,1)S(1)} %get-tuple-element.47.refs_4_), channel_id=1, source_target_pairs={{0,1},{1,0},{2,3},{3,2},{4,5},{5,4},{6,7},{7,6},{8,9},{9,8},{10,11... | collective-permute-start | bytes 786440 | tf_op jit(solution)/shard_map/ppermute | solution.py:512
  94.2 11.2 %collective-permute-start.14 = (bf16[4,64,512]{2,1,0:T(8,128)(2,1)S(1)}, bf16[4,64,512]{2,1,0:T(8,128)(2,1)}, u32[]{:S(2)}, u32[]{:S(2)}) collective-permute-start(bf16[4,64,512]{2,1,0:T(8,128)(2,1)S(1)} %collective-permute-done.12.refs_1_), channel_id=1, source_target_pairs={{0,2},{1,3},{2,0},{3,1},{4,6},{5,7},{6,4},{7,5},{8,10},{9,11},{10,... | collective-permute-start | bytes 786440 | tf_op jit(solution)/shard_map/ppermute | solution.py:512
  95.8 9.6 %collective-permute-start.17 = (bf16[4,64,512]{2,1,0:T(8,128)(2,1)}, bf16[4,64,512]{2,1,0:T(8,128)(2,1)}, u32[]{:S(2)}, u32[]{:S(2)}) collective-permute-start(bf16[4,64,512]{2,1,0:T(8,128)(2,1)} %collective-permute-done.16.refs_6_), channel_id=1, source_target_pairs={{0,1},{1,0},{2,3},{3,2},{4,5},{5,4},{6,7},{7,6},{8,9},{9,8},{10,11... | collective-permute-start | bytes 786440 | tf_op jit(solution)/shard_map/ppermute | solution.py:512
  97.3 0.6 copy-start.3
  105.4 0.6 copy-start.4
  114.3 1.3 copy-start
  115.7 10.8 %collective-permute-start.30 = (f32[512,512]{1,0:T(8,128)}, f32[512,512]{1,0:T(8,128)}, u32[]{:S(2)}, u32[]{:S(2)}) collective-permute-start(f32[512,512]{1,0:T(8,128)} %get-tuple-element.32.block_ref), channel_id=1, source_target_pairs={{0,16},{16,0},{1,17},{17,1},{2,18},{18,2},{3,19},{19,3},{4,20},{20... | collective-permute-start | bytes 3145736 | tf_op jit(solution)/shard_map/ppermute | solution.py:509
  115.7 11.1 %slice-start = ((s8[10485760]{0:T(1024)(128)(4,1)}), s8[4194304]{0:T(1024)(128)(4,1)S(1)}, s32[]{:S(2)}) async-start(s8[10485760]{0:T(1024)(128)(4,1)} %bitcast.54), calls=%async_computation | async-start | bytes 8388608
  115.7 11.1 %slice-start.1 = ((s8[10485760]{0:T(1024)(128)(4,1)}), s8[4194304]{0:T(1024)(128)(4,1)S(1)}, s32[]{:S(2)}) async-start(s8[10485760]{0:T(1024)(128)(4,1)} %bitcast.54), calls=%async_computation.1 | async-start | bytes 8388608
  121.3 33.0 %collective-permute-start.8 = (bf16[2,1024,1280]{2,1,0:T(8,128)(2,1)}, bf16[2,1024,1280]{2,1,0:T(8,128)(2,1)S(1)}, u32[]{:S(2)}, u32[]{:S(2)}) collective-permute-start(bf16[2,1024,1280]{2,1,0:T(8,128)(2,1)} %constant_dynamic-slice_fusion), channel_id=1, source_target_pairs={{0,16},{16,0},{1,17},{17,1},{2,18},{18,2},{3,19},{19,3},{4,20},{20... | collective-permute-start | bytes 15728648 | tf_op jit(solution)/shard_map/ppermute | solution.py:509
  121.8 1.6 copy-start.1
  123.4 3.4 %slice-start.2 = ((s8[10485760]{0:T(1024)(128)(4,1)}), s8[2097152]{0:T(1024)(128)(4,1)S(1)}, s32[]{:S(2)}) async-start(s8[10485760]{0:T(1024)(128)(4,1)} %bitcast.54), calls=%async_computation.2 | async-start | bytes 4194304
  126.5 27.8 %collective-permute-start.31 = (bf16[2,1024,1024]{2,1,0:T(8,128)(2,1)S(1)}, bf16[2,1024,1024]{2,1,0:T(8,128)(2,1)S(1)}, u32[]{:S(2)}, u32[]{:S(2)}) collective-permute-start(bf16[2,1024,1024]{2,1,0:T(8,128)(2,1)S(1)} %back_solve.1.qs), channel_id=1, source_target_pairs={{0,16},{16,0},{1,17},{17,1},{2,18},{18,2},{3,19},{19,3},{4,20},{20... | collective-permute-start | bytes 12582920 | tf_op jit(solution)/shard_map/ppermute | solution.py:509

commit v5 on v4

--- a/solution.py
+++ b/solution.py
@@ -129,18 +129,27 @@
 
 def invert_pieces_kernel(first, place_ref, *refs):
     pieces, (high, low, rest, fine) = refs[:-4], refs[-4:]
-    arcs, size, _ = high.shape
+    arcs, _, _ = high.shape
     rows = pieces[0].shape[0]
-    planes = size // (4 * rows)
-    for index, piece in enumerate(pieces):
-        arc, seat = index // 4, place_ref[index % 4]
-        left = 0
-        for plane in range(planes):
-            width = 4 * rows * (plane + 1)
-            at = pl.multiple_of((4 * plane + seat) * rows, 16)
-            fine[arc, pl.ds(at, rows), :] = piece[:, left : left + LANE]
-            rest[arc, pl.ds(at, rows), :width] = piece[:, left + LANE : left + LANE + width]
-            left += LANE + width
+
+    def unpack(outer):
+        for index, piece in enumerate(pieces):
+            arc, seat = index // 8, place_ref[index % 4]
+            left = 0
+            for plane in (0, 3) if (index // 4 % 2 == 0) == outer else (1, 2):
+                width = 4 * rows * (plane + 1)
+                at = pl.multiple_of((4 * plane + seat) * rows, 16)
+                fine[arc, pl.ds(at, rows), :] = piece[:, left : left + LANE]
+                rest[arc, pl.ds(at, rows), :width] = piece[:, left + LANE : left + LANE + width]
+                left += LANE + width
+
+    @pl.when(place_ref[4] > 0)
+    def _():
+        unpack(True)
+
+    @pl.when(place_ref[4] == 0)
+    def _():
+        unpack(False)
 
     def one(arc, _):
         invert_factor(rest.at[arc], fine.at[arc], high.at[arc], low.at[arc], first)
@@ -552,24 +561,19 @@
         chunk += gone
 
     lower = factor_rows(cov_factor, me)
-    near = {0: lower}
-    for sign in (1, -1):
-        value = lower
-        for k in range(1, planes):
-            low, top = (k - 1, planes - 1) if sign > 0 else (1, planes - k + 1)
-            pairs = [(p, p + 4 * sign) for p in range(4 * low, 4 * top)]
-            value = lax.ppermute(value, "par", pairs)
-            near[sign * k] = value
-    packed = []
-    for index in range(planes):
-        width = LANE + 4 * rows * (index + 1)
-        value = lower[:, :, :width]
-        for source in range(planes):
-            if source != index:
-                value = jnp.where(plane == source, near[source - index][:, :, :width], value)
-        packed.append(value)
-    packed = jnp.concatenate(packed, axis=2)
+    paired_rows = hop(lower, 12)
+    ends = (plane == 0) | (plane == 3)
+    above = jnp.where(plane < 2, lower, paired_rows)
+    below = jnp.where(plane < 2, paired_rows, lower)
+
+    def pack(top, bottom):
+        widths = [LANE + 4 * rows * (index + 1) for index in (top, bottom)]
+        return jnp.concatenate([above[:, :, : widths[0]], below[:, :, : widths[1]]], axis=2)
+
+    packed = jnp.where(ends, pack(0, 3), pack(1, 2))
+    others = hop(packed, 4)
     seats = (me & 3) ^ jnp.arange(4, dtype=jnp.int32)
+    seats = jnp.concatenate([seats, ends.astype(jnp.int32)[None]])
 
     first_column = me * columns + core * share
     both = jnp.concatenate([active_blocks, swap(active_blocks)], axis=0)
@@ -595,8 +599,9 @@
 
     shares = [seats]
     for arc in range(arcs):
-        pieces = spread(packed[arc], 1 + arc % 2)
-        shares += [pieces[k] for k in range(4)]
+        for value in (packed, others):
+            pieces = spread(value[arc], 1 + arc % 2)
+            shares += [pieces[k] for k in range(4)]
     factors = invert_call(
         functools.partial(invert_pieces_kernel, rows), arcs, observed, shares,
         [pltpu.VMEM((arcs, observed, observed), BF16), pltpu.VMEM((arcs, observed, LANE), BF16)],
@@ -623,6 +628,7 @@
         lax.axis_size("arc") == 2
         and design.shape[0] == 2
         and chips == 16
+        and 16 * cov_factor.shape[1] == cov_factor.shape[2]
         and columns % PANEL == 0
         and columns % (2 * BLK) == 0
         and LANE % cov_factor.shape[1] == 0

time: 163 us -> 171 us (1.049); the launches traced: 162 us -> 168 us
  local copies, waits for them, and re-layouts: 12 us -> 22 us
  waiting for transfers between devices: 40.3 us -> 37.4 us
    ppermute x6 -> x0, starting transfers between devices: 11 us -> none  [paired(): value = lax.ppermute(value, 'par', pairs)]
    ppermute x22 -> x30, starting transfers between devices: 30.1 us -> 40.6 us  [hop(): return lax.ppermute(value, 'par', [(p, p ^ bits) for p in range(chips)])]
    unnamed x20 -> x42, local copies, waits for them, and re-layouts: 4.17 us -> 14.2 us
    ppermute x22 -> x30, waiting for transfers between devices: 39.4 us -> 37.3 us  [hop(): return lax.ppermute(value, 'par', [(p, p ^ bits) for p in range(chips)])]
  transfers between devices with their start and end apart: 32 -> 34, of which waited for: 10 -> 12; matrix products, arithmetic and copies ran while one was open for 8% -> 10% of each run, Pallas kernels for 23% -> 24%
where the time goes in v5:
time: 171 us; the launch traced here: 168 us
  Pallas kernels  56 us (33%)
  starting transfers between devices  42 us (25%)
  waiting for transfers between devices  37.4 us (22%)
  local copies, waits for them, and re-layouts  22 us (13%)
  other arithmetic  9.43 us (6%)
    ppermute x30, starting transfers between devices, hop(): return lax.ppermute(value, 'par', [(p, p ^ bits) for p in range(chips)])  40.6 us
    ppermute x30, waiting for transfers between devices, hop(): return lax.ppermute(value, 'par', [(p, p ^ bits) for p in range(chips)])  37.3 us
    pallas_call x1, Pallas kernels, chol_normals(): pl.pallas_call(chol_normals_kernel, out_shape=(jax.ShapeDtypeStruct((size...  27.4 us
    unnamed x42, local copies, waits for them, and re-layouts  14.2 us
    pallas_call x1, Pallas kernels, invert_call(): pl.pallas_call(kernel, out_shape=(out, out), in_specs=[SM if value.dtype...  7.67 us
    pallas_call x1, Pallas kernels, panel_call(): pl.pallas_call(functools.partial(panel_kernel, arcs), out_shape=(jax.Shap...  7.59 us
    pallas_call x1, Pallas kernels, normals_call(): pl.pallas_call(normals_kernel, out_shape=jax.ShapeDtypeStruct((width, sha...  7.35 us
    dynamic_slice x1, local copies, waits for them, and re-layouts, paired(): far = lax.dynamic_slice_in_dim(design, (1 - core) * share, share, 2)  5.64 us
  transfers between devices with their start and end apart: 34, of which 12 were waited for; matrix products, arithmetic and copies ran while one was open for 10% of the time, Pallas kernels for 24%

profile of v5, /device:TPU:0, one launch (start us, length us, event | category | flops | bytes accessed | tf_op | source)
XLA Modules:
  0.0 168.0 jit_solution(1622972566073206052)
XLA Ops:
  1.2 0.9 compare_reduce_fusion.1
  2.3 3.5 %bitcast_select_fusion = (bf16[512,512]{1,0:T(8,128)(2,1)S(1)}, bf16[512,512]{1,0:T(8,128)(2,1)}, bf16[512,512]{1,0:T(8,128)(2,1)S(1)}, bf16[512,512]{1,0:T(8,128)(2,1)S(1)}) fusion(bf16[2,1024,2560]{2,1,0:T(8,128)(2,1)} %own.1, s32[]{:T(128)S(6)} %select_n.107, s32[]{:T(128)S(6)} %min.4, pred[512]{0:T(512)(128)(4,1)S(1)} %broadcast_in_dim.58, ...), kind=kLoop, calls=%fused_computation.9 | loop fusion | flops 1048576 | bytes 4195348 | tf_op jit(solution)/shard_map/jit(_where)/select_n | solution.py:537
  5.9 2.9 %factor_rows.1 = bf16[2,64,1152]{2,1,0:T(8,128)(2,1)S(1)} custom-call(s32[2]{0:T(128)S(1)} %pad_add_fusion.4.place_ref, f32[2,64,1024]{2,1,0:T(8,128)S(1)} %copy-done.2), custom_call_target="tpu_custom_call" | custom-call | tf_op jit(solution)/shard_map/factor_rows/pallas_call | solution.py:76
  8.8 5.0 %collective-permute-start.18 = (bf16[2,64,1152]{2,1,0:T(8,128)(2,1)S(1)}, bf16[2,64,1152]{2,1,0:T(8,128)(2,1)S(1)}, u32[]{:S(2)}, u32[]{:S(2)}) collective-permute-start(bf16[2,64,1152]{2,1,0:T(8,128)(2,1)S(1)} %factor_rows.1), channel_id=1, source_target_pairs={{0,12},{1,13},{2,14},{3,15},{4,8},{5,9},{6,10},{7,11},{8,4},{9,5},... | collective-permute-start | bytes 884744 | tf_op jit(solution)/shard_map/ppermute | solution.py:521
  13.8 1.5 collective-permute-start.2
  15.3 1.5 collective-permute-start
  19.2 2.3 %collective-permute-done.18 = bf16[2,64,1152]{2,1,0:T(8,128)(2,1)S(1)} collective-permute-done((bf16[2,64,1152]{2,1,0:T(8,128)(2,1)S(1)}, bf16[2,64,1152]{2,1,0:T(8,128)(2,1)S(1)}, u32[]{:S(2)}, u32[]{:S(2)}) %collective-permute-start.18) | collective-permute-done | bytes 294944 | tf_op jit(solution)/shard_map/ppermute | solution.py:521
  21.6 6.5 %collective-permute-done.2 = bf16[512,512]{1,0:T(8,128)(2,1)} collective-permute-done((bf16[512,512]{1,0:T(8,128)(2,1)}, bf16[512,512]{1,0:T(8,128)(2,1)}, u32[]{:S(2)}, u32[]{:S(2)}) %collective-permute-start.2) | collective-permute-done | bytes 524320 | tf_op jit(solution)/shard_map/ppermute | solution.py:521
  28.1 1.0 dynamic-slice_add_fusion
  29.1 1.6 collective-permute-start.3
  30.7 1.0 dynamic-slice_add_fusion.1
  31.7 1.6 collective-permute-start.1
  33.4 3.2 %collective-permute-done.3 = bf16[256,512]{1,0:T(8,128)(2,1)S(1)} collective-permute-done((bf16[256,512]{1,0:T(8,128)(2,1)S(1)}, bf16[256,512]{1,0:T(8,128)(2,1)S(1)}, u32[]{:S(2)}, u32[]{:S(2)}) %collective-permute-start.3) | collective-permute-done | bytes 262176 | tf_op jit(solution)/shard_map/ppermute | solution.py:521
  36.7 1.1 add_add_fusion
  37.7 1.2 collective-permute-done.1
  39.0 1.1 add_add_fusion.1
  40.2 1.2 collective-permute-start.5
  41.4 3.2 %collective-permute-start.6 = (bf16[2,64,512]{2,1,0:T(8,128)(2,1)S(1)}, bf16[2,64,512]{2,1,0:T(8,128)(2,1)S(1)}, u32[]{:S(2)}, u32[]{:S(2)}) collective-permute-start(bf16[2,64,512]{2,1,0:T(8,128)(2,1)S(1)} %get-tuple-element.51), channel_id=1, source_target_pairs={{0,12},{1,13},{2,14},{3,15},{4,8},{5,9},{6,10},{7,11},{8,4},{9,5},... | collective-permute-start | bytes 393224 | tf_op jit(solution)/shard_map/ppermute | solution.py:521
  45.2 5.0 %collective-permute-done.4 = bf16[2,64,512]{2,1,0:T(8,128)(2,1)S(1)} collective-permute-done((bf16[2,64,512]{2,1,0:T(8,128)(2,1)S(1)}, bf16[2,64,512]{2,1,0:T(8,128)(2,1)S(1)}, u32[]{:S(2)}, u32[]{:S(2)}) %collective-permute-start.4) | collective-permute-done | bytes 131104 | tf_op jit(solution)/shard_map/ppermute | solution.py:521
  50.2 3.1 %collective-permute-start.27 = (bf16[64,1536]{1,0:T(8,128)(2,1)S(1)}, bf16[64,1536]{1,0:T(8,128)(2,1)S(1)}, u32[]{:S(2)}, u32[]{:S(2)}) collective-permute-start(bf16[64,1536]{1,0:T(8,128)(2,1)S(1)} %get-tuple-element.54.refs_8_), channel_id=1, source_target_pairs={{0,2},{1,3},{2,0},{3,1},{4,6},{5,7},{6,4},{7,5},{8,10},{9,11},{10,... | collective-permute-start | bytes 589832 | tf_op jit(solution)/shard_map/ppermute | solution.py:521
  53.9 2.1 %collective-permute-start.10 = (bf16[2,64,512]{2,1,0:T(8,128)(2,1)S(1)}, bf16[2,64,512]{2,1,0:T(8,128)(2,1)S(1)}, u32[]{:S(2)}, u32[]{:S(2)}) collective-permute-start(bf16[2,64,512]{2,1,0:T(8,128)(2,1)S(1)} %fusion.6), channel_id=1, source_target_pairs={{0,8},{1,9},{2,10},{3,11},{4,12},{5,13},{6,14},{7,15},{8,0},{9,1},... | collective-permute-start | bytes 393224 | tf_op jit(solution)/shard_map/ppermute | solution.py:521
  56.0 1.8 %collective-permute-start.11 = (bf16[2,64,512]{2,1,0:T(8,128)(2,1)S(1)}, bf16[2,64,512]{2,1,0:T(8,128)(2,1)S(1)}, u32[]{:S(2)}, u32[]{:S(2)}) collective-permute-start(bf16[2,64,512]{2,1,0:T(8,128)(2,1)S(1)} %fusion.6), channel_id=1, source_target_pairs={{0,12},{1,13},{2,14},{3,15},{4,8},{5,9},{6,10},{7,11},{8,4},{9,5},... | collective-permute-start | bytes 393224 | tf_op jit(solution)/shard_map/ppermute | solution.py:521
  58.6 1.0 collective-permute-done.9
  59.9 3.3 %collective-permute-done.10 = bf16[2,64,512]{2,1,0:T(8,128)(2,1)S(1)} collective-permute-done((bf16[2,64,512]{2,1,0:T(8,128)(2,1)S(1)}, bf16[2,64,512]{2,1,0:T(8,128)(2,1)S(1)}, u32[]{:S(2)}, u32[]{:S(2)}) %collective-permute-start.10) | collective-permute-done | bytes 131104 | tf_op jit(solution)/shard_map/ppermute | solution.py:521
  63.8 1.5 collective-permute-start.23
  65.4 2.9 %collective-permute-start.30 = (bf16[64,1536]{1,0:T(8,128)(2,1)S(1)}, bf16[64,1536]{1,0:T(8,128)(2,1)}, u32[]{:S(2)}, u32[]{:S(2)}) collective-permute-start(bf16[64,1536]{1,0:T(8,128)(2,1)S(1)} %get-tuple-element.52.refs_12_), channel_id=1, source_target_pairs={{0,2},{1,3},{2,0},{3,1},{4,6},{5,7},{6,4},{7,5},{8,10},{9,11},{10,... | collective-permute-start | bytes 589832 | tf_op jit(solution)/shard_map/ppermute | solution.py:521
  71.7 2.8 %collective-permute-start.24 = (bf16[64,1536]{1,0:T(8,128)(2,1)S(1)}, bf16[64,1536]{1,0:T(8,128)(2,1)S(1)}, u32[]{:S(2)}, u32[]{:S(2)}) collective-permute-start(bf16[64,1536]{1,0:T(8,128)(2,1)S(1)} %get-tuple-element.53.refs_4_), channel_id=1, source_target_pairs={{0,2},{1,3},{2,0},{3,1},{4,6},{5,7},{6,4},{7,5},{8,10},{9,11},{10,... | collective-permute-start | bytes 589832 | tf_op jit(solution)/shard_map/ppermute | solution.py:521
  75.8 2.1 %collective-permute-start.25 = (bf16[64,1536]{1,0:T(8,128)(2,1)S(1)}, bf16[64,1536]{1,0:T(8,128)(2,1)S(1)}, u32[]{:S(2)}, u32[]{:S(2)}) collective-permute-start(bf16[64,1536]{1,0:T(8,128)(2,1)S(1)} %collective-permute-done.23.refs_5_), channel_id=1, source_target_pairs={{0,2},{1,3},{2,0},{3,1},{4,6},{5,7},{6,4},{7,5},{8,10},{9,11},{10,... | collective-permute-start | bytes 589832 | tf_op jit(solution)/shard_map/ppermute | solution.py:521
  78.6 5.2 %collective-permute-done.24.refs_6_ = bf16[64,1536]{1,0:T(8,128)(2,1)S(1)} collective-permute-done((bf16[64,1536]{1,0:T(8,128)(2,1)S(1)}, bf16[64,1536]{1,0:T(8,128)(2,1)S(1)}, u32[]{:S(2)}, u32[]{:S(2)}) %collective-permute-start.24) | collective-permute-done | bytes 196640 | tf_op jit(solution)/shard_map/ppermute | solution.py:521
  84.6 2.0 %collective-permute-start.13 = (bf16[4,64,512]{2,1,0:T(8,128)(2,1)S(1)}, bf16[4,64,512]{2,1,0:T(8,128)(2,1)S(1)}, u32[]{:S(2)}, u32[]{:S(2)}) collective-permute-start(bf16[4,64,512]{2,1,0:T(8,128)(2,1)S(1)} %get-tuple-element.48.refs_0_), channel_id=1, source_target_pairs={{0,2},{1,3},{2,0},{3,1},{4,6},{5,7},{6,4},{7,5},{8,10},{9,11},{10,... | collective-permute-start | bytes 786440 | tf_op jit(solution)/shard_map/ppermute | solution.py:521
  88.5 0.8 collective-permute-start.17
  90.1 1.2 collective-permute-start.31
  91.3 7.4 %collective-permute-done.31.refs_15_ = bf16[64,1536]{1,0:T(8,128)(2,1)} collective-permute-done((bf16[64,1536]{1,0:T(8,128)(2,1)}, bf16[64,1536]{1,0:T(8,128)(2,1)}, u32[]{:S(2)}, u32[]{:S(2)}) %collective-permute-start.31) | collective-permute-done | bytes 196640 | tf_op jit(solution)/shard_map/ppermute | solution.py:521
  98.7 0.9 copy-done.4
  99.6 0.9 copy-done.6
  100.5 0.9 copy-done.8
  101.4 0.9 copy-done.10
  102.4 0.9 copy-done.12
  103.3 0.9 copy-done.14
  104.2 0.9 copy-done.16
  105.2 7.7 %invert_factor.1 = (bf16[2,1024,1024]{2,1,0:T(8,128)(2,1)S(1)}, bf16[2,1024,1024]{2,1,0:T(8,128)(2,1)S(1)}) custom-call(s32[5]{0:T(128)S(1)} %pad_add_fusion.1.place_ref, bf16[64,1536]{1,0:T(8,128)(2,1)S(1)} %get-tuple-element.55.refs_0_, bf16[64,1536]{1,0:T(8,128)(2,1)S(1)} %collective-permute-done.19.refs_1_, ...), custom_call_target="tpu_custom_call" | custom-call | tf_op jit(solution)/shard_map/invert_factor/pallas_call | solution.py:172
  112.9 7.6 %panel_block.1 = (bf16[2,512,1024]{2,1,0:T(8,128)(2,1)S(1)}, f32[512,512]{1,0:T(8,128)}) custom-call(s32[32]{0:T(128)S(1)} %pad_add_fusion.3.place_ref, bf16[4,64,512]{2,1,0:T(8,128)(2,1)S(1)} %get-tuple-element.48.refs_0_, bf16[4,64,512]{2,1,0:T(8,128)(2,1)S(1)} %collective-permute-done.12.refs_1_, bf16[4,64,512]{2,1,0:T(8,128)(2,1)S(1)} %collective-permute-done.13.refs_2_, ...), custom_call_target="tpu_custom_call" | custom-call | tf_op jit(solution)/shard_map/panel_block/pallas_call | solution.py:230
  120.5 1.3 copy-done
  121.8 5.6 %constant_dynamic-slice_fusion = bf16[2,1024,1280]{2,1,0:T(8,128)(2,1)} fusion(bf16[2,1024,2560]{2,1,0:T(8,128)(2,1)} %own.1, s32[]{:T(128)S(6)} %select_n.118), kind=kLoop, calls=%fused_computation.38 | loop fusion | bytes 10485764 | tf_op jit(solution)/shard_map/dynamic_slice | solution.py:594
  127.9 1.6 copy-done.1
  129.5 3.0 %back_solve.1.qs = bf16[2,1024,1024]{2,1,0:T(8,128)(2,1)S(1)} custom-call(bf16[2,512,1024]{2,1,0:T(8,128)(2,1)S(1)} %copy-done.1, bf16[2,1024,1024]{2,1,0:T(8,128)(2,1)S(1)} %get-tuple-element.29.refs_8_.high, bf16[2,1024,1024]{2,1,0:T(8,128)(2,1)S(1)} %get-tuple-element.30.refs_9_.low), custom_call_target="tpu_custom_call" | custom-call | tf_op jit(solution)/shard_map/back_solve/pallas_call | solution.py:246
  132.9 27.4 %chol_normals.1 = (f32[512,512]{1,0:T(8,128)S(1)}, f32[6,512,256]{2,1,0:T(8,128)S(1)}) custom-call(s32[22]{0:T(128)S(1)} %pad_add_fusion.2.info, f32[512,512]{1,0:T(8,128)} %get-tuple-element.32.block_ref, f32[512,512]{1,0:T(8,128)} %collective-permute-done.32.other_ref, f32[1,512]{1,0:T(1,128)S(1)} %bitcast.61, bf16[2,1024,2560]{2,1,0:T(8,128)(2,1)S(1)} %bitcast.60, ...), custom_call_target="tpu_custom_call" | custom-call | tf_op jit(solution)/shard_map/chol_normals/pallas_call | solution.py:430
  160.4 7.4 %normals.1 = f32[512,1280]{1,0:T(8,128)} custom-call(s32[22]{0:T(128)S(1)} %pad_add_fusion.2.info, bf16[2,1024,1280]{2,1,0:T(8,128)(2,1)S(1)} %collective-permute-done.8.far, bf16[2,1024,1024]{2,1,0:T(8,128)(2,1)S(1)} %collective-permute-done.33.qs, f32[6,512,256]{2,1,0:T(8,128)S(1)} %get-tuple-element.36.sums, f32[512,512]{1,0:T(8,128)S(1)} %get-tuple-element.37.inv_ref, ...), custom_call_target="tpu_custom_call" | custom-call | tf_op jit(solution)/shard_map/normals/pallas_call | solution.py:296
  (113 shorter events, 16.1 us)
Async XLA Ops:
  0.0 18.8 %copy-start.17 = (s32[2,80]{1,0:T(2,128)S(1)}, s32[2,80]{1,0:T(2,128)}, u32[]{:S(2)}) copy-start(s32[2,80]{1,0:T(2,128)} %param.7) | copy-start | bytes 1924
  0.0 5.9 %copy-start.2 = (f32[2,64,1024]{2,1,0:T(8,128)S(1)}, f32[2,64,1024]{2,1,0:T(8,128)}, u32[]{:S(2)}) copy-start(f32[2,64,1024]{2,1,0:T(8,128)} %rows_ref) | copy-start | bytes 1572868
  0.0 18.8 %collective-permute-start.7 = (s32[2,80]{1,0:T(2,128)}, s32[2,80]{1,0:T(2,128)S(1)}, u32[]{:S(2)}, u32[]{:S(2)}) collective-permute-start(s32[2,80]{1,0:T(2,128)} %param.7), channel_id=1, source_target_pairs={{0,16},{16,0},{1,17},{17,1},{2,18},{18,2},{3,19},{19,3},{4,20},{20... | collective-permute-start | bytes 1928 | tf_op jit(solution)/shard_map/ppermute | solution.py:518
  8.8 12.7 %collective-permute-start.18 = (bf16[2,64,1152]{2,1,0:T(8,128)(2,1)S(1)}, bf16[2,64,1152]{2,1,0:T(8,128)(2,1)S(1)}, u32[]{:S(2)}, u32[]{:S(2)}) collective-permute-start(bf16[2,64,1152]{2,1,0:T(8,128)(2,1)S(1)} %factor_rows.1), channel_id=1, source_target_pairs={{0,12},{1,13},{2,14},{3,15},{4,8},{5,9},{6,10},{7,11},{8,4},{9,5},... | collective-permute-start | bytes 884744 | tf_op jit(solution)/shard_map/ppermute | solution.py:521
  13.8 14.3 %collective-permute-start.2 = (bf16[512,512]{1,0:T(8,128)(2,1)}, bf16[512,512]{1,0:T(8,128)(2,1)}, u32[]{:S(2)}, u32[]{:S(2)}) collective-permute-start(bf16[512,512]{1,0:T(8,128)(2,1)} %get-tuple-element.23), channel_id=1, source_target_pairs={{0,2},{1,3},{2,0},{3,1},{4,6},{5,7},{6,4},{7,5},{8,10},{9,11},{10,... | collective-permute-start | bytes 1572872 | tf_op jit(solution)/shard_map/ppermute | solution.py:521
  15.3 15.4 %collective-permute-start = (bf16[512,512]{1,0:T(8,128)(2,1)S(1)}, bf16[512,512]{1,0:T(8,128)(2,1)}, u32[]{:S(2)}, u32[]{:S(2)}) collective-permute-start(bf16[512,512]{1,0:T(8,128)(2,1)S(1)} %get-tuple-element.22), channel_id=1, source_target_pairs={{0,1},{1,0},{2,3},{3,2},{4,5},{5,4},{6,7},{7,6},{8,9},{9,8},{10,11... | collective-permute-start | bytes 1572872 | tf_op jit(solution)/shard_map/ppermute | solution.py:521
  29.1 7.6 %collective-permute-start.3 = (bf16[256,512]{1,0:T(8,128)(2,1)S(1)}, bf16[256,512]{1,0:T(8,128)(2,1)S(1)}, u32[]{:S(2)}, u32[]{:S(2)}) collective-permute-start(bf16[256,512]{1,0:T(8,128)(2,1)S(1)} %dynamic-slice_add_fusion), channel_id=1, source_target_pairs={{0,1},{1,0},{2,3},{3,2},{4,5},{5,4},{6,7},{7,6},{8,9},{9,8},{10,11... | collective-permute-start | bytes 786440 | tf_op jit(solution)/shard_map/ppermute | solution.py:521
  31.7 7.3 %collective-permute-start.1 = (bf16[256,512]{1,0:T(8,128)(2,1)S(1)}, bf16[256,512]{1,0:T(8,128)(2,1)S(1)}, u32[]{:S(2)}, u32[]{:S(2)}) collective-permute-start(bf16[256,512]{1,0:T(8,128)(2,1)S(1)} %dynamic-slice_add_fusion.1), channel_id=1, source_target_pairs={{0,2},{1,3},{2,0},{3,1},{4,6},{5,7},{6,4},{7,5},{8,10},{9,11},{10,... | collective-permute-start | bytes 786440 | tf_op jit(solution)/shard_map/ppermute | solution.py:521
  33.4 22.7 %collective-permute-start.22 = (bf16[2,64,1536]{2,1,0:T(8,128)(2,1)S(1)}, bf16[2,64,1536]{2,1,0:T(8,128)(2,1)S(1)}, u32[]{:S(2)}, u32[]{:S(2)}) collective-permute-start(bf16[2,64,1536]{2,1,0:T(8,128)(2,1)S(1)} %maximum_select_fusion), channel_id=1, source_target_pairs={{0,4},{1,5},{2,6},{3,7},{4,0},{5,1},{6,2},{7,3},{8,12},{9,13},{10,... | collective-permute-start | bytes 1179656 | tf_op jit(solution)/shard_map/ppermute | solution.py:521
  40.1 10.1 %collective-permute-start.4 = (bf16[2,64,512]{2,1,0:T(8,128)(2,1)S(1)}, bf16[2,64,512]{2,1,0:T(8,128)(2,1)S(1)}, u32[]{:S(2)}, u32[]{:S(2)}) collective-permute-start(bf16[2,64,512]{2,1,0:T(8,128)(2,1)S(1)} %get-tuple-element.49), channel_id=1, source_target_pairs={{0,4},{1,5},{2,6},{3,7},{4,0},{5,1},{6,2},{7,3},{8,12},{9,13},{10,... | collective-permute-start | bytes 393224 | tf_op jit(solution)/shard_map/ppermute | solution.py:521
  40.2 10.0 %collective-permute-start.5 = (bf16[2,64,512]{2,1,0:T(8,128)(2,1)S(1)}, bf16[2,64,512]{2,1,0:T(8,128)(2,1)S(1)}, u32[]{:S(2)}, u32[]{:S(2)}) collective-permute-start(bf16[2,64,512]{2,1,0:T(8,128)(2,1)S(1)} %get-tuple-element.50), channel_id=1, source_target_pairs={{0,8},{1,9},{2,10},{3,11},{4,12},{5,13},{6,14},{7,15},{8,0},{9,1},... | collective-permute-start | bytes 393224 | tf_op jit(solution)/shard_map/ppermute | solution.py:521
  41.4 11.9 %collective-permute-start.6 = (bf16[2,64,512]{2,1,0:T(8,128)(2,1)S(1)}, bf16[2,64,512]{2,1,0:T(8,128)(2,1)S(1)}, u32[]{:S(2)}, u32[]{:S(2)}) collective-permute-start(bf16[2,64,512]{2,1,0:T(8,128)(2,1)S(1)} %get-tuple-element.51), channel_id=1, source_target_pairs={{0,12},{1,13},{2,14},{3,15},{4,8},{5,9},{6,10},{7,11},{8,4},{9,5},... | collective-permute-start | bytes 393224 | tf_op jit(solution)/shard_map/ppermute | solution.py:521
  44.6 9.3 %collective-permute-start.19 = (bf16[64,1536]{1,0:T(8,128)(2,1)S(1)}, bf16[64,1536]{1,0:T(8,128)(2,1)S(1)}, u32[]{:S(2)}, u32[]{:S(2)}) collective-permute-start(bf16[64,1536]{1,0:T(8,128)(2,1)S(1)} %get-tuple-element.55.refs_0_), channel_id=1, source_target_pairs={{0,1},{1,0},{2,3},{3,2},{4,5},{5,4},{6,7},{7,6},{8,9},{9,8},{10,11... | collective-permute-start | bytes 589832 | tf_op jit(solution)/shard_map/ppermute | solution.py:521
  50.2 15.2 %collective-permute-start.20 = (bf16[64,1536]{1,0:T(8,128)(2,1)S(1)}, bf16[64,1536]{1,0:T(8,128)(2,1)S(1)}, u32[]{:S(2)}, u32[]{:S(2)}) collective-permute-start(bf16[64,1536]{1,0:T(8,128)(2,1)S(1)} %get-tuple-element.55.refs_0_), channel_id=1, source_target_pairs={{0,2},{1,3},{2,0},{3,1},{4,6},{5,7},{6,4},{7,5},{8,10},{9,11},{10,... | collective-permute-start | bytes 589832 | tf_op jit(solution)/shard_map/ppermute | solution.py:521
  50.2 8.1 %collective-permute-start.27 = (bf16[64,1536]{1,0:T(8,128)(2,1)S(1)}, bf16[64,1536]{1,0:T(8,128)(2,1)S(1)}, u32[]{:S(2)}, u32[]{:S(2)}) collective-permute-start(bf16[64,1536]{1,0:T(8,128)(2,1)S(1)} %get-tuple-element.54.refs_8_), channel_id=1, source_target_pairs={{0,2},{1,3},{2,0},{3,1},{4,6},{5,7},{6,4},{7,5},{8,10},{9,11},{10,... | collective-permute-start | bytes 589832 | tf_op jit(solution)/shard_map/ppermute | solution.py:521
  53.3 6.3 %collective-permute-start.9 = (bf16[2,64,512]{2,1,0:T(8,128)(2,1)S(1)}, bf16[2,64,512]{2,1,0:T(8,128)(2,1)S(1)}, u32[]{:S(2)}, u32[]{:S(2)}) collective-permute-start(bf16[2,64,512]{2,1,0:T(8,128)(2,1)S(1)} %fusion.6), channel_id=1, source_target_pairs={{0,4},{1,5},{2,6},{3,7},{4,0},{5,1},{6,2},{7,3},{8,12},{9,13},{10,... | collective-permute-start | bytes 393224 | tf_op jit(solution)/shard_map/ppermute | solution.py:521
  53.9 9.4 %collective-permute-start.10 = (bf16[2,64,512]{2,1,0:T(8,128)(2,1)S(1)}, bf16[2,64,512]{2,1,0:T(8,128)(2,1)S(1)}, u32[]{:S(2)}, u32[]{:S(2)}) collective-permute-start(bf16[2,64,512]{2,1,0:T(8,128)(2,1)S(1)} %fusion.6), channel_id=1, source_target_pairs={{0,8},{1,9},{2,10},{3,11},{4,12},{5,13},{6,14},{7,15},{8,0},{9,1},... | collective-permute-start | bytes 393224 | tf_op jit(solution)/shard_map/ppermute | solution.py:521
  56.0 7.8 %collective-permute-start.11 = (bf16[2,64,512]{2,1,0:T(8,128)(2,1)S(1)}, bf16[2,64,512]{2,1,0:T(8,128)(2,1)S(1)}, u32[]{:S(2)}, u32[]{:S(2)}) collective-permute-start(bf16[2,64,512]{2,1,0:T(8,128)(2,1)S(1)} %fusion.6), channel_id=1, source_target_pairs={{0,12},{1,13},{2,14},{3,15},{4,8},{5,9},{6,10},{7,11},{8,4},{9,5},... | collective-permute-start | bytes 393224 | tf_op jit(solution)/shard_map/ppermute | solution.py:521
  58.3 10.0 %collective-permute-start.26 = (bf16[64,1536]{1,0:T(8,128)(2,1)S(1)}, bf16[64,1536]{1,0:T(8,128)(2,1)S(1)}, u32[]{:S(2)}, u32[]{:S(2)}) collective-permute-start(bf16[64,1536]{1,0:T(8,128)(2,1)S(1)} %get-tuple-element.54.refs_8_), channel_id=1, source_target_pairs={{0,1},{1,0},{2,3},{3,2},{4,5},{5,4},{6,7},{7,6},{8,9},{9,8},{10,11... | collective-permute-start | bytes 589832 | tf_op jit(solution)/shard_map/ppermute | solution.py:521
  59.6 9.9 %collective-permute-start.21 = (bf16[64,1536]{1,0:T(8,128)(2,1)S(1)}, bf16[64,1536]{1,0:T(8,128)(2,1)S(1)}, u32[]{:S(2)}, u32[]{:S(2)}) collective-permute-start(bf16[64,1536]{1,0:T(8,128)(2,1)S(1)} %collective-permute-done.19.refs_1_), channel_id=1, source_target_pairs={{0,2},{1,3},{2,0},{3,1},{4,6},{5,7},{6,4},{7,5},{8,10},{9,11},{10,... | collective-permute-start | bytes 589832 | tf_op jit(solution)/shard_map/ppermute | solution.py:521
  63.3 7.8 %collective-permute-start.28 = (bf16[64,1536]{1,0:T(8,128)(2,1)S(1)}, bf16[64,1536]{1,0:T(8,128)(2,1)S(1)}, u32[]{:S(2)}, u32[]{:S(2)}) collective-permute-start(bf16[64,1536]{1,0:T(8,128)(2,1)S(1)} %collective-permute-done.27.refs_10_), channel_id=1, source_target_pairs={{0,1},{1,0},{2,3},{3,2},{4,5},{5,4},{6,7},{7,6},{8,9},{9,8},{10,11... | collective-permute-start | bytes 589832 | tf_op jit(solution)/shard_map/ppermute | solution.py:521
  63.8 11.4 %collective-permute-start.23 = (bf16[64,1536]{1,0:T(8,128)(2,1)S(1)}, bf16[64,1536]{1,0:T(8,128)(2,1)S(1)}, u32[]{:S(2)}, u32[]{:S(2)}) collective-permute-start(bf16[64,1536]{1,0:T(8,128)(2,1)S(1)} %get-tuple-element.53.refs_4_), channel_id=1, source_target_pairs={{0,1},{1,0},{2,3},{3,2},{4,5},{5,4},{6,7},{7,6},{8,9},{9,8},{10,11... | collective-permute-start | bytes 589832 | tf_op jit(solution)/shard_map/ppermute | solution.py:521
  65.4 10.4 %collective-permute-start.30 = (bf16[64,1536]{1,0:T(8,128)(2,1)S(1)}, bf16[64,1536]{1,0:T(8,128)(2,1)}, u32[]{:S(2)}, u32[]{:S(2)}) collective-permute-start(bf16[64,1536]{1,0:T(8,128)(2,1)S(1)} %get-tuple-element.52.refs_12_), channel_id=1, source_target_pairs={{0,2},{1,3},{2,0},{3,1},{4,6},{5,7},{6,4},{7,5},{8,10},{9,11},{10,... | collective-permute-start | bytes 589832 | tf_op jit(solution)/shard_map/ppermute | solution.py:521
  69.0 18.7 %collective-permute-start.12 = (bf16[4,64,512]{2,1,0:T(8,128)(2,1)S(1)}, bf16[4,64,512]{2,1,0:T(8,128)(2,1)S(1)}, u32[]{:S(2)}, u32[]{:S(2)}) collective-permute-start(bf16[4,64,512]{2,1,0:T(8,128)(2,1)S(1)} %get-tuple-element.48.refs_0_), channel_id=1, source_target_pairs={{0,1},{1,0},{2,3},{3,2},{4,5},{5,4},{6,7},{7,6},{8,9},{9,8},{10,11... | collective-permute-start | bytes 786440 | tf_op jit(solution)/shard_map/ppermute | solution.py:521
  70.2 18.3 %collective-permute-start.16 = (bf16[4,64,512]{2,1,0:T(8,128)(2,1)S(1)}, bf16[4,64,512]{2,1,0:T(8,128)(2,1)S(1)}, u32[]{:S(2)}, u32[]{:S(2)}) collective-permute-start(bf16[4,64,512]{2,1,0:T(8,128)(2,1)S(1)} %get-tuple-element.47.refs_4_), channel_id=1, source_target_pairs={{0,2},{1,3},{2,0},{3,1},{4,6},{5,7},{6,4},{7,5},{8,10},{9,11},{10,... | collective-permute-start | bytes 786440 | tf_op jit(solution)/shard_map/ppermute | solution.py:521
  71.7 12.1 %collective-permute-start.24 = (bf16[64,1536]{1,0:T(8,128)(2,1)S(1)}, bf16[64,1536]{1,0:T(8,128)(2,1)S(1)}, u32[]{:S(2)}, u32[]{:S(2)}) collective-permute-start(bf16[64,1536]{1,0:T(8,128)(2,1)S(1)} %get-tuple-element.53.refs_4_), channel_id=1, source_target_pairs={{0,2},{1,3},{2,0},{3,1},{4,6},{5,7},{6,4},{7,5},{8,10},{9,11},{10,... | collective-permute-start | bytes 589832 | tf_op jit(solution)/shard_map/ppermute | solution.py:521
  75.3 11.3 %collective-permute-start.29 = (bf16[64,1536]{1,0:T(8,128)(2,1)S(1)}, bf16[64,1536]{1,0:T(8,128)(2,1)S(1)}, u32[]{:S(2)}, u32[]{:S(2)}) collective-permute-start(bf16[64,1536]{1,0:T(8,128)(2,1)S(1)} %get-tuple-element.52.refs_12_), channel_id=1, source_target_pairs={{0,1},{1,0},{2,3},{3,2},{4,5},{5,4},{6,7},{7,6},{8,9},{9,8},{10,11... | collective-permute-start | bytes 589832 | tf_op jit(solution)/shard_map/ppermute | solution.py:521
  75.8 13.6 %collective-permute-start.25 = (bf16[64,1536]{1,0:T(8,128)(2,1)S(1)}, bf16[64,1536]{1,0:T(8,128)(2,1)S(1)}, u32[]{:S(2)}, u32[]{:S(2)}) collective-permute-start(bf16[64,1536]{1,0:T(8,128)(2,1)S(1)} %collective-permute-done.23.refs_5_), channel_id=1, source_target_pairs={{0,2},{1,3},{2,0},{3,1},{4,6},{5,7},{6,4},{7,5},{8,10},{9,11},{10,... | collective-permute-start | bytes 589832 | tf_op jit(solution)/shard_map/ppermute | solution.py:521
  84.6 28.3 %collective-permute-start.13 = (bf16[4,64,512]{2,1,0:T(8,128)(2,1)S(1)}, bf16[4,64,512]{2,1,0:T(8,128)(2,1)S(1)}, u32[]{:S(2)}, u32[]{:S(2)}) collective-permute-start(bf16[4,64,512]{2,1,0:T(8,128)(2,1)S(1)} %get-tuple-element.48.refs_0_), channel_id=1, source_target_pairs={{0,2},{1,3},{2,0},{3,1},{4,6},{5,7},{6,4},{7,5},{8,10},{9,11},{10,... | collective-permute-start | bytes 786440 | tf_op jit(solution)/shard_map/ppermute | solution.py:521
  87.3 25.6 %collective-permute-start.15 = (bf16[4,64,512]{2,1,0:T(8,128)(2,1)S(1)}, bf16[4,64,512]{2,1,0:T(8,128)(2,1)S(1)}, u32[]{:S(2)}, u32[]{:S(2)}) collective-permute-start(bf16[4,64,512]{2,1,0:T(8,128)(2,1)S(1)} %get-tuple-element.47.refs_4_), channel_id=1, source_target_pairs={{0,1},{1,0},{2,3},{3,2},{4,5},{5,4},{6,7},{7,6},{8,9},{9,8},{10,11... | collective-permute-start | bytes 786440 | tf_op jit(solution)/shard_map/ppermute | solution.py:521
  87.8 25.1 %collective-permute-start.14 = (bf16[4,64,512]{2,1,0:T(8,128)(2,1)S(1)}, bf16[4,64,512]{2,1,0:T(8,128)(2,1)S(1)}, u32[]{:S(2)}, u32[]{:S(2)}) collective-permute-start(bf16[4,64,512]{2,1,0:T(8,128)(2,1)S(1)} %collective-permute-done.12.refs_1_), channel_id=1, source_target_pairs={{0,2},{1,3},{2,0},{3,1},{4,6},{5,7},{6,4},{7,5},{8,10},{9,11},{10,... | collective-permute-start | bytes 786440 | tf_op jit(solution)/shard_map/ppermute | solution.py:521
  88.5 24.3 %collective-permute-start.17 = (bf16[4,64,512]{2,1,0:T(8,128)(2,1)S(1)}, bf16[4,64,512]{2,1,0:T(8,128)(2,1)S(1)}, u32[]{:S(2)}, u32[]{:S(2)}) collective-permute-start(bf16[4,64,512]{2,1,0:T(8,128)(2,1)S(1)} %collective-permute-done.16.refs_6_), channel_id=1, source_target_pairs={{0,1},{1,0},{2,3},{3,2},{4,5},{5,4},{6,7},{7,6},{8,9},{9,8},{10,11... | collective-permute-start | bytes 786440 | tf_op jit(solution)/shard_map/ppermute | solution.py:521
  90.1 8.6 %collective-permute-start.31 = (bf16[64,1536]{1,0:T(8,128)(2,1)}, bf16[64,1536]{1,0:T(8,128)(2,1)}, u32[]{:S(2)}, u32[]{:S(2)}) collective-permute-start(bf16[64,1536]{1,0:T(8,128)(2,1)} %collective-permute-done.30.refs_14_), channel_id=1, source_target_pairs={{0,1},{1,0},{2,3},{3,2},{4,5},{5,4},{6,7},{7,6},{8,9},{9,8},{10,11... | collective-permute-start | bytes 589832 | tf_op jit(solution)/shard_map/ppermute | solution.py:521
  98.7 0.9 copy-start.4
  99.6 0.9 copy-start.6
  100.5 0.9 copy-start.8
  101.4 0.9 copy-start.10
  102.4 0.9 copy-start.12
  103.3 0.9 copy-start.14
  104.2 0.9 copy-start.16
  120.5 1.3 copy-start
  121.8 10.8 %collective-permute-start.32 = (f32[512,512]{1,0:T(8,128)}, f32[512,512]{1,0:T(8,128)}, u32[]{:S(2)}, u32[]{:S(2)}) collective-permute-start(f32[512,512]{1,0:T(8,128)} %get-tuple-element.32.block_ref), channel_id=1, source_target_pairs={{0,16},{16,0},{1,17},{17,1},{2,18},{18,2},{3,19},{19,3},{4,20},{20... | collective-permute-start | bytes 3145736 | tf_op jit(solution)/shard_map/ppermute | solution.py:518
  121.8 11.1 %slice-start = ((s8[10485760]{0:T(1024)(128)(4,1)}), s8[4194304]{0:T(1024)(128)(4,1)S(1)}, s32[]{:S(2)}) async-start(s8[10485760]{0:T(1024)(128)(4,1)} %bitcast.59), calls=%async_computation | async-start | bytes 8388608
  121.8 11.1 %slice-start.1 = ((s8[10485760]{0:T(1024)(128)(4,1)}), s8[4194304]{0:T(1024)(128)(4,1)S(1)}, s32[]{:S(2)}) async-start(s8[10485760]{0:T(1024)(128)(4,1)} %bitcast.59), calls=%async_computation.1 | async-start | bytes 8388608
  127.4 33.0 %collective-permute-start.8 = (bf16[2,1024,1280]{2,1,0:T(8,128)(2,1)}, bf16[2,1024,1280]{2,1,0:T(8,128)(2,1)S(1)}, u32[]{:S(2)}, u32[]{:S(2)}) collective-permute-start(bf16[2,1024,1280]{2,1,0:T(8,128)(2,1)} %constant_dynamic-slice_fusion), channel_id=1, source_target_pairs={{0,16},{16,0},{1,17},{17,1},{2,18},{18,2},{3,19},{19,3},{4,20},{20... | collective-permute-start | bytes 15728648 | tf_op jit(solution)/shard_map/ppermute | solution.py:518
  127.9 1.6 copy-start.1
  129.5 3.4 %slice-start.2 = ((s8[10485760]{0:T(1024)(128)(4,1)}), s8[2097152]{0:T(1024)(128)(4,1)S(1)}, s32[]{:S(2)}) async-start(s8[10485760]{0:T(1024)(128)(4,1)} %bitcast.59), calls=%async_computation.2 | async-start | bytes 4194304
  132.6 27.8 %collective-permute-start.33 = (bf16[2,1024,1024]{2,1,0:T(8,128)(2,1)S(1)}, bf16[2,1024,1024]{2,1,0:T(8,128)(2,1)S(1)}, u32[]{:S(2)}, u32[]{:S(2)}) collective-permute-start(bf16[2,1024,1024]{2,1,0:T(8,128)(2,1)S(1)} %back_solve.1.qs), channel_id=1, source_target_pairs={{0,16},{16,0},{1,17},{17,1},{2,18},{18,2},{3,19},{19,3},{4,20},{20... | collective-permute-start | bytes 12582920 | tf_op jit(solution)/shard_map/ppermute | solution.py:518
  (7 other events, 4.8 us)

commit v6 on v5

--- a/solution.py
+++ b/solution.py
@@ -321,33 +321,40 @@
 def factor_diag(work, between):
     tn = ((0,), (0,))
     wide = work.shape[1]
+
+    def across(value, at):
+        return jnp.broadcast_to(value[:, at : at + 1], (1, LANE))
+
+    def twice(value):
+        return jnp.concatenate([value] * (wide // LANE), axis=1)
+
+    rows = [work[i : i + 1, :] for i in range(SUB)]
     for top in range(0, LANE, SUB):
-        rows = [work[top + i : top + i + 1, :] for i in range(SUB)]
-        e = {}
-        for j in range(SUB):
-            for i in range(j, SUB):
-                at = top + i
-                e[j, i] = jnp.broadcast_to(rows[j][:, at : at + 1], (1, LANE))
+        e = {(j, i): across(rows[j], top + i) for j in range(SUB) for i in range(j, SUB)}
         for j in range(SUB):
             inv = lax.rsqrt(e[j, j])
-            inv2 = jnp.concatenate([inv] * (wide // LANE), axis=1)
-            rows[j] = rows[j] * inv2
+            rows[j] = rows[j] * twice(inv)
             for i in range(j + 1, SUB):
                 e[j, i] = e[j, i] * inv
             for i in range(j + 1, SUB):
                 for k in range(i, SUB):
                     e[i, k] = e[i, k] - e[j, i] * e[j, k]
-                coef = jnp.concatenate([e[j, i]] * (wide // LANE), axis=1)
-                rows[i] = rows[i] - coef * rows[j]
+                rows[i] = rows[i] - twice(e[j, i]) * rows[j]
         part = jnp.concatenate(rows, axis=0)
         work[top : top + SUB, :] = part
         end = top + SUB
         if end < LANE:
+            later = [work[end + i : end + i + 1, :] for i in range(SUB)]
+            for i in range(SUB):
+                for j in range(SUB):
+                    later[i] = later[i] - twice(across(rows[j], end + i)) * rows[j]
+            rows = later
+        if end + SUB < LANE:
             h, m, l = three(part)
             lhs = jnp.concatenate([h, h, m, m, h, l], axis=0)[:, :LANE]
             rhs = jnp.concatenate([h, m, h, m, l, h], axis=0)
             gone = mm(lhs, rhs, tn)
-            work[end:, :] = work[end:, :] - gone[end:, :]
+            work[end + SUB :, :] = work[end + SUB :, :] - gone[end + SUB :, :]
         between()
 
 
@@ -607,7 +614,9 @@
         [pltpu.VMEM((arcs, observed, observed), BF16), pltpu.VMEM((arcs, observed, LANE), BF16)],
     )
 
-    stack = [chunk] + [hop(chunk, 4 * k) for k in range(1, planes)]
+    stack = [chunk]
+    for k in range(1, planes):
+        stack.append(hop(chunk, 4 * k))
     stack = jnp.stack(stack, axis=1)
     pieces = []
     for arc in range(arcs):

time: 171 us -> 165 us (0.965)
  Pallas kernels: 56 us -> 50.3 us
    pallas_call x1, Pallas kernels: 27.4 us -> 21.8 us  [chol_normals(): pl.pallas_call(chol_normals_kernel, out_shape=(jax.ShapeDtypeStruct((size...]
  transfers between devices with their start and end apart: 34 -> 34, of which waited for: 12 -> 12; matrix products, arithmetic and copies ran while one was open for 10% -> 11% of each run, Pallas kernels for 24% -> 22%
where the time goes in v6:
time: 165 us; the launch traced here: 162 us
  Pallas kernels  50.3 us (30%)
  starting transfers between devices  42 us (25%)
  waiting for transfers between devices  37.4 us (23%)
  local copies, waits for them, and re-layouts  22 us (13%)
  other arithmetic  9.43 us (6%)
    ppermute x30, starting transfers between devices, hop(): return lax.ppermute(value, 'par', [(p, p ^ bits) for p in range(chips)])  40.6 us
    ppermute x30, waiting for transfers between devices, hop(): return lax.ppermute(value, 'par', [(p, p ^ bits) for p in range(chips)])  37.3 us
    pallas_call x1, Pallas kernels, chol_normals(): pl.pallas_call(chol_normals_kernel, out_shape=(jax.ShapeDtypeStruct((size...  21.8 us
    unnamed x42, local copies, waits for them, and re-layouts  14.2 us
    pallas_call x1, Pallas kernels, invert_call(): pl.pallas_call(kernel, out_shape=(out, out), in_specs=[SM if value.dtype...  7.67 us
    pallas_call x1, Pallas kernels, panel_call(): pl.pallas_call(functools.partial(panel_kernel, arcs), out_shape=(jax.Shap...  7.59 us
    pallas_call x1, Pallas kernels, normals_call(): pl.pallas_call(normals_kernel, out_shape=jax.ShapeDtypeStruct((width, sha...  7.35 us
    dynamic_slice x1, local copies, waits for them, and re-layouts, paired(): far = lax.dynamic_slice_in_dim(design, (1 - core) * share, share, 2)  5.64 us
  transfers between devices with their start and end apart: 34, of which 12 were waited for; matrix products, arithmetic and copies ran while one was open for 11% of the time, Pallas kernels for 22%

profile of v6, /device:TPU:0, one launch (start us, length us, event | category | flops | bytes accessed | tf_op | source)
XLA Modules:
  0.0 162.3 jit_solution(14694962601696944189)
XLA Ops:
  1.2 0.9 compare_reduce_fusion.1
  2.3 3.5 %bitcast_select_fusion = (bf16[512,512]{1,0:T(8,128)(2,1)S(1)}, bf16[512,512]{1,0:T(8,128)(2,1)}, bf16[512,512]{1,0:T(8,128)(2,1)S(1)}, bf16[512,512]{1,0:T(8,128)(2,1)S(1)}) fusion(bf16[2,1024,2560]{2,1,0:T(8,128)(2,1)} %own.1, s32[]{:T(128)S(6)} %select_n.107, s32[]{:T(128)S(6)} %min.4, pred[512]{0:T(512)(128)(4,1)S(1)} %broadcast_in_dim.58, ...), kind=kLoop, calls=%fused_computation.9 | loop fusion | flops 1048576 | bytes 4195348 | tf_op jit(solution)/shard_map/jit(_where)/select_n | solution.py:544
  5.9 2.9 %factor_rows.1 = bf16[2,64,1152]{2,1,0:T(8,128)(2,1)S(1)} custom-call(s32[2]{0:T(128)S(1)} %pad_add_fusion.4.place_ref, f32[2,64,1024]{2,1,0:T(8,128)S(1)} %copy-done.2), custom_call_target="tpu_custom_call" | custom-call | tf_op jit(solution)/shard_map/factor_rows/pallas_call | solution.py:76
  8.8 5.0 %collective-permute-start.18 = (bf16[2,64,1152]{2,1,0:T(8,128)(2,1)S(1)}, bf16[2,64,1152]{2,1,0:T(8,128)(2,1)S(1)}, u32[]{:S(2)}, u32[]{:S(2)}) collective-permute-start(bf16[2,64,1152]{2,1,0:T(8,128)(2,1)S(1)} %factor_rows.1), channel_id=1, source_target_pairs={{0,12},{1,13},{2,14},{3,15},{4,8},{5,9},{6,10},{7,11},{8,4},{9,5},... | collective-permute-start | bytes 884744 | tf_op jit(solution)/shard_map/ppermute | solution.py:528
  13.8 1.5 collective-permute-start.2
  15.3 1.5 collective-permute-start
  19.2 2.3 %collective-permute-done.18 = bf16[2,64,1152]{2,1,0:T(8,128)(2,1)S(1)} collective-permute-done((bf16[2,64,1152]{2,1,0:T(8,128)(2,1)S(1)}, bf16[2,64,1152]{2,1,0:T(8,128)(2,1)S(1)}, u32[]{:S(2)}, u32[]{:S(2)}) %collective-permute-start.18) | collective-permute-done | bytes 294944 | tf_op jit(solution)/shard_map/ppermute | solution.py:528
  21.6 6.5 %collective-permute-done.2 = bf16[512,512]{1,0:T(8,128)(2,1)} collective-permute-done((bf16[512,512]{1,0:T(8,128)(2,1)}, bf16[512,512]{1,0:T(8,128)(2,1)}, u32[]{:S(2)}, u32[]{:S(2)}) %collective-permute-start.2) | collective-permute-done | bytes 524320 | tf_op jit(solution)/shard_map/ppermute | solution.py:528
  28.1 1.0 dynamic-slice_add_fusion
  29.1 1.6 collective-permute-start.3
  30.7 1.0 dynamic-slice_add_fusion.1
  31.7 1.6 collective-permute-start.1
  33.4 3.2 %collective-permute-done.3 = bf16[256,512]{1,0:T(8,128)(2,1)S(1)} collective-permute-done((bf16[256,512]{1,0:T(8,128)(2,1)S(1)}, bf16[256,512]{1,0:T(8,128)(2,1)S(1)}, u32[]{:S(2)}, u32[]{:S(2)}) %collective-permute-start.3) | collective-permute-done | bytes 262176 | tf_op jit(solution)/shard_map/ppermute | solution.py:528
  36.7 1.1 add_add_fusion
  37.7 1.2 collective-permute-done.1
  39.0 1.1 add_add_fusion.1
  40.2 1.2 collective-permute-start.5
  41.4 3.2 %collective-permute-start.6 = (bf16[2,64,512]{2,1,0:T(8,128)(2,1)S(1)}, bf16[2,64,512]{2,1,0:T(8,128)(2,1)S(1)}, u32[]{:S(2)}, u32[]{:S(2)}) collective-permute-start(bf16[2,64,512]{2,1,0:T(8,128)(2,1)S(1)} %get-tuple-element.51), channel_id=1, source_target_pairs={{0,12},{1,13},{2,14},{3,15},{4,8},{5,9},{6,10},{7,11},{8,4},{9,5},... | collective-permute-start | bytes 393224 | tf_op jit(solution)/shard_map/ppermute | solution.py:528
  45.2 5.0 %collective-permute-done.4 = bf16[2,64,512]{2,1,0:T(8,128)(2,1)S(1)} collective-permute-done((bf16[2,64,512]{2,1,0:T(8,128)(2,1)S(1)}, bf16[2,64,512]{2,1,0:T(8,128)(2,1)S(1)}, u32[]{:S(2)}, u32[]{:S(2)}) %collective-permute-start.4) | collective-permute-done | bytes 131104 | tf_op jit(solution)/shard_map/ppermute | solution.py:528
  50.2 3.1 %collective-permute-start.27 = (bf16[64,1536]{1,0:T(8,128)(2,1)S(1)}, bf16[64,1536]{1,0:T(8,128)(2,1)S(1)}, u32[]{:S(2)}, u32[]{:S(2)}) collective-permute-start(bf16[64,1536]{1,0:T(8,128)(2,1)S(1)} %get-tuple-element.54.refs_8_), channel_id=1, source_target_pairs={{0,2},{1,3},{2,0},{3,1},{4,6},{5,7},{6,4},{7,5},{8,10},{9,11},{10,... | collective-permute-start | bytes 589832 | tf_op jit(solution)/shard_map/ppermute | solution.py:528
  53.9 2.1 %collective-permute-start.10 = (bf16[2,64,512]{2,1,0:T(8,128)(2,1)S(1)}, bf16[2,64,512]{2,1,0:T(8,128)(2,1)S(1)}, u32[]{:S(2)}, u32[]{:S(2)}) collective-permute-start(bf16[2,64,512]{2,1,0:T(8,128)(2,1)S(1)} %fusion.6), channel_id=1, source_target_pairs={{0,8},{1,9},{2,10},{3,11},{4,12},{5,13},{6,14},{7,15},{8,0},{9,1},... | collective-permute-start | bytes 393224 | tf_op jit(solution)/shard_map/ppermute | solution.py:528
  56.0 1.8 %collective-permute-start.11 = (bf16[2,64,512]{2,1,0:T(8,128)(2,1)S(1)}, bf16[2,64,512]{2,1,0:T(8,128)(2,1)S(1)}, u32[]{:S(2)}, u32[]{:S(2)}) collective-permute-start(bf16[2,64,512]{2,1,0:T(8,128)(2,1)S(1)} %fusion.6), channel_id=1, source_target_pairs={{0,12},{1,13},{2,14},{3,15},{4,8},{5,9},{6,10},{7,11},{8,4},{9,5},... | collective-permute-start | bytes 393224 | tf_op jit(solution)/shard_map/ppermute | solution.py:528
  58.6 1.0 collective-permute-done.9
  59.9 3.3 %collective-permute-done.10 = bf16[2,64,512]{2,1,0:T(8,128)(2,1)S(1)} collective-permute-done((bf16[2,64,512]{2,1,0:T(8,128)(2,1)S(1)}, bf16[2,64,512]{2,1,0:T(8,128)(2,1)S(1)}, u32[]{:S(2)}, u32[]{:S(2)}) %collective-permute-start.10) | collective-permute-done | bytes 131104 | tf_op jit(solution)/shard_map/ppermute | solution.py:528
  63.8 1.5 collective-permute-start.23
  65.4 2.9 %collective-permute-start.30 = (bf16[64,1536]{1,0:T(8,128)(2,1)S(1)}, bf16[64,1536]{1,0:T(8,128)(2,1)}, u32[]{:S(2)}, u32[]{:S(2)}) collective-permute-start(bf16[64,1536]{1,0:T(8,128)(2,1)S(1)} %get-tuple-element.52.refs_12_), channel_id=1, source_target_pairs={{0,2},{1,3},{2,0},{3,1},{4,6},{5,7},{6,4},{7,5},{8,10},{9,11},{10,... | collective-permute-start | bytes 589832 | tf_op jit(solution)/shard_map/ppermute | solution.py:528
  71.7 2.8 %collective-permute-start.24 = (bf16[64,1536]{1,0:T(8,128)(2,1)S(1)}, bf16[64,1536]{1,0:T(8,128)(2,1)S(1)}, u32[]{:S(2)}, u32[]{:S(2)}) collective-permute-start(bf16[64,1536]{1,0:T(8,128)(2,1)S(1)} %get-tuple-element.53.refs_4_), channel_id=1, source_target_pairs={{0,2},{1,3},{2,0},{3,1},{4,6},{5,7},{6,4},{7,5},{8,10},{9,11},{10,... | collective-permute-start | bytes 589832 | tf_op jit(solution)/shard_map/ppermute | solution.py:528
  75.8 2.1 %collective-permute-start.25 = (bf16[64,1536]{1,0:T(8,128)(2,1)S(1)}, bf16[64,1536]{1,0:T(8,128)(2,1)S(1)}, u32[]{:S(2)}, u32[]{:S(2)}) collective-permute-start(bf16[64,1536]{1,0:T(8,128)(2,1)S(1)} %collective-permute-done.23.refs_5_), channel_id=1, source_target_pairs={{0,2},{1,3},{2,0},{3,1},{4,6},{5,7},{6,4},{7,5},{8,10},{9,11},{10,... | collective-permute-start | bytes 589832 | tf_op jit(solution)/shard_map/ppermute | solution.py:528
  78.6 5.2 %collective-permute-done.24.refs_6_ = bf16[64,1536]{1,0:T(8,128)(2,1)S(1)} collective-permute-done((bf16[64,1536]{1,0:T(8,128)(2,1)S(1)}, bf16[64,1536]{1,0:T(8,128)(2,1)S(1)}, u32[]{:S(2)}, u32[]{:S(2)}) %collective-permute-start.24) | collective-permute-done | bytes 196640 | tf_op jit(solution)/shard_map/ppermute | solution.py:528
  84.6 2.0 %collective-permute-start.13 = (bf16[4,64,512]{2,1,0:T(8,128)(2,1)S(1)}, bf16[4,64,512]{2,1,0:T(8,128)(2,1)S(1)}, u32[]{:S(2)}, u32[]{:S(2)}) collective-permute-start(bf16[4,64,512]{2,1,0:T(8,128)(2,1)S(1)} %get-tuple-element.48.refs_0_), channel_id=1, source_target_pairs={{0,2},{1,3},{2,0},{3,1},{4,6},{5,7},{6,4},{7,5},{8,10},{9,11},{10,... | collective-permute-start | bytes 786440 | tf_op jit(solution)/shard_map/ppermute | solution.py:528
  88.5 0.8 collective-permute-start.17
  90.1 1.2 collective-permute-start.31
  91.3 7.4 %collective-permute-done.31.refs_15_ = bf16[64,1536]{1,0:T(8,128)(2,1)} collective-permute-done((bf16[64,1536]{1,0:T(8,128)(2,1)}, bf16[64,1536]{1,0:T(8,128)(2,1)}, u32[]{:S(2)}, u32[]{:S(2)}) %collective-permute-start.31) | collective-permute-done | bytes 196640 | tf_op jit(solution)/shard_map/ppermute | solution.py:528
  98.7 0.9 copy-done.4
  99.6 0.9 copy-done.6
  100.5 0.9 copy-done.8
  101.4 0.9 copy-done.10
  102.4 0.9 copy-done.12
  103.3 0.9 copy-done.14
  104.2 0.9 copy-done.16
  105.2 7.7 %invert_factor.1 = (bf16[2,1024,1024]{2,1,0:T(8,128)(2,1)S(1)}, bf16[2,1024,1024]{2,1,0:T(8,128)(2,1)S(1)}) custom-call(s32[5]{0:T(128)S(1)} %pad_add_fusion.1.place_ref, bf16[64,1536]{1,0:T(8,128)(2,1)S(1)} %get-tuple-element.55.refs_0_, bf16[64,1536]{1,0:T(8,128)(2,1)S(1)} %collective-permute-done.19.refs_1_, ...), custom_call_target="tpu_custom_call" | custom-call | tf_op jit(solution)/shard_map/invert_factor/pallas_call | solution.py:172
  112.9 7.6 %panel_block.1 = (bf16[2,512,1024]{2,1,0:T(8,128)(2,1)S(1)}, f32[512,512]{1,0:T(8,128)}) custom-call(s32[32]{0:T(128)S(1)} %pad_add_fusion.3.place_ref, bf16[4,64,512]{2,1,0:T(8,128)(2,1)S(1)} %get-tuple-element.48.refs_0_, bf16[4,64,512]{2,1,0:T(8,128)(2,1)S(1)} %collective-permute-done.12.refs_1_, bf16[4,64,512]{2,1,0:T(8,128)(2,1)S(1)} %collective-permute-done.13.refs_2_, ...), custom_call_target="tpu_custom_call" | custom-call | tf_op jit(solution)/shard_map/panel_block/pallas_call | solution.py:230
  120.5 1.3 copy-done
  121.8 5.6 %constant_dynamic-slice_fusion = bf16[2,1024,1280]{2,1,0:T(8,128)(2,1)} fusion(bf16[2,1024,2560]{2,1,0:T(8,128)(2,1)} %own.1, s32[]{:T(128)S(6)} %select_n.118), kind=kLoop, calls=%fused_computation.38 | loop fusion | bytes 10485764 | tf_op jit(solution)/shard_map/dynamic_slice | solution.py:601
  127.9 1.6 copy-done.1
  129.5 3.0 %back_solve.1.qs = bf16[2,1024,1024]{2,1,0:T(8,128)(2,1)S(1)} custom-call(bf16[2,512,1024]{2,1,0:T(8,128)(2,1)S(1)} %copy-done.1, bf16[2,1024,1024]{2,1,0:T(8,128)(2,1)S(1)} %get-tuple-element.29.refs_8_.high, bf16[2,1024,1024]{2,1,0:T(8,128)(2,1)S(1)} %get-tuple-element.30.refs_9_.low), custom_call_target="tpu_custom_call" | custom-call | tf_op jit(solution)/shard_map/back_solve/pallas_call | solution.py:246
  132.9 21.8 %chol_normals.1 = (f32[512,512]{1,0:T(8,128)S(1)}, f32[6,512,256]{2,1,0:T(8,128)S(1)}) custom-call(s32[22]{0:T(128)S(1)} %pad_add_fusion.2.info, f32[512,512]{1,0:T(8,128)} %get-tuple-element.32.block_ref, f32[512,512]{1,0:T(8,128)} %collective-permute-done.32.other_ref, f32[1,512]{1,0:T(1,128)S(1)} %bitcast.61, bf16[2,1024,2560]{2,1,0:T(8,128)(2,1)S(1)} %bitcast.60, ...), custom_call_target="tpu_custom_call" | custom-call | tf_op jit(solution)/shard_map/chol_normals/pallas_call | solution.py:437
  154.8 7.4 %normals.1 = f32[512,1280]{1,0:T(8,128)} custom-call(s32[22]{0:T(128)S(1)} %pad_add_fusion.2.info, bf16[2,1024,1280]{2,1,0:T(8,128)(2,1)S(1)} %collective-permute-done.8.far, bf16[2,1024,1024]{2,1,0:T(8,128)(2,1)S(1)} %collective-permute-done.33.qs, f32[6,512,256]{2,1,0:T(8,128)S(1)} %get-tuple-element.36.sums, f32[512,512]{1,0:T(8,128)S(1)} %get-tuple-element.37.inv_ref, ...), custom_call_target="tpu_custom_call" | custom-call | tf_op jit(solution)/shard_map/normals/pallas_call | solution.py:296
  (113 shorter events, 16.1 us)
Async XLA Ops:
  0.0 18.8 %copy-start.17 = (s32[2,80]{1,0:T(2,128)S(1)}, s32[2,80]{1,0:T(2,128)}, u32[]{:S(2)}) copy-start(s32[2,80]{1,0:T(2,128)} %param.7) | copy-start | bytes 1924
  0.0 5.9 %copy-start.2 = (f32[2,64,1024]{2,1,0:T(8,128)S(1)}, f32[2,64,1024]{2,1,0:T(8,128)}, u32[]{:S(2)}) copy-start(f32[2,64,1024]{2,1,0:T(8,128)} %rows_ref) | copy-start | bytes 1572868
  0.0 18.8 %collective-permute-start.7 = (s32[2,80]{1,0:T(2,128)}, s32[2,80]{1,0:T(2,128)S(1)}, u32[]{:S(2)}, u32[]{:S(2)}) collective-permute-start(s32[2,80]{1,0:T(2,128)} %param.7), channel_id=1, source_target_pairs={{0,16},{16,0},{1,17},{17,1},{2,18},{18,2},{3,19},{19,3},{4,20},{20... | collective-permute-start | bytes 1928 | tf_op jit(solution)/shard_map/ppermute | solution.py:525
  8.8 12.7 %collective-permute-start.18 = (bf16[2,64,1152]{2,1,0:T(8,128)(2,1)S(1)}, bf16[2,64,1152]{2,1,0:T(8,128)(2,1)S(1)}, u32[]{:S(2)}, u32[]{:S(2)}) collective-permute-start(bf16[2,64,1152]{2,1,0:T(8,128)(2,1)S(1)} %factor_rows.1), channel_id=1, source_target_pairs={{0,12},{1,13},{2,14},{3,15},{4,8},{5,9},{6,10},{7,11},{8,4},{9,5},... | collective-permute-start | bytes 884744 | tf_op jit(solution)/shard_map/ppermute | solution.py:528
  13.8 14.3 %collective-permute-start.2 = (bf16[512,512]{1,0:T(8,128)(2,1)}, bf16[512,512]{1,0:T(8,128)(2,1)}, u32[]{:S(2)}, u32[]{:S(2)}) collective-permute-start(bf16[512,512]{1,0:T(8,128)(2,1)} %get-tuple-element.23), channel_id=1, source_target_pairs={{0,2},{1,3},{2,0},{3,1},{4,6},{5,7},{6,4},{7,5},{8,10},{9,11},{10,... | collective-permute-start | bytes 1572872 | tf_op jit(solution)/shard_map/ppermute | solution.py:528
  15.3 15.4 %collective-permute-start = (bf16[512,512]{1,0:T(8,128)(2,1)S(1)}, bf16[512,512]{1,0:T(8,128)(2,1)}, u32[]{:S(2)}, u32[]{:S(2)}) collective-permute-start(bf16[512,512]{1,0:T(8,128)(2,1)S(1)} %get-tuple-element.22), channel_id=1, source_target_pairs={{0,1},{1,0},{2,3},{3,2},{4,5},{5,4},{6,7},{7,6},{8,9},{9,8},{10,11... | collective-permute-start | bytes 1572872 | tf_op jit(solution)/shard_map/ppermute | solution.py:528
  29.1 7.6 %collective-permute-start.3 = (bf16[256,512]{1,0:T(8,128)(2,1)S(1)}, bf16[256,512]{1,0:T(8,128)(2,1)S(1)}, u32[]{:S(2)}, u32[]{:S(2)}) collective-permute-start(bf16[256,512]{1,0:T(8,128)(2,1)S(1)} %dynamic-slice_add_fusion), channel_id=1, source_target_pairs={{0,1},{1,0},{2,3},{3,2},{4,5},{5,4},{6,7},{7,6},{8,9},{9,8},{10,11... | collective-permute-start | bytes 786440 | tf_op jit(solution)/shard_map/ppermute | solution.py:528
  31.7 7.3 %collective-permute-start.1 = (bf16[256,512]{1,0:T(8,128)(2,1)S(1)}, bf16[256,512]{1,0:T(8,128)(2,1)S(1)}, u32[]{:S(2)}, u32[]{:S(2)}) collective-permute-start(bf16[256,512]{1,0:T(8,128)(2,1)S(1)} %dynamic-slice_add_fusion.1), channel_id=1, source_target_pairs={{0,2},{1,3},{2,0},{3,1},{4,6},{5,7},{6,4},{7,5},{8,10},{9,11},{10,... | collective-permute-start | bytes 786440 | tf_op jit(solution)/shard_map/ppermute | solution.py:528
  33.4 22.7 %collective-permute-start.22 = (bf16[2,64,1536]{2,1,0:T(8,128)(2,1)S(1)}, bf16[2,64,1536]{2,1,0:T(8,128)(2,1)S(1)}, u32[]{:S(2)}, u32[]{:S(2)}) collective-permute-start(bf16[2,64,1536]{2,1,0:T(8,128)(2,1)S(1)} %maximum_select_fusion), channel_id=1, source_target_pairs={{0,4},{1,5},{2,6},{3,7},{4,0},{5,1},{6,2},{7,3},{8,12},{9,13},{10,... | collective-permute-start | bytes 1179656 | tf_op jit(solution)/shard_map/ppermute | solution.py:528
  40.1 10.1 %collective-permute-start.4 = (bf16[2,64,512]{2,1,0:T(8,128)(2,1)S(1)}, bf16[2,64,512]{2,1,0:T(8,128)(2,1)S(1)}, u32[]{:S(2)}, u32[]{:S(2)}) collective-permute-start(bf16[2,64,512]{2,1,0:T(8,128)(2,1)S(1)} %get-tuple-element.49), channel_id=1, source_target_pairs={{0,4},{1,5},{2,6},{3,7},{4,0},{5,1},{6,2},{7,3},{8,12},{9,13},{10,... | collective-permute-start | bytes 393224 | tf_op jit(solution)/shard_map/ppermute | solution.py:528
  40.2 10.0 %collective-permute-start.5 = (bf16[2,64,512]{2,1,0:T(8,128)(2,1)S(1)}, bf16[2,64,512]{2,1,0:T(8,128)(2,1)S(1)}, u32[]{:S(2)}, u32[]{:S(2)}) collective-permute-start(bf16[2,64,512]{2,1,0:T(8,128)(2,1)S(1)} %get-tuple-element.50), channel_id=1, source_target_pairs={{0,8},{1,9},{2,10},{3,11},{4,12},{5,13},{6,14},{7,15},{8,0},{9,1},... | collective-permute-start | bytes 393224 | tf_op jit(solution)/shard_map/ppermute | solution.py:528
  41.4 11.9 %collective-permute-start.6 = (bf16[2,64,512]{2,1,0:T(8,128)(2,1)S(1)}, bf16[2,64,512]{2,1,0:T(8,128)(2,1)S(1)}, u32[]{:S(2)}, u32[]{:S(2)}) collective-permute-start(bf16[2,64,512]{2,1,0:T(8,128)(2,1)S(1)} %get-tuple-element.51), channel_id=1, source_target_pairs={{0,12},{1,13},{2,14},{3,15},{4,8},{5,9},{6,10},{7,11},{8,4},{9,5},... | collective-permute-start | bytes 393224 | tf_op jit(solution)/shard_map/ppermute | solution.py:528
  44.6 9.3 %collective-permute-start.19 = (bf16[64,1536]{1,0:T(8,128)(2,1)S(1)}, bf16[64,1536]{1,0:T(8,128)(2,1)S(1)}, u32[]{:S(2)}, u32[]{:S(2)}) collective-permute-start(bf16[64,1536]{1,0:T(8,128)(2,1)S(1)} %get-tuple-element.55.refs_0_), channel_id=1, source_target_pairs={{0,1},{1,0},{2,3},{3,2},{4,5},{5,4},{6,7},{7,6},{8,9},{9,8},{10,11... | collective-permute-start | bytes 589832 | tf_op jit(solution)/shard_map/ppermute | solution.py:528
  50.2 15.2 %collective-permute-start.20 = (bf16[64,1536]{1,0:T(8,128)(2,1)S(1)}, bf16[64,1536]{1,0:T(8,128)(2,1)S(1)}, u32[]{:S(2)}, u32[]{:S(2)}) collective-permute-start(bf16[64,1536]{1,0:T(8,128)(2,1)S(1)} %get-tuple-element.55.refs_0_), channel_id=1, source_target_pairs={{0,2},{1,3},{2,0},{3,1},{4,6},{5,7},{6,4},{7,5},{8,10},{9,11},{10,... | collective-permute-start | bytes 589832 | tf_op jit(solution)/shard_map/ppermute | solution.py:528
  50.2 8.1 %collective-permute-start.27 = (bf16[64,1536]{1,0:T(8,128)(2,1)S(1)}, bf16[64,1536]{1,0:T(8,128)(2,1)S(1)}, u32[]{:S(2)}, u32[]{:S(2)}) collective-permute-start(bf16[64,1536]{1,0:T(8,128)(2,1)S(1)} %get-tuple-element.54.refs_8_), channel_id=1, source_target_pairs={{0,2},{1,3},{2,0},{3,1},{4,6},{5,7},{6,4},{7,5},{8,10},{9,11},{10,... | collective-permute-start | bytes 589832 | tf_op jit(solution)/shard_map/ppermute | solution.py:528
  53.3 6.3 %collective-permute-start.9 = (bf16[2,64,512]{2,1,0:T(8,128)(2,1)S(1)}, bf16[2,64,512]{2,1,0:T(8,128)(2,1)S(1)}, u32[]{:S(2)}, u32[]{:S(2)}) collective-permute-start(bf16[2,64,512]{2,1,0:T(8,128)(2,1)S(1)} %fusion.6), channel_id=1, source_target_pairs={{0,4},{1,5},{2,6},{3,7},{4,0},{5,1},{6,2},{7,3},{8,12},{9,13},{10,... | collective-permute-start | bytes 393224 | tf_op jit(solution)/shard_map/ppermute | solution.py:528
  53.9 9.4 %collective-permute-start.10 = (bf16[2,64,512]{2,1,0:T(8,128)(2,1)S(1)}, bf16[2,64,512]{2,1,0:T(8,128)(2,1)S(1)}, u32[]{:S(2)}, u32[]{:S(2)}) collective-permute-start(bf16[2,64,512]{2,1,0:T(8,128)(2,1)S(1)} %fusion.6), channel_id=1, source_target_pairs={{0,8},{1,9},{2,10},{3,11},{4,12},{5,13},{6,14},{7,15},{8,0},{9,1},... | collective-permute-start | bytes 393224 | tf_op jit(solution)/shard_map/ppermute | solution.py:528
  56.0 7.8 %collective-permute-start.11 = (bf16[2,64,512]{2,1,0:T(8,128)(2,1)S(1)}, bf16[2,64,512]{2,1,0:T(8,128)(2,1)S(1)}, u32[]{:S(2)}, u32[]{:S(2)}) collective-permute-start(bf16[2,64,512]{2,1,0:T(8,128)(2,1)S(1)} %fusion.6), channel_id=1, source_target_pairs={{0,12},{1,13},{2,14},{3,15},{4,8},{5,9},{6,10},{7,11},{8,4},{9,5},... | collective-permute-start | bytes 393224 | tf_op jit(solution)/shard_map/ppermute | solution.py:528
  58.3 10.0 %collective-permute-start.26 = (bf16[64,1536]{1,0:T(8,128)(2,1)S(1)}, bf16[64,1536]{1,0:T(8,128)(2,1)S(1)}, u32[]{:S(2)}, u32[]{:S(2)}) collective-permute-start(bf16[64,1536]{1,0:T(8,128)(2,1)S(1)} %get-tuple-element.54.refs_8_), channel_id=1, source_target_pairs={{0,1},{1,0},{2,3},{3,2},{4,5},{5,4},{6,7},{7,6},{8,9},{9,8},{10,11... | collective-permute-start | bytes 589832 | tf_op jit(solution)/shard_map/ppermute | solution.py:528
  59.6 9.9 %collective-permute-start.21 = (bf16[64,1536]{1,0:T(8,128)(2,1)S(1)}, bf16[64,1536]{1,0:T(8,128)(2,1)S(1)}, u32[]{:S(2)}, u32[]{:S(2)}) collective-permute-start(bf16[64,1536]{1,0:T(8,128)(2,1)S(1)} %collective-permute-done.19.refs_1_), channel_id=1, source_target_pairs={{0,2},{1,3},{2,0},{3,1},{4,6},{5,7},{6,4},{7,5},{8,10},{9,11},{10,... | collective-permute-start | bytes 589832 | tf_op jit(solution)/shard_map/ppermute | solution.py:528
  63.3 7.8 %collective-permute-start.28 = (bf16[64,1536]{1,0:T(8,128)(2,1)S(1)}, bf16[64,1536]{1,0:T(8,128)(2,1)S(1)}, u32[]{:S(2)}, u32[]{:S(2)}) collective-permute-start(bf16[64,1536]{1,0:T(8,128)(2,1)S(1)} %collective-permute-done.27.refs_10_), channel_id=1, source_target_pairs={{0,1},{1,0},{2,3},{3,2},{4,5},{5,4},{6,7},{7,6},{8,9},{9,8},{10,11... | collective-permute-start | bytes 589832 | tf_op jit(solution)/shard_map/ppermute | solution.py:528
  63.8 11.4 %collective-permute-start.23 = (bf16[64,1536]{1,0:T(8,128)(2,1)S(1)}, bf16[64,1536]{1,0:T(8,128)(2,1)S(1)}, u32[]{:S(2)}, u32[]{:S(2)}) collective-permute-start(bf16[64,1536]{1,0:T(8,128)(2,1)S(1)} %get-tuple-element.53.refs_4_), channel_id=1, source_target_pairs={{0,1},{1,0},{2,3},{3,2},{4,5},{5,4},{6,7},{7,6},{8,9},{9,8},{10,11... | collective-permute-start | bytes 589832 | tf_op jit(solution)/shard_map/ppermute | solution.py:528
  65.4 10.4 %collective-permute-start.30 = (bf16[64,1536]{1,0:T(8,128)(2,1)S(1)}, bf16[64,1536]{1,0:T(8,128)(2,1)}, u32[]{:S(2)}, u32[]{:S(2)}) collective-permute-start(bf16[64,1536]{1,0:T(8,128)(2,1)S(1)} %get-tuple-element.52.refs_12_), channel_id=1, source_target_pairs={{0,2},{1,3},{2,0},{3,1},{4,6},{5,7},{6,4},{7,5},{8,10},{9,11},{10,... | collective-permute-start | bytes 589832 | tf_op jit(solution)/shard_map/ppermute | solution.py:528
  69.0 18.7 %collective-permute-start.12 = (bf16[4,64,512]{2,1,0:T(8,128)(2,1)S(1)}, bf16[4,64,512]{2,1,0:T(8,128)(2,1)S(1)}, u32[]{:S(2)}, u32[]{:S(2)}) collective-permute-start(bf16[4,64,512]{2,1,0:T(8,128)(2,1)S(1)} %get-tuple-element.48.refs_0_), channel_id=1, source_target_pairs={{0,1},{1,0},{2,3},{3,2},{4,5},{5,4},{6,7},{7,6},{8,9},{9,8},{10,11... | collective-permute-start | bytes 786440 | tf_op jit(solution)/shard_map/ppermute | solution.py:528
  70.2 18.3 %collective-permute-start.16 = (bf16[4,64,512]{2,1,0:T(8,128)(2,1)S(1)}, bf16[4,64,512]{2,1,0:T(8,128)(2,1)S(1)}, u32[]{:S(2)}, u32[]{:S(2)}) collective-permute-start(bf16[4,64,512]{2,1,0:T(8,128)(2,1)S(1)} %get-tuple-element.47.refs_4_), channel_id=1, source_target_pairs={{0,2},{1,3},{2,0},{3,1},{4,6},{5,7},{6,4},{7,5},{8,10},{9,11},{10,... | collective-permute-start | bytes 786440 | tf_op jit(solution)/shard_map/ppermute | solution.py:528
  71.7 12.1 %collective-permute-start.24 = (bf16[64,1536]{1,0:T(8,128)(2,1)S(1)}, bf16[64,1536]{1,0:T(8,128)(2,1)S(1)}, u32[]{:S(2)}, u32[]{:S(2)}) collective-permute-start(bf16[64,1536]{1,0:T(8,128)(2,1)S(1)} %get-tuple-element.53.refs_4_), channel_id=1, source_target_pairs={{0,2},{1,3},{2,0},{3,1},{4,6},{5,7},{6,4},{7,5},{8,10},{9,11},{10,... | collective-permute-start | bytes 589832 | tf_op jit(solution)/shard_map/ppermute | solution.py:528
  75.3 11.3 %collective-permute-start.29 = (bf16[64,1536]{1,0:T(8,128)(2,1)S(1)}, bf16[64,1536]{1,0:T(8,128)(2,1)S(1)}, u32[]{:S(2)}, u32[]{:S(2)}) collective-permute-start(bf16[64,1536]{1,0:T(8,128)(2,1)S(1)} %get-tuple-element.52.refs_12_), channel_id=1, source_target_pairs={{0,1},{1,0},{2,3},{3,2},{4,5},{5,4},{6,7},{7,6},{8,9},{9,8},{10,11... | collective-permute-start | bytes 589832 | tf_op jit(solution)/shard_map/ppermute | solution.py:528
  75.8 13.6 %collective-permute-start.25 = (bf16[64,1536]{1,0:T(8,128)(2,1)S(1)}, bf16[64,1536]{1,0:T(8,128)(2,1)S(1)}, u32[]{:S(2)}, u32[]{:S(2)}) collective-permute-start(bf16[64,1536]{1,0:T(8,128)(2,1)S(1)} %collective-permute-done.23.refs_5_), channel_id=1, source_target_pairs={{0,2},{1,3},{2,0},{3,1},{4,6},{5,7},{6,4},{7,5},{8,10},{9,11},{10,... | collective-permute-start | bytes 589832 | tf_op jit(solution)/shard_map/ppermute | solution.py:528
  84.6 28.3 %collective-permute-start.13 = (bf16[4,64,512]{2,1,0:T(8,128)(2,1)S(1)}, bf16[4,64,512]{2,1,0:T(8,128)(2,1)S(1)}, u32[]{:S(2)}, u32[]{:S(2)}) collective-permute-start(bf16[4,64,512]{2,1,0:T(8,128)(2,1)S(1)} %get-tuple-element.48.refs_0_), channel_id=1, source_target_pairs={{0,2},{1,3},{2,0},{3,1},{4,6},{5,7},{6,4},{7,5},{8,10},{9,11},{10,... | collective-permute-start | bytes 786440 | tf_op jit(solution)/shard_map/ppermute | solution.py:528
  87.3 25.6 %collective-permute-start.15 = (bf16[4,64,512]{2,1,0:T(8,128)(2,1)S(1)}, bf16[4,64,512]{2,1,0:T(8,128)(2,1)S(1)}, u32[]{:S(2)}, u32[]{:S(2)}) collective-permute-start(bf16[4,64,512]{2,1,0:T(8,128)(2,1)S(1)} %get-tuple-element.47.refs_4_), channel_id=1, source_target_pairs={{0,1},{1,0},{2,3},{3,2},{4,5},{5,4},{6,7},{7,6},{8,9},{9,8},{10,11... | collective-permute-start | bytes 786440 | tf_op jit(solution)/shard_map/ppermute | solution.py:528
  87.8 25.1 %collective-permute-start.14 = (bf16[4,64,512]{2,1,0:T(8,128)(2,1)S(1)}, bf16[4,64,512]{2,1,0:T(8,128)(2,1)S(1)}, u32[]{:S(2)}, u32[]{:S(2)}) collective-permute-start(bf16[4,64,512]{2,1,0:T(8,128)(2,1)S(1)} %collective-permute-done.12.refs_1_), channel_id=1, source_target_pairs={{0,2},{1,3},{2,0},{3,1},{4,6},{5,7},{6,4},{7,5},{8,10},{9,11},{10,... | collective-permute-start | bytes 786440 | tf_op jit(solution)/shard_map/ppermute | solution.py:528
  88.5 24.3 %collective-permute-start.17 = (bf16[4,64,512]{2,1,0:T(8,128)(2,1)S(1)}, bf16[4,64,512]{2,1,0:T(8,128)(2,1)S(1)}, u32[]{:S(2)}, u32[]{:S(2)}) collective-permute-start(bf16[4,64,512]{2,1,0:T(8,128)(2,1)S(1)} %collective-permute-done.16.refs_6_), channel_id=1, source_target_pairs={{0,1},{1,0},{2,3},{3,2},{4,5},{5,4},{6,7},{7,6},{8,9},{9,8},{10,11... | collective-permute-start | bytes 786440 | tf_op jit(solution)/shard_map/ppermute | solution.py:528
  90.1 8.6 %collective-permute-start.31 = (bf16[64,1536]{1,0:T(8,128)(2,1)}, bf16[64,1536]{1,0:T(8,128)(2,1)}, u32[]{:S(2)}, u32[]{:S(2)}) collective-permute-start(bf16[64,1536]{1,0:T(8,128)(2,1)} %collective-permute-done.30.refs_14_), channel_id=1, source_target_pairs={{0,1},{1,0},{2,3},{3,2},{4,5},{5,4},{6,7},{7,6},{8,9},{9,8},{10,11... | collective-permute-start | bytes 589832 | tf_op jit(solution)/shard_map/ppermute | solution.py:528
  98.7 0.9 copy-start.4
  99.6 0.9 copy-start.6
  100.5 0.9 copy-start.8
  101.4 0.9 copy-start.10
  102.4 0.9 copy-start.12
  103.3 0.9 copy-start.14
  104.2 0.9 copy-start.16
  120.5 1.3 copy-start
  121.8 10.8 %collective-permute-start.32 = (f32[512,512]{1,0:T(8,128)}, f32[512,512]{1,0:T(8,128)}, u32[]{:S(2)}, u32[]{:S(2)}) collective-permute-start(f32[512,512]{1,0:T(8,128)} %get-tuple-element.32.block_ref), channel_id=1, source_target_pairs={{0,16},{16,0},{1,17},{17,1},{2,18},{18,2},{3,19},{19,3},{4,20},{20... | collective-permute-start | bytes 3145736 | tf_op jit(solution)/shard_map/ppermute | solution.py:525
  121.8 11.1 %slice-start = ((s8[10485760]{0:T(1024)(128)(4,1)}), s8[4194304]{0:T(1024)(128)(4,1)S(1)}, s32[]{:S(2)}) async-start(s8[10485760]{0:T(1024)(128)(4,1)} %bitcast.59), calls=%async_computation | async-start | bytes 8388608
  121.8 11.1 %slice-start.1 = ((s8[10485760]{0:T(1024)(128)(4,1)}), s8[4194304]{0:T(1024)(128)(4,1)S(1)}, s32[]{:S(2)}) async-start(s8[10485760]{0:T(1024)(128)(4,1)} %bitcast.59), calls=%async_computation.1 | async-start | bytes 8388608
  127.4 27.3 %collective-permute-start.8 = (bf16[2,1024,1280]{2,1,0:T(8,128)(2,1)}, bf16[2,1024,1280]{2,1,0:T(8,128)(2,1)S(1)}, u32[]{:S(2)}, u32[]{:S(2)}) collective-permute-start(bf16[2,1024,1280]{2,1,0:T(8,128)(2,1)} %constant_dynamic-slice_fusion), channel_id=1, source_target_pairs={{0,16},{16,0},{1,17},{17,1},{2,18},{18,2},{3,19},{19,3},{4,20},{20... | collective-permute-start | bytes 15728648 | tf_op jit(solution)/shard_map/ppermute | solution.py:525
  127.9 1.6 copy-start.1
  129.5 3.4 %slice-start.2 = ((s8[10485760]{0:T(1024)(128)(4,1)}), s8[2097152]{0:T(1024)(128)(4,1)S(1)}, s32[]{:S(2)}) async-start(s8[10485760]{0:T(1024)(128)(4,1)} %bitcast.59), calls=%async_computation.2 | async-start | bytes 4194304
  132.6 22.2 %collective-permute-start.33 = (bf16[2,1024,1024]{2,1,0:T(8,128)(2,1)S(1)}, bf16[2,1024,1024]{2,1,0:T(8,128)(2,1)S(1)}, u32[]{:S(2)}, u32[]{:S(2)}) collective-permute-start(bf16[2,1024,1024]{2,1,0:T(8,128)(2,1)S(1)} %back_solve.1.qs), channel_id=1, source_target_pairs={{0,16},{16,0},{1,17},{17,1},{2,18},{18,2},{3,19},{19,3},{4,20},{20... | collective-permute-start | bytes 12582920 | tf_op jit(solution)/shard_map/ppermute | solution.py:525
  (7 other events, 4.8 us)

commit v7 on v6

--- a/solution.py
+++ b/solution.py
@@ -194,19 +194,17 @@
                 at = pl.multiple_of(place_ref[index], 16)
                 panel[arc, pl.ds(at, rows), :] = piece[z].astype(F32)
                 index += 1
+    half = panel.shape[2] // 2
     block_ref[...] = jnp.zeros_like(block_ref)
-
-    def one(arc, _):
+    for arc in range(arcs):
         raw = panel[arc].T.astype(BF16)
         for top in range(0, size, span):
             end = top + span
             value = mm(raw[:, :end], high[arc, top:end, :end], nt)
             value += mm(raw[:, :end], low[arc, top:end, :end], nt)
             pt[arc, :, top:end] = value.astype(BF16)
-        block_ref[...] += mm(pt[arc], pt[arc], nt)
-        return 0
-
-    lax.fori_loop(0, arcs, one, 0)
+        block_ref[:half, :] += mm(pt[arc, :half], pt[arc], nt)
+        block_ref[half:, half:] += mm(pt[arc, half:], pt[arc, half:], nt)
 
 
 def back_kernel(pt, high, low, q_ref):
@@ -544,7 +542,7 @@
         return jnp.where(live[arc][None, :], value, 0)
 
     sends = [window(arc, (1 - sides[arc % 2]) * half) for arc in range(arcs)]
-    sends, cov_factor = lax.optimization_barrier((sends, cov_factor))
+    sends, cov_factor, listed = lax.optimization_barrier((sends, cov_factor, active_blocks))
     keeps = [window(arc, sides[arc % 2] * half) for arc in range(arcs)]
     seeds = []
     for arc in range(arcs):
@@ -583,7 +581,7 @@
     seats = jnp.concatenate([seats, ends.astype(jnp.int32)[None]])
 
     first_column = me * columns + core * share
-    both = jnp.concatenate([active_blocks, swap(active_blocks)], axis=0)
+    both = jnp.concatenate([listed, swap(listed)], axis=0)
     lives = block_hits(both, first_column // BLK, share // BLK).T.reshape(-1).astype(jnp.int32)
     info = jnp.stack([core * (share // BLK), start - first_column]).astype(jnp.int32)
     info = jnp.concatenate([info, lives])

time: 165 us -> 160 us (0.970)
  starting transfers between devices: 42 us -> 36.8 us
    ppermute x30, starting transfers between devices: 40.6 us -> 36 us  [hop(): return lax.ppermute(value, 'par', [(p, p ^ bits) for p in range(chips)])]
    ppermute x30, waiting for transfers between devices: 37.3 us -> 39 us  [hop(): return lax.ppermute(value, 'par', [(p, p ^ bits) for p in range(chips)])]
  transfers between devices with their start and end apart: 34 -> 34, of which waited for: 12 -> 12; matrix products, arithmetic and copies ran while one was open for 11% -> 8% of each run, Pallas kernels for 22% -> 20%
where the time goes in v7:
time: 160 us; the launch traced here: 159 us
  Pallas kernels  50.3 us (31%)
  waiting for transfers between devices  39 us (24%)
  starting transfers between devices  36.8 us (23%)
  local copies, waits for them, and re-layouts  22 us (14%)
  other arithmetic  9.44 us (6%)
    ppermute x30, waiting for transfers between devices, hop(): return lax.ppermute(value, 'par', [(p, p ^ bits) for p in range(chips)])  39 us
    ppermute x30, starting transfers between devices, hop(): return lax.ppermute(value, 'par', [(p, p ^ bits) for p in range(chips)])  36 us
    pallas_call x1, Pallas kernels, chol_normals(): pl.pallas_call(chol_normals_kernel, out_shape=(jax.ShapeDtypeStruct((size...  21.8 us
    unnamed x42, local copies, waits for them, and re-layouts  14.2 us
    pallas_call x1, Pallas kernels, invert_call(): pl.pallas_call(kernel, out_shape=(out, out), in_specs=[SM if value.dtype...  7.68 us
    pallas_call x1, Pallas kernels, panel_call(): pl.pallas_call(functools.partial(panel_kernel, arcs), out_shape=(jax.Shap...  7.55 us
    pallas_call x1, Pallas kernels, normals_call(): pl.pallas_call(normals_kernel, out_shape=jax.ShapeDtypeStruct((width, sha...  7.35 us
    dynamic_slice x1, local copies, waits for them, and re-layouts, paired(): far = lax.dynamic_slice_in_dim(design, (1 - core) * share, share, 2)  5.64 us
  transfers between devices with their start and end apart: 34, of which 12 were waited for; matrix products, arithmetic and copies ran while one was open for 8% of the time, Pallas kernels for 20%

profile of v7, /device:TPU:0, one launch (start us, length us, event | category | flops | bytes accessed | tf_op | source)
XLA Modules:
  0.0 158.9 jit_solution(73257594166662753)
XLA Ops:
  1.9 3.5 %bitcast_select_fusion = (bf16[512,512]{1,0:T(8,128)(2,1)S(1)}, bf16[512,512]{1,0:T(8,128)(2,1)}, bf16[512,512]{1,0:T(8,128)(2,1)S(1)}, bf16[512,512]{1,0:T(8,128)(2,1)S(1)}) fusion(bf16[2,1024,2560]{2,1,0:T(8,128)(2,1)} %own.1, s32[]{:T(128)S(6)} %select_n.107, s32[]{:T(128)S(6)} %min.4, pred[512]{0:T(512)(128)(4,1)S(1)} %broadcast_in_dim.58, ...), kind=kLoop, calls=%fused_computation.9 | loop fusion | flops 1048576 | bytes 4195348 | tf_op jit(solution)/shard_map/jit(_where)/select_n | solution.py:542
  5.5 2.9 %factor_rows.1 = bf16[2,64,1152]{2,1,0:T(8,128)(2,1)S(1)} custom-call(s32[2]{0:T(128)S(1)} %pad_add_fusion.4.place_ref, f32[2,64,1024]{2,1,0:T(8,128)S(1)} %copy-done.2), custom_call_target="tpu_custom_call" | custom-call | tf_op jit(solution)/shard_map/factor_rows/pallas_call | solution.py:76
  8.3 5.4 %collective-permute-start.18 = (bf16[2,64,1152]{2,1,0:T(8,128)(2,1)S(1)}, bf16[2,64,1152]{2,1,0:T(8,128)(2,1)S(1)}, u32[]{:S(2)}, u32[]{:S(2)}) collective-permute-start(bf16[2,64,1152]{2,1,0:T(8,128)(2,1)S(1)} %factor_rows.1), channel_id=1, source_target_pairs={{0,12},{1,13},{2,14},{3,15},{4,8},{5,9},{6,10},{7,11},{8,4},{9,5},... | collective-permute-start | bytes 884744 | tf_op jit(solution)/shard_map/ppermute | solution.py:526
  13.8 1.5 collective-permute-start.2
  15.3 1.5 collective-permute-start
  19.2 1.6 %collective-permute-done.18 = bf16[2,64,1152]{2,1,0:T(8,128)(2,1)S(1)} collective-permute-done((bf16[2,64,1152]{2,1,0:T(8,128)(2,1)S(1)}, bf16[2,64,1152]{2,1,0:T(8,128)(2,1)S(1)}, u32[]{:S(2)}, u32[]{:S(2)}) %collective-permute-start.18) | collective-permute-done | bytes 294944 | tf_op jit(solution)/shard_map/ppermute | solution.py:526
  21.0 6.5 %collective-permute-done.2 = bf16[512,512]{1,0:T(8,128)(2,1)} collective-permute-done((bf16[512,512]{1,0:T(8,128)(2,1)}, bf16[512,512]{1,0:T(8,128)(2,1)}, u32[]{:S(2)}, u32[]{:S(2)}) %collective-permute-start.2) | collective-permute-done | bytes 524320 | tf_op jit(solution)/shard_map/ppermute | solution.py:526
  27.5 1.0 dynamic-slice_add_fusion
  28.5 1.6 collective-permute-start.3
  30.1 1.0 dynamic-slice_add_fusion.1
  31.1 1.6 collective-permute-start.1
  32.8 2.6 %collective-permute-done.3 = bf16[256,512]{1,0:T(8,128)(2,1)S(1)} collective-permute-done((bf16[256,512]{1,0:T(8,128)(2,1)S(1)}, bf16[256,512]{1,0:T(8,128)(2,1)S(1)}, u32[]{:S(2)}, u32[]{:S(2)}) %collective-permute-start.3) | collective-permute-done | bytes 262176 | tf_op jit(solution)/shard_map/ppermute | solution.py:526
  35.5 1.1 add_add_fusion
  36.5 1.2 collective-permute-done.1
  37.8 1.1 add_add_fusion.1
  39.0 1.2 collective-permute-start.5
  40.1 3.2 %collective-permute-start.6 = (bf16[2,64,512]{2,1,0:T(8,128)(2,1)S(1)}, bf16[2,64,512]{2,1,0:T(8,128)(2,1)S(1)}, u32[]{:S(2)}, u32[]{:S(2)}) collective-permute-start(bf16[2,64,512]{2,1,0:T(8,128)(2,1)S(1)} %get-tuple-element.53), channel_id=1, source_target_pairs={{0,12},{1,13},{2,14},{3,15},{4,8},{5,9},{6,10},{7,11},{8,4},{9,5},... | collective-permute-start | bytes 393224 | tf_op jit(solution)/shard_map/ppermute | solution.py:526
  44.0 5.0 %collective-permute-done.4 = bf16[2,64,512]{2,1,0:T(8,128)(2,1)S(1)} collective-permute-done((bf16[2,64,512]{2,1,0:T(8,128)(2,1)S(1)}, bf16[2,64,512]{2,1,0:T(8,128)(2,1)S(1)}, u32[]{:S(2)}, u32[]{:S(2)}) %collective-permute-start.4) | collective-permute-done | bytes 131104 | tf_op jit(solution)/shard_map/ppermute | solution.py:526
  49.0 2.5 %collective-permute-start.27 = (bf16[64,1536]{1,0:T(8,128)(2,1)S(1)}, bf16[64,1536]{1,0:T(8,128)(2,1)S(1)}, u32[]{:S(2)}, u32[]{:S(2)}) collective-permute-start(bf16[64,1536]{1,0:T(8,128)(2,1)S(1)} %get-tuple-element.56.refs_8_), channel_id=1, source_target_pairs={{0,2},{1,3},{2,0},{3,1},{4,6},{5,7},{6,4},{7,5},{8,10},{9,11},{10,... | collective-permute-start | bytes 589832 | tf_op jit(solution)/shard_map/ppermute | solution.py:526
  52.1 2.3 %collective-permute-start.10 = (bf16[2,64,512]{2,1,0:T(8,128)(2,1)S(1)}, bf16[2,64,512]{2,1,0:T(8,128)(2,1)S(1)}, u32[]{:S(2)}, u32[]{:S(2)}) collective-permute-start(bf16[2,64,512]{2,1,0:T(8,128)(2,1)S(1)} %fusion.6), channel_id=1, source_target_pairs={{0,8},{1,9},{2,10},{3,11},{4,12},{5,13},{6,14},{7,15},{8,0},{9,1},... | collective-permute-start | bytes 393224 | tf_op jit(solution)/shard_map/ppermute | solution.py:526
  54.4 1.6 collective-permute-start.11
  56.0 1.6 %collective-permute-done.27.refs_10_ = bf16[64,1536]{1,0:T(8,128)(2,1)S(1)} collective-permute-done((bf16[64,1536]{1,0:T(8,128)(2,1)S(1)}, bf16[64,1536]{1,0:T(8,128)(2,1)S(1)}, u32[]{:S(2)}, u32[]{:S(2)}) %collective-permute-start.27) | collective-permute-done | bytes 196640 | tf_op jit(solution)/shard_map/ppermute | solution.py:526
  58.5 3.0 %collective-permute-done.10 = bf16[2,64,512]{2,1,0:T(8,128)(2,1)S(1)} collective-permute-done((bf16[2,64,512]{2,1,0:T(8,128)(2,1)S(1)}, bf16[2,64,512]{2,1,0:T(8,128)(2,1)S(1)}, u32[]{:S(2)}, u32[]{:S(2)}) %collective-permute-start.10) | collective-permute-done | bytes 131104 | tf_op jit(solution)/shard_map/ppermute | solution.py:526
  61.9 1.7 %collective-permute-start.23 = (bf16[64,1536]{1,0:T(8,128)(2,1)S(1)}, bf16[64,1536]{1,0:T(8,128)(2,1)S(1)}, u32[]{:S(2)}, u32[]{:S(2)}) collective-permute-start(bf16[64,1536]{1,0:T(8,128)(2,1)S(1)} %get-tuple-element.55.refs_4_), channel_id=1, source_target_pairs={{0,1},{1,0},{2,3},{3,2},{4,5},{5,4},{6,7},{7,6},{8,9},{9,8},{10,11... | collective-permute-start | bytes 589832 | tf_op jit(solution)/shard_map/ppermute | solution.py:526
  63.7 1.3 collective-permute-start.30
  67.5 2.0 %collective-permute-done.28.refs_11_ = bf16[64,1536]{1,0:T(8,128)(2,1)S(1)} collective-permute-done((bf16[64,1536]{1,0:T(8,128)(2,1)S(1)}, bf16[64,1536]{1,0:T(8,128)(2,1)S(1)}, u32[]{:S(2)}, u32[]{:S(2)}) %collective-permute-start.28) | collective-permute-done | bytes 196640 | tf_op jit(solution)/shard_map/ppermute | solution.py:526
  70.3 0.9 collective-permute-start.24
  71.2 2.6 %collective-permute-done.23.refs_5_ = bf16[64,1536]{1,0:T(8,128)(2,1)S(1)} collective-permute-done((bf16[64,1536]{1,0:T(8,128)(2,1)S(1)}, bf16[64,1536]{1,0:T(8,128)(2,1)S(1)}, u32[]{:S(2)}, u32[]{:S(2)}) %collective-permute-start.23) | collective-permute-done | bytes 196640 | tf_op jit(solution)/shard_map/ppermute | solution.py:526
  74.2 1.1 collective-permute-start.25
  76.0 5.3 %collective-permute-done.24.refs_6_ = bf16[64,1536]{1,0:T(8,128)(2,1)S(1)} collective-permute-done((bf16[64,1536]{1,0:T(8,128)(2,1)S(1)}, bf16[64,1536]{1,0:T(8,128)(2,1)S(1)}, u32[]{:S(2)}, u32[]{:S(2)}) %collective-permute-start.24) | collective-permute-done | bytes 196640 | tf_op jit(solution)/shard_map/ppermute | solution.py:526
  82.0 1.2 collective-permute-start.13
  84.5 1.1 collective-permute-start.14
  85.6 1.2 collective-permute-start.17
  88.3 7.0 %collective-permute-done.31.refs_15_ = bf16[64,1536]{1,0:T(8,128)(2,1)} collective-permute-done((bf16[64,1536]{1,0:T(8,128)(2,1)}, bf16[64,1536]{1,0:T(8,128)(2,1)}, u32[]{:S(2)}, u32[]{:S(2)}) %collective-permute-start.31) | collective-permute-done | bytes 196640 | tf_op jit(solution)/shard_map/ppermute | solution.py:526
  95.3 0.9 copy-done.4
  96.2 0.9 copy-done.6
  97.2 0.9 copy-done.8
  98.1 0.9 copy-done.10
  99.9 0.9 copy-done.14
  100.9 0.9 copy-done.16
  101.8 7.7 %invert_factor.1 = (bf16[2,1024,1024]{2,1,0:T(8,128)(2,1)S(1)}, bf16[2,1024,1024]{2,1,0:T(8,128)(2,1)S(1)}) custom-call(s32[5]{0:T(128)S(1)} %pad_add_fusion.1.place_ref, bf16[64,1536]{1,0:T(8,128)(2,1)S(1)} %get-tuple-element.57.refs_0_, bf16[64,1536]{1,0:T(8,128)(2,1)S(1)} %collective-permute-done.19.refs_1_, ...), custom_call_target="tpu_custom_call" | custom-call | tf_op jit(solution)/shard_map/invert_factor/pallas_call | solution.py:172
  109.5 7.6 %panel_block.1 = (bf16[2,512,1024]{2,1,0:T(8,128)(2,1)S(1)}, f32[512,512]{1,0:T(8,128)}) custom-call(s32[32]{0:T(128)S(1)} %pad_add_fusion.3.place_ref, bf16[4,64,512]{2,1,0:T(8,128)(2,1)S(1)} %get-tuple-element.50.refs_0_, bf16[4,64,512]{2,1,0:T(8,128)(2,1)S(1)} %collective-permute-done.12.refs_1_, bf16[4,64,512]{2,1,0:T(8,128)(2,1)S(1)} %collective-permute-done.13.refs_2_, ...), custom_call_target="tpu_custom_call" | custom-call | tf_op jit(solution)/shard_map/panel_block/pallas_call | solution.py:228
  117.1 1.3 copy-done
  118.4 5.6 %constant_dynamic-slice_fusion = bf16[2,1024,1280]{2,1,0:T(8,128)(2,1)} fusion(bf16[2,1024,2560]{2,1,0:T(8,128)(2,1)} %own.1, s32[]{:T(128)S(6)} %select_n.118), kind=kLoop, calls=%fused_computation.38 | loop fusion | bytes 10485764 | tf_op jit(solution)/shard_map/dynamic_slice | solution.py:599
  124.6 1.6 copy-done.1
  126.1 3.0 %back_solve.1.qs = bf16[2,1024,1024]{2,1,0:T(8,128)(2,1)S(1)} custom-call(bf16[2,512,1024]{2,1,0:T(8,128)(2,1)S(1)} %copy-done.1, bf16[2,1024,1024]{2,1,0:T(8,128)(2,1)S(1)} %get-tuple-element.31.refs_8_.high, bf16[2,1024,1024]{2,1,0:T(8,128)(2,1)S(1)} %get-tuple-element.32.refs_9_.low), custom_call_target="tpu_custom_call" | custom-call | tf_op jit(solution)/shard_map/back_solve/pallas_call | solution.py:244
  129.5 21.8 %chol_normals.1 = (f32[512,512]{1,0:T(8,128)S(1)}, f32[6,512,256]{2,1,0:T(8,128)S(1)}) custom-call(s32[22]{0:T(128)S(1)} %pad_add_fusion.2.info, f32[512,512]{1,0:T(8,128)} %get-tuple-element.34.block_ref, f32[512,512]{1,0:T(8,128)} %collective-permute-done.32.other_ref, f32[1,512]{1,0:T(1,128)S(1)} %bitcast.61, bf16[2,1024,2560]{2,1,0:T(8,128)(2,1)S(1)} %bitcast.60, ...), custom_call_target="tpu_custom_call" | custom-call | tf_op jit(solution)/shard_map/chol_normals/pallas_call | solution.py:435
  151.4 7.4 %normals.1 = f32[512,1280]{1,0:T(8,128)} custom-call(s32[22]{0:T(128)S(1)} %pad_add_fusion.2.info, bf16[2,1024,1280]{2,1,0:T(8,128)(2,1)S(1)} %collective-permute-done.8.far, bf16[2,1024,1024]{2,1,0:T(8,128)(2,1)S(1)} %collective-permute-done.33.qs, f32[6,512,256]{2,1,0:T(8,128)S(1)} %get-tuple-element.38.sums, f32[512,512]{1,0:T(8,128)S(1)} %get-tuple-element.39.inv_ref, ...), custom_call_target="tpu_custom_call" | custom-call | tf_op jit(solution)/shard_map/normals/pallas_call | solution.py:294
  (113 shorter events, 16.3 us)
Async XLA Ops:
  0.0 16.8 %copy-start.17 = (s32[2,80]{1,0:T(2,128)S(1)}, s32[2,80]{1,0:T(2,128)}, u32[]{:S(2)}) copy-start(s32[2,80]{1,0:T(2,128)} %param.7) | copy-start | bytes 1924
  0.0 5.5 %copy-start.2 = (f32[2,64,1024]{2,1,0:T(8,128)S(1)}, f32[2,64,1024]{2,1,0:T(8,128)}, u32[]{:S(2)}) copy-start(f32[2,64,1024]{2,1,0:T(8,128)} %rows_ref) | copy-start | bytes 1572868
  8.3 12.5 %collective-permute-start.18 = (bf16[2,64,1152]{2,1,0:T(8,128)(2,1)S(1)}, bf16[2,64,1152]{2,1,0:T(8,128)(2,1)S(1)}, u32[]{:S(2)}, u32[]{:S(2)}) collective-permute-start(bf16[2,64,1152]{2,1,0:T(8,128)(2,1)S(1)} %factor_rows.1), channel_id=1, source_target_pairs={{0,12},{1,13},{2,14},{3,15},{4,8},{5,9},{6,10},{7,11},{8,4},{9,5},... | collective-permute-start | bytes 884744 | tf_op jit(solution)/shard_map/ppermute | solution.py:526
  13.8 13.7 %collective-permute-start.2 = (bf16[512,512]{1,0:T(8,128)(2,1)}, bf16[512,512]{1,0:T(8,128)(2,1)}, u32[]{:S(2)}, u32[]{:S(2)}) collective-permute-start(bf16[512,512]{1,0:T(8,128)(2,1)} %get-tuple-element.24), channel_id=1, source_target_pairs={{0,2},{1,3},{2,0},{3,1},{4,6},{5,7},{6,4},{7,5},{8,10},{9,11},{10,... | collective-permute-start | bytes 1572872 | tf_op jit(solution)/shard_map/ppermute | solution.py:526
  15.3 14.8 %collective-permute-start = (bf16[512,512]{1,0:T(8,128)(2,1)S(1)}, bf16[512,512]{1,0:T(8,128)(2,1)}, u32[]{:S(2)}, u32[]{:S(2)}) collective-permute-start(bf16[512,512]{1,0:T(8,128)(2,1)S(1)} %get-tuple-element.23), channel_id=1, source_target_pairs={{0,1},{1,0},{2,3},{3,2},{4,5},{5,4},{6,7},{7,6},{8,9},{9,8},{10,11... | collective-permute-start | bytes 1572872 | tf_op jit(solution)/shard_map/ppermute | solution.py:526
  16.8 2.0 %collective-permute-start.7 = (s32[2,80]{1,0:T(2,128)S(1)}, s32[2,80]{1,0:T(2,128)S(1)}, u32[]{:S(2)}, u32[]{:S(2)}) collective-permute-start(s32[2,80]{1,0:T(2,128)S(1)} %copy-done.17), channel_id=1, source_target_pairs={{0,16},{16,0},{1,17},{17,1},{2,18},{18,2},{3,19},{19,3},{4,20},{20... | collective-permute-start | bytes 1928 | tf_op jit(solution)/shard_map/ppermute | solution.py:523
  28.5 7.0 %collective-permute-start.3 = (bf16[256,512]{1,0:T(8,128)(2,1)S(1)}, bf16[256,512]{1,0:T(8,128)(2,1)S(1)}, u32[]{:S(2)}, u32[]{:S(2)}) collective-permute-start(bf16[256,512]{1,0:T(8,128)(2,1)S(1)} %dynamic-slice_add_fusion), channel_id=1, source_target_pairs={{0,1},{1,0},{2,3},{3,2},{4,5},{5,4},{6,7},{7,6},{8,9},{9,8},{10,11... | collective-permute-start | bytes 786440 | tf_op jit(solution)/shard_map/ppermute | solution.py:526
  31.1 6.7 %collective-permute-start.1 = (bf16[256,512]{1,0:T(8,128)(2,1)S(1)}, bf16[256,512]{1,0:T(8,128)(2,1)S(1)}, u32[]{:S(2)}, u32[]{:S(2)}) collective-permute-start(bf16[256,512]{1,0:T(8,128)(2,1)S(1)} %dynamic-slice_add_fusion.1), channel_id=1, source_target_pairs={{0,2},{1,3},{2,0},{3,1},{4,6},{5,7},{6,4},{7,5},{8,10},{9,11},{10,... | collective-permute-start | bytes 786440 | tf_op jit(solution)/shard_map/ppermute | solution.py:526
  32.8 21.7 %collective-permute-start.22 = (bf16[2,64,1536]{2,1,0:T(8,128)(2,1)S(1)}, bf16[2,64,1536]{2,1,0:T(8,128)(2,1)S(1)}, u32[]{:S(2)}, u32[]{:S(2)}) collective-permute-start(bf16[2,64,1536]{2,1,0:T(8,128)(2,1)S(1)} %maximum_select_fusion), channel_id=1, source_target_pairs={{0,4},{1,5},{2,6},{3,7},{4,0},{5,1},{6,2},{7,3},{8,12},{9,13},{10,... | collective-permute-start | bytes 1179656 | tf_op jit(solution)/shard_map/ppermute | solution.py:526
  38.9 10.1 %collective-permute-start.4 = (bf16[2,64,512]{2,1,0:T(8,128)(2,1)S(1)}, bf16[2,64,512]{2,1,0:T(8,128)(2,1)S(1)}, u32[]{:S(2)}, u32[]{:S(2)}) collective-permute-start(bf16[2,64,512]{2,1,0:T(8,128)(2,1)S(1)} %get-tuple-element.51), channel_id=1, source_target_pairs={{0,4},{1,5},{2,6},{3,7},{4,0},{5,1},{6,2},{7,3},{8,12},{9,13},{10,... | collective-permute-start | bytes 393224 | tf_op jit(solution)/shard_map/ppermute | solution.py:526
  39.0 10.0 %collective-permute-start.5 = (bf16[2,64,512]{2,1,0:T(8,128)(2,1)S(1)}, bf16[2,64,512]{2,1,0:T(8,128)(2,1)S(1)}, u32[]{:S(2)}, u32[]{:S(2)}) collective-permute-start(bf16[2,64,512]{2,1,0:T(8,128)(2,1)S(1)} %get-tuple-element.52), channel_id=1, source_target_pairs={{0,8},{1,9},{2,10},{3,11},{4,12},{5,13},{6,14},{7,15},{8,0},{9,1},... | collective-permute-start | bytes 393224 | tf_op jit(solution)/shard_map/ppermute | solution.py:526
  40.1 11.3 %collective-permute-start.6 = (bf16[2,64,512]{2,1,0:T(8,128)(2,1)S(1)}, bf16[2,64,512]{2,1,0:T(8,128)(2,1)S(1)}, u32[]{:S(2)}, u32[]{:S(2)}) collective-permute-start(bf16[2,64,512]{2,1,0:T(8,128)(2,1)S(1)} %get-tuple-element.53), channel_id=1, source_target_pairs={{0,12},{1,13},{2,14},{3,15},{4,8},{5,9},{6,10},{7,11},{8,4},{9,5},... | collective-permute-start | bytes 393224 | tf_op jit(solution)/shard_map/ppermute | solution.py:526
  43.4 8.8 %collective-permute-start.19 = (bf16[64,1536]{1,0:T(8,128)(2,1)S(1)}, bf16[64,1536]{1,0:T(8,128)(2,1)S(1)}, u32[]{:S(2)}, u32[]{:S(2)}) collective-permute-start(bf16[64,1536]{1,0:T(8,128)(2,1)S(1)} %get-tuple-element.57.refs_0_), channel_id=1, source_target_pairs={{0,1},{1,0},{2,3},{3,2},{4,5},{5,4},{6,7},{7,6},{8,9},{9,8},{10,11... | collective-permute-start | bytes 589832 | tf_op jit(solution)/shard_map/ppermute | solution.py:526
  49.0 14.7 %collective-permute-start.20 = (bf16[64,1536]{1,0:T(8,128)(2,1)S(1)}, bf16[64,1536]{1,0:T(8,128)(2,1)S(1)}, u32[]{:S(2)}, u32[]{:S(2)}) collective-permute-start(bf16[64,1536]{1,0:T(8,128)(2,1)S(1)} %get-tuple-element.57.refs_0_), channel_id=1, source_target_pairs={{0,2},{1,3},{2,0},{3,1},{4,6},{5,7},{6,4},{7,5},{8,10},{9,11},{10,... | collective-permute-start | bytes 589832 | tf_op jit(solution)/shard_map/ppermute | solution.py:526
  49.0 8.6 %collective-permute-start.27 = (bf16[64,1536]{1,0:T(8,128)(2,1)S(1)}, bf16[64,1536]{1,0:T(8,128)(2,1)S(1)}, u32[]{:S(2)}, u32[]{:S(2)}) collective-permute-start(bf16[64,1536]{1,0:T(8,128)(2,1)S(1)} %get-tuple-element.56.refs_8_), channel_id=1, source_target_pairs={{0,2},{1,3},{2,0},{3,1},{4,6},{5,7},{6,4},{7,5},{8,10},{9,11},{10,... | collective-permute-start | bytes 589832 | tf_op jit(solution)/shard_map/ppermute | solution.py:526
  51.5 6.8 %collective-permute-start.9 = (bf16[2,64,512]{2,1,0:T(8,128)(2,1)S(1)}, bf16[2,64,512]{2,1,0:T(8,128)(2,1)S(1)}, u32[]{:S(2)}, u32[]{:S(2)}) collective-permute-start(bf16[2,64,512]{2,1,0:T(8,128)(2,1)S(1)} %fusion.6), channel_id=1, source_target_pairs={{0,4},{1,5},{2,6},{3,7},{4,0},{5,1},{6,2},{7,3},{8,12},{9,13},{10,... | collective-permute-start | bytes 393224 | tf_op jit(solution)/shard_map/ppermute | solution.py:526
  52.1 9.4 %collective-permute-start.10 = (bf16[2,64,512]{2,1,0:T(8,128)(2,1)S(1)}, bf16[2,64,512]{2,1,0:T(8,128)(2,1)S(1)}, u32[]{:S(2)}, u32[]{:S(2)}) collective-permute-start(bf16[2,64,512]{2,1,0:T(8,128)(2,1)S(1)} %fusion.6), channel_id=1, source_target_pairs={{0,8},{1,9},{2,10},{3,11},{4,12},{5,13},{6,14},{7,15},{8,0},{9,1},... | collective-permute-start | bytes 393224 | tf_op jit(solution)/shard_map/ppermute | solution.py:526
  54.4 7.5 %collective-permute-start.11 = (bf16[2,64,512]{2,1,0:T(8,128)(2,1)S(1)}, bf16[2,64,512]{2,1,0:T(8,128)(2,1)S(1)}, u32[]{:S(2)}, u32[]{:S(2)}) collective-permute-start(bf16[2,64,512]{2,1,0:T(8,128)(2,1)S(1)} %fusion.6), channel_id=1, source_target_pairs={{0,12},{1,13},{2,14},{3,15},{4,8},{5,9},{6,10},{7,11},{8,4},{9,5},... | collective-permute-start | bytes 393224 | tf_op jit(solution)/shard_map/ppermute | solution.py:526
  57.6 7.8 %collective-permute-start.26 = (bf16[64,1536]{1,0:T(8,128)(2,1)S(1)}, bf16[64,1536]{1,0:T(8,128)(2,1)S(1)}, u32[]{:S(2)}, u32[]{:S(2)}) collective-permute-start(bf16[64,1536]{1,0:T(8,128)(2,1)S(1)} %get-tuple-element.56.refs_8_), channel_id=1, source_target_pairs={{0,1},{1,0},{2,3},{3,2},{4,5},{5,4},{6,7},{7,6},{8,9},{9,8},{10,11... | collective-permute-start | bytes 589832 | tf_op jit(solution)/shard_map/ppermute | solution.py:526
  58.3 8.5 %collective-permute-start.21 = (bf16[64,1536]{1,0:T(8,128)(2,1)S(1)}, bf16[64,1536]{1,0:T(8,128)(2,1)S(1)}, u32[]{:S(2)}, u32[]{:S(2)}) collective-permute-start(bf16[64,1536]{1,0:T(8,128)(2,1)S(1)} %collective-permute-done.19.refs_1_), channel_id=1, source_target_pairs={{0,2},{1,3},{2,0},{3,1},{4,6},{5,7},{6,4},{7,5},{8,10},{9,11},{10,... | collective-permute-start | bytes 589832 | tf_op jit(solution)/shard_map/ppermute | solution.py:526
  61.5 8.0 %collective-permute-start.28 = (bf16[64,1536]{1,0:T(8,128)(2,1)S(1)}, bf16[64,1536]{1,0:T(8,128)(2,1)S(1)}, u32[]{:S(2)}, u32[]{:S(2)}) collective-permute-start(bf16[64,1536]{1,0:T(8,128)(2,1)S(1)} %collective-permute-done.27.refs_10_), channel_id=1, source_target_pairs={{0,1},{1,0},{2,3},{3,2},{4,5},{5,4},{6,7},{7,6},{8,9},{9,8},{10,11... | collective-permute-start | bytes 589832 | tf_op jit(solution)/shard_map/ppermute | solution.py:526
  61.9 11.9 %collective-permute-start.23 = (bf16[64,1536]{1,0:T(8,128)(2,1)S(1)}, bf16[64,1536]{1,0:T(8,128)(2,1)S(1)}, u32[]{:S(2)}, u32[]{:S(2)}) collective-permute-start(bf16[64,1536]{1,0:T(8,128)(2,1)S(1)} %get-tuple-element.55.refs_4_), channel_id=1, source_target_pairs={{0,1},{1,0},{2,3},{3,2},{4,5},{5,4},{6,7},{7,6},{8,9},{9,8},{10,11... | collective-permute-start | bytes 589832 | tf_op jit(solution)/shard_map/ppermute | solution.py:526
  63.7 10.6 %collective-permute-start.30 = (bf16[64,1536]{1,0:T(8,128)(2,1)S(1)}, bf16[64,1536]{1,0:T(8,128)(2,1)}, u32[]{:S(2)}, u32[]{:S(2)}) collective-permute-start(bf16[64,1536]{1,0:T(8,128)(2,1)S(1)} %get-tuple-element.54.refs_12_), channel_id=1, source_target_pairs={{0,2},{1,3},{2,0},{3,1},{4,6},{5,7},{6,4},{7,5},{8,10},{9,11},{10,... | collective-permute-start | bytes 589832 | tf_op jit(solution)/shard_map/ppermute | solution.py:526
  66.1 18.5 %collective-permute-start.12 = (bf16[4,64,512]{2,1,0:T(8,128)(2,1)S(1)}, bf16[4,64,512]{2,1,0:T(8,128)(2,1)S(1)}, u32[]{:S(2)}, u32[]{:S(2)}) collective-permute-start(bf16[4,64,512]{2,1,0:T(8,128)(2,1)S(1)} %get-tuple-element.50.refs_0_), channel_id=1, source_target_pairs={{0,1},{1,0},{2,3},{3,2},{4,5},{5,4},{6,7},{7,6},{8,9},{9,8},{10,11... | collective-permute-start | bytes 786440 | tf_op jit(solution)/shard_map/ppermute | solution.py:526
  67.5 18.1 %collective-permute-start.16 = (bf16[4,64,512]{2,1,0:T(8,128)(2,1)S(1)}, bf16[4,64,512]{2,1,0:T(8,128)(2,1)S(1)}, u32[]{:S(2)}, u32[]{:S(2)}) collective-permute-start(bf16[4,64,512]{2,1,0:T(8,128)(2,1)S(1)} %get-tuple-element.49.refs_4_), channel_id=1, source_target_pairs={{0,2},{1,3},{2,0},{3,1},{4,6},{5,7},{6,4},{7,5},{8,10},{9,11},{10,... | collective-permute-start | bytes 786440 | tf_op jit(solution)/shard_map/ppermute | solution.py:526
  70.3 11.1 %collective-permute-start.24 = (bf16[64,1536]{1,0:T(8,128)(2,1)S(1)}, bf16[64,1536]{1,0:T(8,128)(2,1)S(1)}, u32[]{:S(2)}, u32[]{:S(2)}) collective-permute-start(bf16[64,1536]{1,0:T(8,128)(2,1)S(1)} %get-tuple-element.55.refs_4_), channel_id=1, source_target_pairs={{0,2},{1,3},{2,0},{3,1},{4,6},{5,7},{6,4},{7,5},{8,10},{9,11},{10,... | collective-permute-start | bytes 589832 | tf_op jit(solution)/shard_map/ppermute | solution.py:526
  73.8 9.4 %collective-permute-start.29 = (bf16[64,1536]{1,0:T(8,128)(2,1)S(1)}, bf16[64,1536]{1,0:T(8,128)(2,1)S(1)}, u32[]{:S(2)}, u32[]{:S(2)}) collective-permute-start(bf16[64,1536]{1,0:T(8,128)(2,1)S(1)} %get-tuple-element.54.refs_12_), channel_id=1, source_target_pairs={{0,1},{1,0},{2,3},{3,2},{4,5},{5,4},{6,7},{7,6},{8,9},{9,8},{10,11... | collective-permute-start | bytes 589832 | tf_op jit(solution)/shard_map/ppermute | solution.py:526
  74.2 12.5 %collective-permute-start.25 = (bf16[64,1536]{1,0:T(8,128)(2,1)S(1)}, bf16[64,1536]{1,0:T(8,128)(2,1)S(1)}, u32[]{:S(2)}, u32[]{:S(2)}) collective-permute-start(bf16[64,1536]{1,0:T(8,128)(2,1)S(1)} %collective-permute-done.23.refs_5_), channel_id=1, source_target_pairs={{0,2},{1,3},{2,0},{3,1},{4,6},{5,7},{6,4},{7,5},{8,10},{9,11},{10,... | collective-permute-start | bytes 589832 | tf_op jit(solution)/shard_map/ppermute | solution.py:526
  82.0 27.5 %collective-permute-start.13 = (bf16[4,64,512]{2,1,0:T(8,128)(2,1)S(1)}, bf16[4,64,512]{2,1,0:T(8,128)(2,1)S(1)}, u32[]{:S(2)}, u32[]{:S(2)}) collective-permute-start(bf16[4,64,512]{2,1,0:T(8,128)(2,1)S(1)} %get-tuple-element.50.refs_0_), channel_id=1, source_target_pairs={{0,2},{1,3},{2,0},{3,1},{4,6},{5,7},{6,4},{7,5},{8,10},{9,11},{10,... | collective-permute-start | bytes 786440 | tf_op jit(solution)/shard_map/ppermute | solution.py:526
  83.9 25.6 %collective-permute-start.15 = (bf16[4,64,512]{2,1,0:T(8,128)(2,1)S(1)}, bf16[4,64,512]{2,1,0:T(8,128)(2,1)S(1)}, u32[]{:S(2)}, u32[]{:S(2)}) collective-permute-start(bf16[4,64,512]{2,1,0:T(8,128)(2,1)S(1)} %get-tuple-element.49.refs_4_), channel_id=1, source_target_pairs={{0,1},{1,0},{2,3},{3,2},{4,5},{5,4},{6,7},{7,6},{8,9},{9,8},{10,11... | collective-permute-start | bytes 786440 | tf_op jit(solution)/shard_map/ppermute | solution.py:526
  84.5 25.0 %collective-permute-start.14 = (bf16[4,64,512]{2,1,0:T(8,128)(2,1)S(1)}, bf16[4,64,512]{2,1,0:T(8,128)(2,1)S(1)}, u32[]{:S(2)}, u32[]{:S(2)}) collective-permute-start(bf16[4,64,512]{2,1,0:T(8,128)(2,1)S(1)} %collective-permute-done.12.refs_1_), channel_id=1, source_target_pairs={{0,2},{1,3},{2,0},{3,1},{4,6},{5,7},{6,4},{7,5},{8,10},{9,11},{10,... | collective-permute-start | bytes 786440 | tf_op jit(solution)/shard_map/ppermute | solution.py:526
  85.6 23.9 %collective-permute-start.17 = (bf16[4,64,512]{2,1,0:T(8,128)(2,1)S(1)}, bf16[4,64,512]{2,1,0:T(8,128)(2,1)S(1)}, u32[]{:S(2)}, u32[]{:S(2)}) collective-permute-start(bf16[4,64,512]{2,1,0:T(8,128)(2,1)S(1)} %collective-permute-done.16.refs_6_), channel_id=1, source_target_pairs={{0,1},{1,0},{2,3},{3,2},{4,5},{5,4},{6,7},{7,6},{8,9},{9,8},{10,11... | collective-permute-start | bytes 786440 | tf_op jit(solution)/shard_map/ppermute | solution.py:526
  87.5 7.8 %collective-permute-start.31 = (bf16[64,1536]{1,0:T(8,128)(2,1)}, bf16[64,1536]{1,0:T(8,128)(2,1)}, u32[]{:S(2)}, u32[]{:S(2)}) collective-permute-start(bf16[64,1536]{1,0:T(8,128)(2,1)} %collective-permute-done.30.refs_14_), channel_id=1, source_target_pairs={{0,1},{1,0},{2,3},{3,2},{4,5},{5,4},{6,7},{7,6},{8,9},{9,8},{10,11... | collective-permute-start | bytes 589832 | tf_op jit(solution)/shard_map/ppermute | solution.py:526
  95.3 0.9 copy-start.4
  96.2 0.9 copy-start.6
  97.2 0.9 copy-start.8
  98.1 0.9 copy-start.10
  99.0 0.9 copy-start.12
  99.9 0.9 copy-start.14
  100.9 0.9 copy-start.16
  117.1 1.3 copy-start
  118.4 10.8 %collective-permute-start.32 = (f32[512,512]{1,0:T(8,128)}, f32[512,512]{1,0:T(8,128)}, u32[]{:S(2)}, u32[]{:S(2)}) collective-permute-start(f32[512,512]{1,0:T(8,128)} %get-tuple-element.34.block_ref), channel_id=1, source_target_pairs={{0,16},{16,0},{1,17},{17,1},{2,18},{18,2},{3,19},{19,3},{4,20},{20... | collective-permute-start | bytes 3145736 | tf_op jit(solution)/shard_map/ppermute | solution.py:523
  118.4 11.1 %slice-start = ((s8[10485760]{0:T(1024)(128)(4,1)}), s8[4194304]{0:T(1024)(128)(4,1)S(1)}, s32[]{:S(2)}) async-start(s8[10485760]{0:T(1024)(128)(4,1)} %bitcast.59), calls=%async_computation | async-start | bytes 8388608
  118.4 11.1 %slice-start.1 = ((s8[10485760]{0:T(1024)(128)(4,1)}), s8[4194304]{0:T(1024)(128)(4,1)S(1)}, s32[]{:S(2)}) async-start(s8[10485760]{0:T(1024)(128)(4,1)} %bitcast.59), calls=%async_computation.1 | async-start | bytes 8388608
  124.0 27.3 %collective-permute-start.8 = (bf16[2,1024,1280]{2,1,0:T(8,128)(2,1)}, bf16[2,1024,1280]{2,1,0:T(8,128)(2,1)S(1)}, u32[]{:S(2)}, u32[]{:S(2)}) collective-permute-start(bf16[2,1024,1280]{2,1,0:T(8,128)(2,1)} %constant_dynamic-slice_fusion), channel_id=1, source_target_pairs={{0,16},{16,0},{1,17},{17,1},{2,18},{18,2},{3,19},{19,3},{4,20},{20... | collective-permute-start | bytes 15728648 | tf_op jit(solution)/shard_map/ppermute | solution.py:523
  124.5 1.6 %copy-start.1 = (bf16[2,512,1024]{2,1,0:T(8,128)(2,1)S(1)}, bf16[2,512,1024]{2,1,0:T(8,128)(2,1)}, u32[]{:S(2)}) copy-start(bf16[2,512,1024]{2,1,0:T(8,128)(2,1)} %copy-done) | copy-start | bytes 6291460
  126.1 3.4 %slice-start.2 = ((s8[10485760]{0:T(1024)(128)(4,1)}), s8[2097152]{0:T(1024)(128)(4,1)S(1)}, s32[]{:S(2)}) async-start(s8[10485760]{0:T(1024)(128)(4,1)} %bitcast.59), calls=%async_computation.2 | async-start | bytes 4194304
  129.2 22.2 %collective-permute-start.33 = (bf16[2,1024,1024]{2,1,0:T(8,128)(2,1)S(1)}, bf16[2,1024,1024]{2,1,0:T(8,128)(2,1)S(1)}, u32[]{:S(2)}, u32[]{:S(2)}) collective-permute-start(bf16[2,1024,1024]{2,1,0:T(8,128)(2,1)S(1)} %back_solve.1.qs), channel_id=1, source_target_pairs={{0,16},{16,0},{1,17},{17,1},{2,18},{18,2},{3,19},{19,3},{4,20},{20... | collective-permute-start | bytes 12582920 | tf_op jit(solution)/shard_map/ppermute | solution.py:523
  (7 other events, 4.8 us)
